TPU v7x, 32 devices: a whole 2x2x4 slice. The times are simulated.
32 devices in a mesh: fsdp: 4 (over y, x), rep: 8 (over z, core).
Axes of the slice: x: 2, y: 2, z: 4, core: 2. Of those that a mesh axis runs over, the one named last changes fastest.
Arguments:
- tokens: bfloat16 [8, 4096, 768], P('rep', 'fsdp'), may hold values from -6 to 6
- counts: int32 [8, 32], P('rep', 'fsdp'), may hold values from 1 to 128, as said below
- cotangent: bfloat16 [8, 4096, 768], P('rep', 'fsdp'), may hold values from -6 to 6
- swe_qkv: bfloat16 [768, 2304], P(('fsdp', 'rep')), may hold values from -0.21875 to 0.21875
- swe_out: bfloat16 [768, 768], P(('fsdp', 'rep')), may hold values from -2.5 to 2.5
- swe_up: bfloat16 [768, 3072], P(('fsdp', 'rep')), may hold values from -0.21875 to 0.21875
- swe_down: bfloat16 [3072, 768], P(('fsdp', 'rep')), may hold values from -0.109375 to 0.109375
- swe_gains: bfloat16 [2, 768], P(None, ('fsdp', 'rep')), may hold values from 0.099609375 to 1.8984375
- swe_biases: bfloat16 [2, 768], P(None, ('fsdp', 'rep')), may hold values from -1.796875 to 1.796875
- cse_qkv: bfloat16 [768, 2304], P(('fsdp', 'rep')), may hold values from -0.21875 to 0.21875
- cse_out: bfloat16 [768, 768], P(('fsdp', 'rep')), may hold values from -1.25 to 1.25
- cse_up: bfloat16 [768, 3072], P(('fsdp', 'rep')), may hold values from -0.21875 to 0.21875
- cse_down: bfloat16 [3072, 768], P(('fsdp', 'rep')), may hold values from -0.109375 to 0.109375
- cse_gains: bfloat16 [2, 768], P(None, ('fsdp', 'rep')), may hold values from 0.099609375 to 1.8984375
- cse_biases: bfloat16 [2, 768], P(None, ('fsdp', 'rep')), may hold values from -1.796875 to 1.796875
- positions: bfloat16 [32, 768], P(None, ('fsdp', 'rep')), may hold values from -6 to 6
Outputs:
- layer_out: bfloat16 [8, 4096, 768], P('rep', 'fsdp')
- token_grad: bfloat16 [8, 4096, 768], P('rep', 'fsdp')
- grad_swe_qkv: float32 [768, 2304], P('fsdp')
- grad_swe_out: float32 [768, 768], P('fsdp')
- grad_swe_up: float32 [768, 3072], P('fsdp')
- grad_swe_down: float32 [3072, 768], P('fsdp')
- grad_swe_gains: float32 [2, 768], P(None, 'fsdp')
- grad_swe_biases: float32 [2, 768], P(None, 'fsdp')
- grad_cse_qkv: float32 [768, 2304], P('fsdp')
- grad_cse_out: float32 [768, 768], P('fsdp')
- grad_cse_up: float32 [768, 3072], P('fsdp')
- grad_cse_down: float32 [3072, 768], P('fsdp')
- grad_cse_gains: float32 [2, 768], P(None, 'fsdp')
- grad_cse_biases: float32 [2, 768], P(None, 'fsdp')
- grad_positions: float32 [32, 768], P(None, 'fsdp')
Inputs may be any that keep to these rules, and one draw needn't show every extreme that they name: counts[d, s] is the number of true tokens in segment s of document d: a document's true tokens fill its segments from the first, every segment before the one that holds its last true token is full, and every segment after it holds only its first token.
All inputs are finite; a program needn't handle non-finite values.
Results may differ from a plain program's by a relative error of at most 0.035.
Values may be sent and summed in bfloat16 or wider, within the bound.
No kernel may reach another device: no remote copies, remote signals or barrier semaphores. Data moves between devices by JAX's collectives and lax.ppermute only.
A program may use at most 256 MiB of HBM per device.

v0:
```python
import math

import jax
import jax.numpy as jnp
from jax import lax
from jax.sharding import PartitionSpec as P

HEAD = 64


norm_eps = 1e-05
masked_score = -1000000000.0


def product(left_op, right_op, einsum_form):
    return jnp.einsum(einsum_form, left_op, right_op, preferred_element_type=jnp.float32)


def normalize(summed_in, gain_row, bias_row):
    row_mean = jnp.mean(summed_in, axis=-1, keepdims=True)
    centered = summed_in - row_mean
    inv_dev = lax.rsqrt(jnp.mean(centered * centered, axis=-1, keepdims=True) + norm_eps)
    unit_rows = centered * inv_dev
    return (unit_rows * gain_row + bias_row, unit_rows, inv_dev)


def norm_back(upstream, unit_rows, inv_dev, gain_row):
    scaled = upstream * gain_row
    grad_in = inv_dev * (
        scaled
        - jnp.mean(scaled, axis=-1, keepdims=True)
        - unit_rows * jnp.mean(scaled * unit_rows, axis=-1, keepdims=True)
    )
    return (grad_in, jnp.sum(upstream * unit_rows, axis=(0, 1)), jnp.sum(upstream, axis=(0, 1)))


def gelu_pair(inner_pre):
    cumul = 0.5 * (1.0 + lax.erf(inner_pre * 0.7071067811865476))
    return (
        inner_pre * cumul,
        cumul + inner_pre * jnp.exp(-0.5 * inner_pre * inner_pre) * 0.3989422804014327,
    )


def split_heads(packed, head_count):
    stacked = packed.reshape(packed.shape[0], packed.shape[1], 3, head_count, HEAD)
    return (stacked[:, :, 0], stacked[:, :, 1], stacked[:, :, 2])


def masked_scores(query_rows, key_rows, key_mask):
    raw_scores = product(query_rows, key_rows, "gqhe,gkhe->ghqk") * (1.0 / math.sqrt(HEAD))
    return jnp.where(key_mask[:, None, None, :], raw_scores, masked_score)


def attend(query_rows, key_rows, value_rows, key_mask):
    scores = masked_scores(query_rows, key_rows, key_mask)
    row_max = jnp.max(scores, axis=-1, keepdims=True)
    log_total = row_max + jnp.log(jnp.sum(jnp.exp(scores - row_max), axis=-1, keepdims=True))
    softmax_w = jnp.exp(scores - log_total).astype(jnp.bfloat16)
    mixed_heads = product(softmax_w, value_rows, "ghqk,gkhe->gqhe").astype(jnp.bfloat16)
    return (mixed_heads, log_total)


def attend_back(query_rows, key_rows, value_rows, key_mask, log_total, grad_mixed):
    scores = masked_scores(query_rows, key_rows, key_mask)
    softmax_w = jnp.exp(scores - log_total)
    grad_value = product(softmax_w.astype(jnp.bfloat16), grad_mixed, "ghqk,gqhe->gkhe")
    grad_probs = product(grad_mixed, value_rows, "gqhe,gkhe->ghqk")
    grad_scores = (
        softmax_w * (grad_probs - jnp.sum(softmax_w * grad_probs, axis=-1, keepdims=True))
    ).astype(jnp.bfloat16)
    inv_root = 1.0 / math.sqrt(HEAD)
    grad_query = product(grad_scores, key_rows, "ghqk,gkhe->gqhe") * inv_root
    grad_key = product(grad_scores, query_rows, "ghqk,gqhe->gkhe") * inv_root
    return (grad_query, grad_key, grad_value)


def finish(resid_in, mixed_flat, block_weights):
    proj_out, proj_up, proj_down, gain_rows, bias_rows = block_weights
    attended = product(mixed_flat, proj_out, "gsd,de->gse")
    first_norm, unit_one, inv_one = normalize(resid_in + attended, gain_rows[0], bias_rows[0])
    first_low = first_norm.astype(jnp.bfloat16)
    inner_pre = product(first_low, proj_up, "gsd,df->gsf")
    activated, gelu_slope = gelu_pair(inner_pre)
    act_low = activated.astype(jnp.bfloat16)
    outer_out = product(act_low, proj_down, "gsf,fd->gsd")
    normed_out, unit_two, inv_two = normalize(first_norm + outer_out, gain_rows[1], bias_rows[1])
    return (normed_out, (unit_one, inv_one, first_low, gelu_slope, act_low, unit_two, inv_two))


def finish_back(upstream, mixed_flat, saved_parts, block_weights):
    proj_out, proj_up, proj_down, gain_rows, bias_rows = block_weights
    unit_one, inv_one, first_low, gelu_slope, act_low, unit_two, inv_two = saved_parts
    grad_two, gain_two, bias_two = norm_back(upstream, unit_two, inv_two, gain_rows[1])
    grad_outer = grad_two.astype(jnp.bfloat16)
    grad_down = product(act_low, grad_outer, "gsf,gsd->fd")
    grad_inner = (product(grad_outer, proj_down, "gsd,fd->gsf") * gelu_slope).astype(jnp.bfloat16)
    grad_up = product(first_low, grad_inner, "gsd,gsf->df")
    grad_first = grad_two + product(grad_inner, proj_up, "gsf,df->gsd")
    grad_one, gain_one, bias_one = norm_back(grad_first, unit_one, inv_one, gain_rows[0])
    grad_attended = grad_one.astype(jnp.bfloat16)
    grad_out = product(mixed_flat, grad_attended, "gsd,gse->de")
    grad_mixed = product(grad_attended, proj_out, "gse,de->gsd").astype(jnp.bfloat16)
    return (
        grad_one,
        grad_mixed,
        (
            grad_out,
            grad_up,
            grad_down,
            jnp.stack([gain_one, gain_two]),
            jnp.stack([bias_one, bias_two]),
        ),
    )


def per_device(
    tokens,
    counts,
    cotangent,
    swe_qkv,
    swe_out,
    swe_up,
    swe_down,
    swe_gains,
    swe_biases,
    cse_qkv,
    cse_out,
    cse_up,
    cse_down,
    cse_gains,
    cse_biases,
    positions,
):
    docs_here, local_len, model_width = tokens.shape
    seg_here = counts.shape[1]
    seg_len = local_len // seg_here
    groups = docs_here * seg_here
    head_count = model_width // HEAD
    seg_rows = tokens.reshape(groups, seg_len, model_width)
    is_valid = jnp.arange(seg_len, dtype=jnp.int32)[None, :] < counts.reshape(groups, 1)
    valid_f = is_valid.astype(jnp.float32)[..., None]
    swe_full = (
        lax.all_gather(swe_qkv, ("fsdp", "rep"), axis=0, tiled=True),
        lax.all_gather(swe_out, ("fsdp", "rep"), axis=0, tiled=True),
        lax.all_gather(swe_up, ("fsdp", "rep"), axis=0, tiled=True),
        lax.all_gather(swe_down, ("fsdp", "rep"), axis=0, tiled=True),
        lax.all_gather(swe_gains, ("fsdp", "rep"), axis=1, tiled=True),
        lax.all_gather(swe_biases, ("fsdp", "rep"), axis=1, tiled=True),
    )
    packed = product(seg_rows, swe_full[0], "gsd,de->gse").astype(jnp.bfloat16)
    queries, key_rows, value_rows = split_heads(packed, head_count)
    mixed_heads, log_total = attend(queries, key_rows, value_rows, is_valid)
    mixed_flat = mixed_heads.reshape(groups, seg_len, model_width)
    normed_out, saved_parts = finish(seg_rows.astype(jnp.float32), mixed_flat, swe_full[1:6])
    hidden = normed_out * valid_f
    cse_full = (
        lax.all_gather(cse_qkv, ("fsdp", "rep"), axis=0, tiled=True),
        lax.all_gather(cse_out, ("fsdp", "rep"), axis=0, tiled=True),
        lax.all_gather(cse_up, ("fsdp", "rep"), axis=0, tiled=True),
        lax.all_gather(cse_down, ("fsdp", "rep"), axis=0, tiled=True),
        lax.all_gather(cse_gains, ("fsdp", "rep"), axis=1, tiled=True),
        lax.all_gather(cse_biases, ("fsdp", "rep"), axis=1, tiled=True),
        lax.all_gather(positions, ("fsdp", "rep"), axis=1, tiled=True),
    )
    first_seg = lax.axis_index("fsdp") * seg_here
    pos_here = lax.dynamic_slice_in_dim(cse_full[6], first_seg, seg_here, 0)
    cls_in = (hidden[:, 0, :].reshape(docs_here, seg_here, model_width) + pos_here[None]).astype(
        jnp.bfloat16
    )
    cls_packed = product(cls_in, cse_full[0], "gsd,de->gse").astype(jnp.bfloat16)
    cls_kv = lax.all_gather(cls_packed[:, :, model_width:], "fsdp", axis=1, tiled=True)
    seg_total = cls_kv.shape[1]
    cls_query = cls_packed[:, :, :model_width].reshape(docs_here, seg_here, head_count, HEAD)
    cls_key = cls_kv[:, :, :model_width].reshape(docs_here, seg_total, head_count, HEAD)
    cls_value = cls_kv[:, :, model_width:].reshape(docs_here, seg_total, head_count, HEAD)
    all_keys = jnp.ones((docs_here, seg_total), dtype=jnp.bool_)
    cls_mixed, cls_total = attend(cls_query, cls_key, cls_value, all_keys)
    cls_flat = cls_mixed.reshape(docs_here, seg_here, model_width)
    cls_out, cls_saved = finish(cls_in.astype(jnp.float32), cls_flat, cse_full[1:6])
    layer_full = hidden.at[:, 0, :].set(cls_out.reshape(groups, model_width))
    layer_out = layer_full.astype(jnp.bfloat16).reshape(tokens.shape)
    again = (
        lax.all_gather(swe_qkv, ("fsdp", "rep"), axis=0, tiled=True),
        lax.all_gather(swe_out, ("fsdp", "rep"), axis=0, tiled=True),
        lax.all_gather(swe_up, ("fsdp", "rep"), axis=0, tiled=True),
        lax.all_gather(swe_down, ("fsdp", "rep"), axis=0, tiled=True),
        lax.all_gather(swe_gains, ("fsdp", "rep"), axis=1, tiled=True),
        lax.all_gather(swe_biases, ("fsdp", "rep"), axis=1, tiled=True),
        lax.all_gather(cse_qkv, ("fsdp", "rep"), axis=0, tiled=True),
        lax.all_gather(cse_out, ("fsdp", "rep"), axis=0, tiled=True),
        lax.all_gather(cse_up, ("fsdp", "rep"), axis=0, tiled=True),
        lax.all_gather(cse_down, ("fsdp", "rep"), axis=0, tiled=True),
        lax.all_gather(cse_gains, ("fsdp", "rep"), axis=1, tiled=True),
        lax.all_gather(cse_biases, ("fsdp", "rep"), axis=1, tiled=True),
        lax.all_gather(positions, ("fsdp", "rep"), axis=1, tiled=True),
    )
    swe_back = again[0:6]
    cse_back = again[6:12]
    upstream = cotangent.reshape(groups, seg_len, model_width).astype(jnp.float32)
    cls_upstream = upstream[:, 0, :].reshape(docs_here, seg_here, model_width)
    cls_resid, cls_grad_mixed, cross_grads = finish_back(
        cls_upstream, cls_flat, cls_saved, cse_back[1:6]
    )
    cls_dquery, cls_dkey, cls_dvalue = attend_back(
        cls_query,
        cls_key,
        cls_value,
        all_keys,
        cls_total,
        cls_grad_mixed.reshape(docs_here, seg_here, head_count, HEAD),
    )
    key_grads = jnp.concatenate(
        [
            cls_dkey.reshape(docs_here, seg_total, model_width),
            cls_dvalue.reshape(docs_here, seg_total, model_width),
        ],
        axis=2,
    )
    key_grads_here = lax.psum_scatter(
        key_grads.astype(jnp.bfloat16), "fsdp", scatter_dimension=1, tiled=True
    ).astype(jnp.float32)
    cls_dpacked = jnp.concatenate(
        [cls_dquery.reshape(docs_here, seg_here, model_width), key_grads_here], axis=2
    ).astype(jnp.bfloat16)
    cross_qkv = product(cls_in, cls_dpacked, "gsd,gse->de")
    cls_dinput = cls_resid + product(cls_dpacked, cse_back[0], "gse,de->gsd")
    grad_pos = lax.dynamic_update_slice_in_dim(
        jnp.zeros((seg_total, model_width), jnp.float32), jnp.sum(cls_dinput, axis=0), first_seg, 0
    )
    grad_hidden = upstream.at[:, 0, :].set(cls_dinput.reshape(groups, model_width)) * valid_f
    seg_resid, seg_grad_mixed, seg_grads = finish_back(
        grad_hidden, mixed_flat, saved_parts, swe_back[1:6]
    )
    grad_query, grad_key, grad_value = attend_back(
        queries,
        key_rows,
        value_rows,
        is_valid,
        log_total,
        seg_grad_mixed.reshape(groups, seg_len, head_count, HEAD),
    )
    grad_packed = jnp.concatenate(
        [
            grad_query.reshape(groups, seg_len, model_width),
            grad_key.reshape(groups, seg_len, model_width),
            grad_value.reshape(groups, seg_len, model_width),
        ],
        axis=2,
    ).astype(jnp.bfloat16)
    grad_qkv = product(seg_rows, grad_packed, "gsd,gse->de")
    grad_rows = seg_resid + product(grad_packed, swe_back[0], "gse,de->gsd")
    token_grad = grad_rows.astype(jnp.bfloat16).reshape(tokens.shape)
    grad_out, grad_up, grad_down, grad_gains, grad_biases = seg_grads
    cross_out, cross_up, cross_down, cross_gains, cross_biases = cross_grads
    (
        grad_qkv,
        grad_out,
        grad_up,
        grad_down,
        grad_gains,
        grad_biases,
        cross_qkv,
        cross_out,
        cross_up,
        cross_down,
        cross_gains,
        cross_biases,
        grad_pos,
    ) = (
        lax.psum_scatter(
            grad_qkv.astype(jnp.bfloat16), "fsdp", scatter_dimension=0, tiled=True
        ).astype(jnp.float32),
        lax.psum_scatter(
            grad_out.astype(jnp.bfloat16), "fsdp", scatter_dimension=0, tiled=True
        ).astype(jnp.float32),
        lax.psum_scatter(
            grad_up.astype(jnp.bfloat16), "fsdp", scatter_dimension=0, tiled=True
        ).astype(jnp.float32),
        lax.psum_scatter(
            grad_down.astype(jnp.bfloat16), "fsdp", scatter_dimension=0, tiled=True
        ).astype(jnp.float32),
        lax.psum_scatter(
            grad_gains.astype(jnp.bfloat16), "fsdp", scatter_dimension=1, tiled=True
        ).astype(jnp.float32),
        lax.psum_scatter(
            grad_biases.astype(jnp.bfloat16), "fsdp", scatter_dimension=1, tiled=True
        ).astype(jnp.float32),
        lax.psum_scatter(
            cross_qkv.astype(jnp.bfloat16), "fsdp", scatter_dimension=0, tiled=True
        ).astype(jnp.float32),
        lax.psum_scatter(
            cross_out.astype(jnp.bfloat16), "fsdp", scatter_dimension=0, tiled=True
        ).astype(jnp.float32),
        lax.psum_scatter(
            cross_up.astype(jnp.bfloat16), "fsdp", scatter_dimension=0, tiled=True
        ).astype(jnp.float32),
        lax.psum_scatter(
            cross_down.astype(jnp.bfloat16), "fsdp", scatter_dimension=0, tiled=True
        ).astype(jnp.float32),
        lax.psum_scatter(
            cross_gains.astype(jnp.bfloat16), "fsdp", scatter_dimension=1, tiled=True
        ).astype(jnp.float32),
        lax.psum_scatter(
            cross_biases.astype(jnp.bfloat16), "fsdp", scatter_dimension=1, tiled=True
        ).astype(jnp.float32),
        lax.psum_scatter(
            grad_pos.astype(jnp.bfloat16), "fsdp", scatter_dimension=1, tiled=True
        ).astype(jnp.float32),
    )
    (
        grad_qkv,
        grad_out,
        grad_up,
        grad_down,
        grad_gains,
        grad_biases,
        cross_qkv,
        cross_out,
        cross_up,
        cross_down,
        cross_gains,
        cross_biases,
        grad_pos,
    ) = lax.psum(
        (
            grad_qkv,
            grad_out,
            grad_up,
            grad_down,
            grad_gains,
            grad_biases,
            cross_qkv,
            cross_out,
            cross_up,
            cross_down,
            cross_gains,
            cross_biases,
            grad_pos,
        ),
        "rep",
    )
    return (
        layer_out,
        token_grad,
        grad_qkv,
        grad_out,
        grad_up,
        grad_down,
        grad_gains,
        grad_biases,
        cross_qkv,
        cross_out,
        cross_up,
        cross_down,
        cross_gains,
        cross_biases,
        grad_pos,
    )


def solution(mesh):
    return jax.shard_map(
        per_device,
        mesh=mesh,
        in_specs=(
            P("rep", "fsdp", None),
            P("rep", "fsdp"),
            P("rep", "fsdp", None),
            P(("fsdp", "rep"), None),
            P(("fsdp", "rep"), None),
            P(("fsdp", "rep"), None),
            P(("fsdp", "rep"), None),
            P(None, ("fsdp", "rep")),
            P(None, ("fsdp", "rep")),
            P(("fsdp", "rep"), None),
            P(("fsdp", "rep"), None),
            P(("fsdp", "rep"), None),
            P(("fsdp", "rep"), None),
            P(None, ("fsdp", "rep")),
            P(None, ("fsdp", "rep")),
            P(None, ("fsdp", "rep")),
        ),
        out_specs=(
            P("rep", "fsdp", None),
            P("rep", "fsdp", None),
            P("fsdp", None),
            P("fsdp", None),
            P("fsdp", None),
            P("fsdp", None),
            P(None, "fsdp"),
            P(None, "fsdp"),
            P("fsdp", None),
            P("fsdp", None),
            P("fsdp", None),
            P("fsdp", None),
            P(None, "fsdp"),
            P(None, "fsdp"),
            P(None, "fsdp"),
        ),
        check_vma=False,
    )
```

profile of v0, /device:TPU:0, one launch (start us, length us, event | category | flops | bytes accessed | tf_op | source)
XLA Modules:
  0.0 1417.8 jit_solution(5317765596628372033)
XLA Ops:
  16.7 43.0 %all-gather = bf16[32,24,2]{1,2,0:T(2,128)(2,1)S(1)} all-gather(bf16[1,24,2]{1,2,0:T(2,128)(2,1)S(1)} %bitcast.229), channel_id=1, replica_groups=mesh['fsdp'=4,'rep'=8] {'fsdp','rep'}, dimensions={0}, use_global_device_ids=true | all-gather | bytes 3168 | tf_op jit(solution)/shard_map/all_gather | solution.py:148
  59.9 36.4 %all-gather.1 = bf16[32,24,2]{1,2,0:T(2,128)(2,1)S(1)} all-gather(bf16[1,24,2]{1,2,0:T(2,128)(2,1)S(1)} %bitcast.230), channel_id=1, replica_groups=mesh['fsdp'=4,'rep'=8] {'fsdp','rep'}, dimensions={0}, use_global_device_ids=true | all-gather | bytes 3168 | tf_op jit(solution)/shard_map/all_gather | solution.py:149
  96.4 38.9 %all_gather.58 = bf16[32,768]{0,1:T(8,128)(2,1)S(1)} all-gather(bf16[32,24]{0,1:T(8,128)(2,1)S(1)} %copy-done.55), channel_id=1, replica_groups=mesh['fsdp'=4,'rep'=8] {'fsdp','rep'}, dimensions={1}, use_global_device_ids=true | all-gather | bytes 50688 | tf_op jit(solution)/shard_map/all_gather | solution.py:164
  135.6 36.7 %all-gather.2 = bf16[32,24,2]{1,2,0:T(2,128)(2,1)S(1)} all-gather(bf16[1,24,2]{1,2,0:T(2,128)(2,1)S(1)} %bitcast.231), channel_id=1, replica_groups=mesh['fsdp'=4,'rep'=8] {'fsdp','rep'}, dimensions={0}, use_global_device_ids=true | all-gather | bytes 3168 | tf_op jit(solution)/shard_map/all_gather | solution.py:162
  172.4 37.9 %all-gather.3 = bf16[32,24,2]{1,2,0:T(2,128)(2,1)S(1)} all-gather(bf16[1,24,2]{1,2,0:T(2,128)(2,1)} %bitcast.232), channel_id=1, replica_groups=mesh['fsdp'=4,'rep'=8] {'fsdp','rep'}, dimensions={0}, use_global_device_ids=true | all-gather | bytes 3168 | tf_op jit(solution)/shard_map/all_gather | solution.py:163
  215.0 8.4 convolution_convert_fusion
  223.4 6.8 copy.96
  246.1 12.6 multiply_convert_fusion
  261.4 9.3 fusion.95
  273.7 49.7 %all-gather.21.cloned.1.call-done = bf16[768,2304]{1,0:T(8,128)(2,1)} async-done(((bf16[24,2304]{1,0:T(8,128)(2,1)}), bf16[768,2304]{1,0:T(8,128)(2,1)}) %all-gather.21.cloned.1.call-update) | async-done | bytes 3538960 | tf_op jit(solution)/shard_map/all_gather | solution.py:158
  326.0 8.7 all_gather.60
  338.9 40.4 %all-gather.23.cloned.1.call-done = bf16[768,768]{1,0:T(8,128)(2,1)} async-done(((bf16[24,768]{1,0:T(8,128)(2,1)}), bf16[768,768]{1,0:T(8,128)(2,1)}) %all-gather.23.cloned.1.call-update) | async-done | bytes 1179664 | tf_op jit(solution)/shard_map/all_gather | solution.py:159
  381.2 63.8 %all-gather.25.cloned.1.call-done = bf16[768,3072]{1,0:T(8,128)(2,1)} async-done(((bf16[24,3072]{1,0:T(8,128)(2,1)}), bf16[768,3072]{1,0:T(8,128)(2,1)}) %all-gather.25.cloned.1.call-update) | async-done | bytes 4718608 | tf_op jit(solution)/shard_map/all_gather | solution.py:160
  448.1 62.4 %all-gather.27.cloned.1.call-done = bf16[3072,768]{1,0:T(8,128)(2,1)} async-done(((bf16[96,768]{1,0:T(8,128)(2,1)}), bf16[3072,768]{1,0:T(8,128)(2,1)}) %all-gather.27.cloned.1.call-update) | async-done | bytes 4718608 | tf_op jit(solution)/shard_map/all_gather | solution.py:161
  539.3 35.0 %all-reduce.5.cloned.1.call-done = bf16[1,32,1536]{2,1,0:T(8,128)(2,1)} async-done(((bf16[1,32,1536]{2,1,0:T(8,128)(2,1)}), bf16[1,32,1536]{2,1,0:T(8,128)(2,1)}) %all-reduce.5.cloned.1.call-update) | async-done | bytes 98320
  584.2 12.2 fusion.5
  596.5 7.6 multiply_reduce_fusion.2
  622.8 8.9 multiply_reduce_fusion
  653.4 6.8 convolution_convert_fusion.5
  662.8 8.6 fusion.14
  688.6 9.9 bitcast_convert_fusion.1
  700.3 9.8 bitcast_convert_fusion
  716.4 9.3 add_convert_fusion
  729.4 13.2 reduce-scatter.35.cloned.1.call-done
  742.7 32.2 %reduce-scatter.27.cloned.1.call-done = bf16[192,768]{1,0:T(8,128)(2,1)} async-done(((bf16[768,768]{1,0:T(8,128)(2,1)}), bf16[192,768]{1,0:T(8,128)(2,1)}) %reduce-scatter.27.cloned.1.call-update) | async-done | bytes 294928 | tf_op jit(solution)/shard_map/reduce_scatter | solution.py:274
  774.8 50.5 %reduce-scatter.41.cloned.1.call-done = bf16[192,2304]{1,0:T(8,128)(2,1)} async-done(((bf16[768,2304]{1,0:T(8,128)(2,1)}), bf16[192,2304]{1,0:T(8,128)(2,1)}) %reduce-scatter.41.cloned.1.call-update) | async-done | bytes 884752
  826.9 49.0 %reduce-scatter.33.cloned.1.call-done = bf16[192,2304]{1,0:T(8,128)(2,1)} async-done(((bf16[768,2304]{1,0:T(8,128)(2,1)}), bf16[192,2304]{1,0:T(8,128)(2,1)}) %reduce-scatter.33.cloned.1.call-update) | async-done | bytes 884752 | tf_op jit(solution)/shard_map/reduce_scatter | solution.py:289
  875.8 60.3 %reduce-scatter.37.cloned.1.call-done = bf16[192,3072]{1,0:T(8,128)(2,1)} async-done(((bf16[768,3072]{1,0:T(8,128)(2,1)}), bf16[192,3072]{1,0:T(8,128)(2,1)}) %reduce-scatter.37.cloned.1.call-update) | async-done | bytes 1179664 | tf_op jit(solution)/shard_map/reduce_scatter | solution.py:295
  936.2 60.2 %reduce-scatter.39.cloned.1.call-done = bf16[768,768]{1,0:T(8,128)(2,1)} async-done(((bf16[3072,768]{1,0:T(8,128)(2,1)}), bf16[768,768]{1,0:T(8,128)(2,1)}) %reduce-scatter.39.cloned.1.call-update) | async-done | bytes 1179664 | tf_op jit(solution)/shard_map/reduce_scatter | solution.py:298
  996.4 60.4 %reduce-scatter.29.cloned.1.call-done = bf16[192,3072]{1,0:T(8,128)(2,1)} async-done(((bf16[768,3072]{1,0:T(8,128)(2,1)}), bf16[192,3072]{1,0:T(8,128)(2,1)}) %reduce-scatter.29.cloned.1.call-update) | async-done | bytes 1179664 | tf_op jit(solution)/shard_map/reduce_scatter | solution.py:277
  1056.8 60.4 %reduce-scatter.31.cloned.1.call-done = bf16[768,768]{1,0:T(8,128)(2,1)} async-done(((bf16[3072,768]{1,0:T(8,128)(2,1)}), bf16[768,768]{1,0:T(8,128)(2,1)}) %reduce-scatter.31.cloned.1.call-update) | async-done | bytes 1179664 | tf_op jit(solution)/shard_map/reduce_scatter | solution.py:280
  1117.2 291.8 %all-reduce.6 = (f32[192,2304]{0,1:T(8,128)S(1)}, f32[192,768]{1,0:T(8,128)}, f32[192,3072]{1,0:T(8,128)}, f32[768,768]{1,0:T(8,128)}, f32[2,192]{1,0:T(2,128)},...) all-reduce(bf16[192,2304]{0,1:T(8,128)(2,1)S(1)} %copy.144, ...), channel_id=1, replica_groups=mesh['fsdp'=4,'rep'=8] {'rep'}, use_global_device_ids=true, to_apply=%region_24.25 | all-reduce | flops 3546624 | bytes 21279744 | tf_op jit(solution)/shard_map/psum | solution.py:325
  (316 shorter events, 160.3 us)
Async XLA Ops:
  7.2 89.2 %copy-start.55 = (bf16[32,24]{0,1:T(8,128)(2,1)S(1)}, bf16[32,24]{0,1:T(8,128)(2,1)}, u32[]{:S(2)}) copy-start(bf16[32,24]{0,1:T(8,128)(2,1)} %param.35) | copy-start | bytes 4612
  7.2 207.8 %all-gather.13.cloned.1.call-start = ((), (), s32[]{:S(2)}) async-start(), calls=%async_computation.13 | async-start | bytes 3649536 | tf_op jit(solution)/shard_map/all_gather | solution.py:144
  8.0 233.1 %all-gather.15.cloned.1.call-start = ((), (), s32[]{:S(2)}) async-start(), calls=%async_computation.14 | async-start | bytes 1216512 | tf_op jit(solution)/shard_map/all_gather | solution.py:145
  8.7 237.3 %all-gather.17.cloned.1.call-start = ((), (), s32[]{:S(2)}) async-start(), calls=%async_computation.15 | async-start | bytes 4866048 | tf_op jit(solution)/shard_map/all_gather | solution.py:146
  9.4 126.1 %copy-start.61 = (bf16[2,24]{1,0:T(2,128)(2,1)S(1)}, bf16[2,24]{1,0:T(2,128)(2,1)}, u32[]{:S(2)}) copy-start(bf16[2,24]{1,0:T(2,128)(2,1)} %param.33) | copy-start | bytes 292
  9.4 252.0 %all-gather.19.cloned.1.call-start = ((), (), s32[]{:S(2)}) async-start(), calls=%async_computation.16 | async-start | bytes 4866048 | tf_op jit(solution)/shard_map/all_gather | solution.py:147
  10.0 313.4 %all-gather.21.cloned.1.call-start = ((), (), s32[]{:S(2)}) async-start(), calls=%async_computation.17 | async-start | bytes 3649536 | tf_op jit(solution)/shard_map/all_gather | solution.py:158
  10.6 368.7 %all-gather.23.cloned.1.call-start = ((), (), s32[]{:S(2)}) async-start(), calls=%async_computation.18 | async-start | bytes 1216512 | tf_op jit(solution)/shard_map/all_gather | solution.py:159
  11.2 433.8 %all-gather.25.cloned.1.call-start = ((), (), s32[]{:S(2)}) async-start(), calls=%async_computation.19 | async-start | bytes 4866048 | tf_op jit(solution)/shard_map/all_gather | solution.py:160
  11.9 498.5 %all-gather.27.cloned.1.call-start = ((), (), s32[]{:S(2)}) async-start(), calls=%async_computation.20 | async-start | bytes 4866048 | tf_op jit(solution)/shard_map/all_gather | solution.py:161
  12.7 561.6 %all-reduce.5.cloned.1.call-start = ((), (), s32[]{:S(2)}) async-start(), calls=%async_computation.34 | async-start | bytes 196608
  16.0 207.5 %copy-start.1 = (f32[8,128,768]{2,1,0:T(8,128)}, f32[8,128,768]{2,1,0:T(8,128)S(1)}, u32[]{:S(2)}) copy-start(f32[8,128,768]{2,1,0:T(8,128)S(1)} %convert.90) | copy-start | bytes 9437188
  16.7 254.6 %copy-start.34 = (f32[8,128]{1,0:T(8,128)}, f32[8,128]{1,0:T(8,128)S(1)}, u32[]{:S(2)}) copy-start(f32[8,128]{1,0:T(8,128)S(1)} %get-tuple-element.123) | copy-start | bytes 12292
  211.0 234.0 %copy-start.38 = (f32[768]{0:T(1024)}, f32[768]{0:T(1024)S(1)}, u32[]{:S(2)}) copy-start(f32[768]{0:T(1024)S(1)} %get-tuple-element.101) | copy-start | bytes 9220
  336.3 111.8 %copy-start.16 = (bf16[32,12,64]{2,1,0:T(8,128)(2,1)}, bf16[32,12,64]{2,1,0:T(8,128)(2,1)S(1)}, u32[]{:S(2)}) copy-start(bf16[32,12,64]{2,1,0:T(8,128)(2,1)S(1)} %reshape.652) | copy-start | bytes 147460
  336.4 108.6 %copy-start.22 = (bf16[8,12,64]{2,1,0:T(8,128)(2,1)}, bf16[8,12,64]{2,1,0:T(8,128)(2,1)S(1)}, u32[]{:S(2)}) copy-start(bf16[8,12,64]{2,1,0:T(8,128)(2,1)S(1)} %reshape.651) | copy-start | bytes 36868
  338.9 106.1 %copy-start.23 = (bf16[8,768]{1,0:T(8,128)(2,1)}, bf16[8,768]{1,0:T(8,128)(2,1)S(1)}, u32[]{:S(2)}) copy-start(bf16[8,768]{1,0:T(8,128)(2,1)S(1)} %reshape.653) | copy-start | bytes 36868
  381.0 64.0 %copy-start.42 = (f32[8]{0:T(128)}, f32[8]{0:T(128)S(1)}, u32[]{:S(2)}) copy-start(f32[8]{0:T(128)S(1)} %broadcast_multiply_fusion.11) | copy-start | bytes 100
  448.1 66.0 %copy-start.20 = (f32[8,1,768]{2,1,0:T(1,128)S(1)}, f32[8,1,768]{2,1,0:T(1,128)}, u32[]{:S(2)}) copy-start(f32[8,1,768]{2,1,0:T(1,128)} %slice.128) | copy-start | bytes 73732
  533.4 180.0 %reduce-scatter.47.cloned.1.call-start = ((), (), s32[]{:S(2)}) async-start(), calls=%async_computation.31 | async-start | bytes 245760
  537.5 177.5 %reduce-scatter.49.cloned.1.call-start = ((), (), s32[]{:S(2)}) async-start(), calls=%async_computation.32 | async-start | bytes 245760
  539.2 186.5 %reduce-scatter.45.cloned.1.call-start = ((), (), s32[]{:S(2)}) async-start(), calls=%async_computation.30 | async-start | bytes 245760
  605.0 122.1 %reduce-scatter.43.cloned.1.call-start = ((), (), s32[]{:S(2)}) async-start(), calls=%async_computation.29 | async-start | bytes 245760
  605.9 122.6 %reduce-scatter.51.cloned.1.call-start = ((), (), s32[]{:S(2)}) async-start(), calls=%async_computation.33 | async-start | bytes 245760
  606.8 135.8 %reduce-scatter.35.cloned.1.call-start = ((), (), s32[]{:S(2)}) async-start(), calls=%async_computation.25 | async-start | bytes 1474560 | tf_op jit(solution)/shard_map/reduce_scatter | solution.py:292
  608.5 166.4 %reduce-scatter.27.cloned.1.call-start = ((), (), s32[]{:S(2)}) async-start(), calls=%async_computation.21 | async-start | bytes 1474560 | tf_op jit(solution)/shard_map/reduce_scatter | solution.py:274
  631.8 193.5 %reduce-scatter.41.cloned.1.call-start = ((), (), s32[]{:S(2)}) async-start(), calls=%async_computation.28 | async-start | bytes 4423680
  677.2 198.6 %reduce-scatter.33.cloned.1.call-start = ((), (), s32[]{:S(2)}) async-start(), calls=%async_computation.24 | async-start | bytes 4423680 | tf_op jit(solution)/shard_map/reduce_scatter | solution.py:289
  680.2 256.0 %reduce-scatter.37.cloned.1.call-start = ((), (), s32[]{:S(2)}) async-start(), calls=%async_computation.26 | async-start | bytes 5898240 | tf_op jit(solution)/shard_map/reduce_scatter | solution.py:295
  684.2 312.2 %reduce-scatter.39.cloned.1.call-start = ((), (), s32[]{:S(2)}) async-start(), calls=%async_computation.27 | async-start | bytes 5898240 | tf_op jit(solution)/shard_map/reduce_scatter | solution.py:298
  687.9 368.9 %reduce-scatter.29.cloned.1.call-start = ((), (), s32[]{:S(2)}) async-start(), calls=%async_computation.22 | async-start | bytes 5898240 | tf_op jit(solution)/shard_map/reduce_scatter | solution.py:277
  698.5 418.7 %reduce-scatter.31.cloned.1.call-start = ((), (), s32[]{:S(2)}) async-start(), calls=%async_computation.23 | async-start | bytes 5898240 | tf_op jit(solution)/shard_map/reduce_scatter | solution.py:280
  (56 other events, 747.4 us)
Sparse Core Ops, SparseCore 0:
  11.1 63.0 all-gather.12
  77.2 52.9 all-gather.14
  133.2 62.7 all-gather.16
  198.9 62.4 all-gather.18
  264.3 59.0 all-gather.20
  326.3 52.9 all-gather.22
  382.3 62.5 all-gather.24
  448.0 62.4 all-gather.26
  533.6 40.6 all-reduce.4
  577.7 23.9 reduce-scatter.46
  604.7 23.9 reduce-scatter.48
  632.1 23.9 reduce-scatter.44
  659.6 23.9 reduce-scatter.42
  686.5 23.9 reduce-scatter.50
  714.1 28.5 reduce-scatter.34
  746.3 28.5 reduce-scatter.26
  778.1 47.2 reduce-scatter.40
  828.6 47.2 reduce-scatter.32
  879.1 57.0 reduce-scatter.36
  939.3 57.0 reduce-scatter.38
  999.7 57.0 reduce-scatter.28
  1060.0 57.0 reduce-scatter.30
where the time goes:
time: 1420 us
  waiting for transfers between devices  646 us (45%)
  blocking collectives  494 us (35%)
  matrix products  172 us (12%)
  local copies, waits for them, and re-layouts  62.4 us (4%)
  other arithmetic  26.5 us (2%)
  between operations  16.3 us (1%)
    psum x1, blocking collectives, per_device(): lax.psum((grad_qkv, grad_out, grad_up, grad_down, grad_gains, grad_biases...  292 us
    dot_general x36, matrix products, product(): jnp.einsum(einsum_form, left_op, right_op, preferred_element_type=jnp.flo...  172 us
    unnamed x29, waiting for transfers between devices  90.8 us
    all_gather x1, waiting for transfers between devices, per_device(): lax.all_gather(cse_up, ('fsdp', 'rep'), axis=0, tiled=True)  63.8 us
    all_gather x1, waiting for transfers between devices, per_device(): lax.all_gather(cse_down, ('fsdp', 'rep'), axis=0, tiled=True)  62.4 us
    reduce_scatter x1, waiting for transfers between devices, per_device(): lax.psum_scatter(grad_up.astype(jnp.bfloat16), 'fsdp', scatter_dimension=...  60.4 us
    reduce_scatter x1, waiting for transfers between devices, per_device(): lax.psum_scatter(grad_down.astype(jnp.bfloat16), 'fsdp', scatter_dimensio...  60.4 us
    reduce_scatter x1, waiting for transfers between devices, per_device(): lax.psum_scatter(cross_up.astype(jnp.bfloat16), 'fsdp', scatter_dimension...  60.3 us
  transfers between devices with their start and end apart: 22, of which 14 were waited for; matrix products, arithmetic and copies ran while one was open for 16% of the time, Pallas kernels for 0%

commit v1 on v0

v1 whole, which is shorter than its diff:
```python
import math

import jax
import jax.numpy as jnp
from jax import lax
from jax.sharding import Mesh
from jax.sharding import PartitionSpec as P

HEAD = 64
norm_eps = 1e-05
masked_score = -1000000000.0
bf16, f32 = jnp.bfloat16, jnp.float32


def product(left_op, right_op, einsum_form):
    return jnp.einsum(einsum_form, left_op, right_op, preferred_element_type=f32)


def swap(value, axis, bit):
    size = lax.axis_size(axis)
    return lax.ppermute(value, axis, [(i, i ^ bit) for i in range(size)])


def bit_of(axis, bit):
    return (lax.axis_index(axis) // bit) % 2


def join(mine, other, side, axis):
    first = side == 0
    return jnp.stack([jnp.where(first, mine, other), jnp.where(first, other, mine)], axis=axis)


def part(value, side, axis):
    return lax.dynamic_index_in_dim(value, side, axis, keepdims=False)


def bits_down(size):
    return [1 << k for k in reversed(range(size.bit_length() - 1))]


def gather_z(value):
    size = lax.axis_size("z")
    inner = value.shape
    got = value[None]
    for level, bit in enumerate(bits_down(size)):
        other = swap(got, "z", bit)
        got = join(got, other, bit_of("z", bit), 1)
        got = got.reshape((2 ** (level + 1),) + inner)
    return got


def gather_c(value, axis):
    return join(value, swap(value, "c", 1), lax.axis_index("c"), axis)


def gather_rows(shard):
    rows, cols = shard.shape
    col_z = gather_z(shard)
    half = (cols // 256) * 128
    one, two = col_z[:, :, :half], col_z[:, :, half:]
    y, x = lax.axis_index("y"), lax.axis_index("x")
    one = join(one, swap(one, "x", 1), x, 0)
    two = join(two, swap(two, "y", 1), y, 0)
    one = join(one, swap(one, "y", 1), y, 0)
    two = join(two, swap(two, "x", 1), x, 1)
    both = jnp.concatenate([one, two], axis=-1)
    both = gather_c(both, 3)
    return both.reshape(-1, cols)


def swap_f(value, dist):
    count = lax.axis_size("y") * lax.axis_size("x")
    return lax.ppermute(value, ("y", "x"), [(i, i ^ dist) for i in range(count)])


def in_order(parts):
    y, x = lax.axis_index("y"), lax.axis_index("x")
    row0 = [jnp.where(x == 0, parts[0], parts[1]), jnp.where(x == 0, parts[1], parts[0])]
    row1 = [jnp.where(x == 0, parts[2], parts[3]), jnp.where(x == 0, parts[3], parts[2])]
    top, low = jnp.stack(row0), jnp.stack(row1)
    return jnp.concatenate([jnp.where(y == 0, top, low), jnp.where(y == 0, low, top)])


def gather_f(value):
    return in_order([value] + [swap_f(value, d) for d in (1, 2, 3)])


def sum_f(value):
    got = [value] + [swap_f(value, d) for d in (1, 2, 3)]
    return (got[0] + got[1]) + (got[2] + got[3])


def reduce_rows(grad):
    rows, cols = grad.shape
    zsize = lax.axis_size("z")
    count = lax.axis_size("y") * lax.axis_size("x")
    y, x, c = lax.axis_index("y"), lax.axis_index("x"), lax.axis_index("c")
    f = y * lax.axis_size("x") + x
    per = rows // count // 2
    halves = grad.reshape(count, 2, per, cols)
    other = swap(part(halves, 1 - c, 1), "c", 1)
    chip = (part(halves, c, 1).astype(f32) + other.astype(f32)).astype(bf16)
    got = [part(chip, f, 0)] + [swap_f(part(chip, f ^ d, 0), d) for d in (1, 2, 3)]
    got = [g.astype(f32) for g in got]
    plane = ((got[0] + got[1]) + (got[2] + got[3])).astype(bf16)
    left = plane.reshape(zsize, per // zsize, cols)
    bit = 1
    while bit < zsize:
        side = bit_of("z", bit)
        pairs = left.reshape((-1, 2) + left.shape[1:])
        other = swap(part(pairs, 1 - side, 1), "z", bit)
        left = (part(pairs, side, 1).astype(f32) + other.astype(f32)).astype(bf16)
        bit *= 2
    whole = gather_z(left[0]).reshape(per, cols)
    return gather_c(whole, 0).reshape(2 * per, cols)


def normalize(summed_in, gain_row, bias_row):
    row_mean = jnp.mean(summed_in, axis=-1, keepdims=True)
    centered = summed_in - row_mean
    inv_dev = lax.rsqrt(jnp.mean(centered * centered, axis=-1, keepdims=True) + norm_eps)
    unit_rows = centered * inv_dev
    return (unit_rows * gain_row + bias_row, unit_rows, inv_dev)


def norm_back(upstream, unit_rows, inv_dev, gain_row):
    scaled = upstream * gain_row
    grad_in = inv_dev * (
        scaled
        - jnp.mean(scaled, axis=-1, keepdims=True)
        - unit_rows * jnp.mean(scaled * unit_rows, axis=-1, keepdims=True)
    )
    sums = tuple(range(upstream.ndim - 1))
    return (grad_in, jnp.sum(upstream * unit_rows, axis=sums), jnp.sum(upstream, axis=sums))


def gelu_pair(inner_pre):
    cumul = 0.5 * (1.0 + lax.erf(inner_pre * 0.7071067811865476))
    return (
        inner_pre * cumul,
        cumul + inner_pre * jnp.exp(-0.5 * inner_pre * inner_pre) * 0.3989422804014327,
    )


def masked_scores(query_rows, key_rows, key_mask):
    raw_scores = product(query_rows, key_rows, "gqhe,gkhe->ghqk") * (1.0 / math.sqrt(HEAD))
    return jnp.where(key_mask[:, None, None, :], raw_scores, masked_score)


def attend(query_rows, key_rows, value_rows, key_mask):
    scores = masked_scores(query_rows, key_rows, key_mask)
    row_max = jnp.max(scores, axis=-1, keepdims=True)
    log_total = row_max + jnp.log(jnp.sum(jnp.exp(scores - row_max), axis=-1, keepdims=True))
    softmax_w = jnp.exp(scores - log_total).astype(bf16)
    mixed_heads = product(softmax_w, value_rows, "ghqk,gkhe->gqhe").astype(bf16)
    return (mixed_heads, log_total)


def attend_back(query_rows, key_rows, value_rows, key_mask, log_total, grad_mixed):
    scores = masked_scores(query_rows, key_rows, key_mask)
    softmax_w = jnp.exp(scores - log_total)
    grad_value = product(softmax_w.astype(bf16), grad_mixed, "ghqk,gqhe->gkhe")
    grad_probs = product(grad_mixed, value_rows, "gqhe,gkhe->ghqk")
    grad_scores = (
        softmax_w * (grad_probs - jnp.sum(softmax_w * grad_probs, axis=-1, keepdims=True))
    ).astype(bf16)
    inv_root = 1.0 / math.sqrt(HEAD)
    grad_query = product(grad_scores, key_rows, "ghqk,gkhe->gqhe") * inv_root
    grad_key = product(grad_scores, query_rows, "ghqk,gqhe->gkhe") * inv_root
    return (grad_query, grad_key, grad_value)


def split_heads(packed, head_count):
    stacked = packed.reshape(packed.shape[0], packed.shape[1], 3, head_count, HEAD)
    return (stacked[:, :, 0], stacked[:, :, 1], stacked[:, :, 2])


def finish(resid_in, mixed_flat, proj_out, proj_up, proj_down, gain_rows, bias_rows):
    attended = product(mixed_flat, proj_out, "gsd,de->gse")
    first_norm, unit_one, inv_one = normalize(resid_in + attended, gain_rows[0], bias_rows[0])
    first_low = first_norm.astype(bf16)
    inner_pre = product(first_low, proj_up, "gsd,df->gsf")
    activated, gelu_slope = gelu_pair(inner_pre)
    act_low = activated.astype(bf16)
    outer_out = product(act_low, proj_down, "gsf,fd->gsd")
    normed_out, unit_two, inv_two = normalize(first_norm + outer_out, gain_rows[1], bias_rows[1])
    return (normed_out, (unit_one, inv_one, first_low, gelu_slope, act_low, unit_two, inv_two))


def finish_back(upstream, mixed_flat, saved_parts, proj_out, proj_up, proj_down, gain_rows):
    unit_one, inv_one, first_low, gelu_slope, act_low, unit_two, inv_two = saved_parts
    grad_two, gain_two, bias_two = norm_back(upstream, unit_two, inv_two, gain_rows[1])
    grad_outer = grad_two.astype(bf16)
    grad_down = product(act_low, grad_outer, "gsf,gsd->fd")
    grad_inner = (product(grad_outer, proj_down, "gsd,fd->gsf") * gelu_slope).astype(bf16)
    grad_up = product(first_low, grad_inner, "gsd,gsf->df")
    grad_first = grad_two + product(grad_inner, proj_up, "gsf,df->gsd")
    grad_one, gain_one, bias_one = norm_back(grad_first, unit_one, inv_one, gain_rows[0])
    grad_attended = grad_one.astype(bf16)
    grad_out = product(mixed_flat, grad_attended, "gsd,gse->de")
    grad_mixed = product(grad_attended, proj_out, "gse,de->gsd").astype(bf16)
    return (grad_one, grad_mixed, grad_out, grad_up, grad_down, (gain_one, gain_two, bias_one, bias_two))


def cross_weights(cse_qkv, cse_out, cse_up, cse_down, fsize, f):
    rows, width = cse_qkv.shape[0], cse_out.shape[1]
    ff = cse_up.shape[1]
    slim = width // fsize
    cols = jnp.concatenate(
        [
            cse_qkv.reshape(rows, 3, fsize, slim).transpose(2, 0, 1, 3).reshape(fsize, rows, 3 * slim),
            cse_up.reshape(rows, fsize, ff // fsize).transpose(1, 0, 2),
        ],
        axis=-1,
    )
    mine = in_order([part(cols, f, 0)] + [swap_f(part(cols, f ^ d, 0), d) for d in (1, 2, 3)])
    flat = mine.reshape(fsize * rows, -1)
    frows = cse_down.shape[0]
    out_flat = cse_out.reshape(frows, -1)
    message = jnp.concatenate([flat, cse_down, out_flat], axis=-1)
    whole = gather_c(gather_z(message), 1)
    reps = whole.shape[0] * whole.shape[1]
    whole = whole.reshape(reps, frows, -1)
    a, b = 3 * slim, 3 * slim + ff // fsize
    by_row = whole[:, :, :b].reshape(reps, fsize, rows, b).transpose(1, 0, 2, 3).reshape(-1, b)
    qkv = by_row[:, :a]
    up = by_row[:, a:]
    down = whole[:, :, b : b + width].reshape(-1, width)
    out = whole[:, :, b + width :].reshape(-1, width)
    return qkv, out, up, down


def cross_block(cls_in, cotan, weights, gains, biases, fsize, f):
    qkv, out, up, down = weights
    segs, width = cls_in.shape
    slim = width // fsize
    heads = slim // HEAD
    packed = product(cls_in[None], qkv, "gsd,de->gse").astype(bf16)
    queries, keys, values = split_heads(packed, heads)
    every = jnp.ones((1, segs), jnp.bool_)
    mixed, log_total = attend(queries, keys, values, every)
    mixed = mixed.reshape(segs, slim)
    attended = sum_f(product(mixed, out, "sd,de->se"))
    first, unit_one, inv_one = normalize(cls_in.astype(f32) + attended, gains[0], biases[0])
    first_low = first.astype(bf16)
    activated, slope = gelu_pair(product(first_low, up, "sd,df->sf"))
    act_low = activated.astype(bf16)
    outer = sum_f(product(act_low, down, "sf,fd->sd"))
    cls_out, unit_two, inv_two = normalize(first + outer, gains[1], biases[1])

    grad_two, gain_two, bias_two = norm_back(cotan, unit_two, inv_two, gains[1])
    grad_outer = grad_two.astype(bf16)
    grad_inner = (product(grad_outer, down, "sd,fd->sf") * slope).astype(bf16)
    grad_first = grad_two + sum_f(product(grad_inner, up, "sf,df->sd"))
    grad_one, gain_one, bias_one = norm_back(grad_first, unit_one, inv_one, gains[0])
    grad_attended = grad_one.astype(bf16)
    grad_mixed = product(grad_attended, out, "se,de->sd").astype(bf16)
    grad_q, grad_k, grad_v = attend_back(
        queries, keys, values, every, log_total, grad_mixed.reshape(1, segs, heads, HEAD)
    )
    grad_packed = jnp.concatenate(
        [grad_q.reshape(segs, slim), grad_k.reshape(segs, slim), grad_v.reshape(segs, slim)], axis=-1
    ).astype(bf16)
    grad_in = grad_one + sum_f(product(grad_packed, qkv, "se,de->sd"))

    def own(value):
        return lax.dynamic_slice_in_dim(value, f * slim, slim, value.ndim - 1)

    sums = jnp.stack([gain_one, gain_two, bias_one, bias_two])
    sums = jnp.pad(own(sums), ((0, segs - 4), (0, 0)))
    spread = gather_f(jnp.concatenate([grad_packed, grad_inner], axis=-1))
    qkv_cols = spread[:, :, : 3 * slim].reshape(fsize, segs, 3, slim).transpose(1, 2, 0, 3)
    up_cols = spread[:, :, 3 * slim :].transpose(1, 0, 2)
    pieces = [
        qkv_cols.reshape(segs, 3 * width),
        up_cols.reshape(segs, -1),
        act_low,
        grad_outer,
        grad_attended,
        mixed,
        own(cls_in),
        own(first_low),
        own(grad_in).astype(bf16),
        sums.astype(bf16),
    ]
    ends, at = [], 0
    for piece in pieces:
        ends.append((at, at + piece.shape[1]))
        at += piece.shape[1]
    docs = gather_c(gather_z(jnp.concatenate(pieces, axis=-1)), 1)
    docs = docs.reshape(-1, segs, at)
    flat = docs.reshape(-1, at)
    cut = [flat[:, a:b] for a, b in ends]
    g_qkv = product(cut[6], cut[0], "rd,re->de")
    g_out = product(cut[5], cut[4], "rd,re->de")
    g_up = product(cut[7], cut[1], "rd,re->de")
    g_down = product(cut[2], cut[3], "rd,re->de")
    g_pos = jnp.sum(docs[:, :, ends[8][0] : ends[8][1]].astype(f32), axis=0)
    g_sums = jnp.sum(docs[:, :4, ends[9][0] : ends[9][1]].astype(f32), axis=0)
    return cls_out, grad_in, (g_qkv, g_out, g_up, g_down, g_sums[0:2], g_sums[2:4], g_pos)


def per_device(
    tokens, counts, cotangent,
    swe_qkv, swe_out, swe_up, swe_down, swe_gains, swe_biases,
    cse_qkv, cse_out, cse_up, cse_down, cse_gains, cse_biases, positions,
):
    docs_here, local_len, width = tokens.shape
    seg_here = counts.shape[1]
    seg_len = local_len // seg_here
    groups = docs_here * seg_here
    head_count = width // HEAD
    fsize = lax.axis_size("y") * lax.axis_size("x")
    f = lax.axis_index("y") * lax.axis_size("x") + lax.axis_index("x")
    segs = fsize * seg_here

    small = jnp.concatenate([swe_gains, swe_biases, cse_gains, cse_biases, positions], axis=0)
    count_small = small.shape[0]
    small = jnp.pad(small.T, ((0, 0), (0, -count_small % 128)))
    first_group = gather_rows(jnp.concatenate([swe_qkv, swe_out, small], axis=-1))
    w_qkv = first_group[:, : 3 * width]
    w_out = first_group[:, 3 * width : 4 * width]
    rows = first_group[:, 4 * width : 4 * width + count_small].T.astype(f32)
    gains, biases, cross_gains, cross_biases, pos = (
        rows[0:2], rows[2:4], rows[4:6], rows[6:8], rows[8:]
    )
    w_up = gather_rows(swe_up)
    w_down = gather_rows(swe_down)
    cross = cross_weights(cse_qkv, cse_out, cse_up, cse_down, fsize, f)

    seg_rows = tokens.reshape(groups, seg_len, width)
    is_valid = jnp.arange(seg_len, dtype=jnp.int32)[None, :] < counts.reshape(groups, 1)
    valid_f = is_valid.astype(f32)[..., None]
    packed = product(seg_rows, w_qkv, "gsd,de->gse").astype(bf16)
    queries, keys, values = split_heads(packed, head_count)
    mixed, log_total = attend(queries, keys, values, is_valid)
    mixed = mixed.reshape(groups, seg_len, width)
    normed, saved = finish(seg_rows.astype(f32), mixed, w_out, w_up, w_down, gains, biases)
    hidden = normed * valid_f

    pos_here = lax.dynamic_slice_in_dim(pos, f * seg_here, seg_here, 0)
    cls_here = (hidden[:, 0, :] + pos_here).astype(bf16)
    upstream = cotangent.reshape(groups, seg_len, width)
    both = gather_f(jnp.concatenate([cls_here, upstream[:, 0, :]], axis=-1)).reshape(segs, 2 * width)
    cls_out, cls_grad, cross_grads = cross_block(
        both[:, :width], both[:, width:].astype(f32), cross, cross_gains, cross_biases, fsize, f
    )
    cls_out = lax.dynamic_slice_in_dim(cls_out, f * seg_here, seg_here, 0)
    cls_grad = lax.dynamic_slice_in_dim(cls_grad, f * seg_here, seg_here, 0)
    layer_out = hidden.at[:, 0, :].set(cls_out).astype(bf16).reshape(tokens.shape)

    grad_hidden = upstream.astype(f32).at[:, 0, :].set(cls_grad) * valid_f
    resid, grad_mixed, grad_out, grad_up, grad_down, sums = finish_back(
        grad_hidden, mixed, saved, w_out, w_up, w_down, gains
    )
    sums = jnp.pad(jnp.stack(sums, axis=1), ((0, 0), (0, 124)))
    red_down = reduce_rows(grad_down.astype(bf16))
    red_up = reduce_rows(grad_up.astype(bf16))
    grad_q, grad_k, grad_v = attend_back(
        queries, keys, values, is_valid, log_total,
        grad_mixed.reshape(groups, seg_len, head_count, HEAD),
    )
    grad_packed = jnp.concatenate(
        [g.reshape(groups, seg_len, width) for g in (grad_q, grad_k, grad_v)], axis=2
    ).astype(bf16)
    grad_qkv = product(seg_rows, grad_packed, "gsd,gse->de")
    last = reduce_rows(jnp.concatenate([grad_qkv, grad_out, sums], axis=-1).astype(bf16)).astype(f32)
    token_grad = (resid + product(grad_packed, w_qkv, "gse,de->gsd")).astype(bf16)
    small_grads = last[:, 4 * width : 4 * width + 4].T
    return (
        layer_out,
        token_grad.reshape(tokens.shape),
        last[:, : 3 * width],
        last[:, 3 * width : 4 * width],
        red_up.astype(f32),
        red_down.astype(f32),
        small_grads[0:2],
        small_grads[2:4],
    ) + cross_grads


def solution(mesh):
    fsize, rsize = mesh.shape["fsdp"], mesh.shape["rep"]
    fine = Mesh(mesh.devices.reshape(2, fsize // 2, rsize // 2, 2), ("y", "x", "z", "c"))
    fs, rep = ("y", "x"), ("z", "c")
    every = fs + rep
    by_rows, by_cols = P(every, None), P(None, every)
    block = (by_rows,) * 4 + (by_cols,) * 2
    grads = (P(fs, None),) * 4 + (P(None, fs),) * 2
    return jax.shard_map(
        per_device,
        mesh=fine,
        in_specs=(P(rep, fs, None), P(rep, fs), P(rep, fs, None)) + block + block + (by_cols,),
        out_specs=(P(rep, fs, None),) * 2 + grads + grads + (P(None, fs),),
        check_vma=False,
    )
```

time: 1420 us -> 527 us (0.37)
  blocking collectives: 494 us -> 0 us
  waiting for transfers between devices: 646 us -> 190 us
  starting transfers between devices: 1.27 us -> 85.1 us
  matrix products: 172 us -> 117 us
  other arithmetic: 26.5 us -> 54.7 us
    reduce_scatter x7 -> x0, waiting for transfers between devices: 336 us -> none  [the longest x1 60.4 us: per_device(): lax.psum_scatter(grad_up.astype(jnp.bfloat16), 'fsdp', scatter_dimension=...]
    psum x1 -> x0, blocking collectives: 292 us -> none  [per_device(): lax.psum((grad_qkv, grad_out, grad_up, grad_down, grad_gains, grad_biases...]
    all_gather x8 -> x0, waiting for transfers between devices: 219 us -> none  [the longest x1 63.8 us: per_device(): lax.all_gather(cse_up, ('fsdp', 'rep'), axis=0, tiled=True)]
    all_gather x6 -> x0, blocking collectives: 202 us -> none  [the longest x1 43 us: per_device(): lax.all_gather(swe_gains, ('fsdp', 'rep'), axis=1, tiled=True)]
    ppermute x0 -> x75, waiting for transfers between devices: none -> 190 us  [the longest x45 117 us: swap(): return lax.ppermute(value, axis, [(i, i ^ bit) for i in range(size)])]
    unnamed x29 -> x0, waiting for transfers between devices: 90.8 us -> none
    ppermute x0 -> x75, starting transfers between devices: none -> 85.1 us  [the longest x45 48.7 us: swap(): return lax.ppermute(value, axis, [(i, i ^ bit) for i in range(size)])]
    dot_general x36, matrix products: 172 us -> 117 us  [product(): jnp.einsum(einsum_form, left_op, right_op, preferred_element_type=f32)]
  transfers between devices with their start and end apart: 22 -> 75, of which waited for: 14 -> 40; matrix products, arithmetic and copies ran while one was open for 16% -> 19% of each run, Pallas kernels for 0% -> 0%
where the time goes in v1:
time: 527 us; the launch traced here: 519 us
  waiting for transfers between devices  190 us (36%)
  matrix products  117 us (22%)
  starting transfers between devices  85.1 us (16%)
  local copies, waits for them, and re-layouts  68.8 us (13%)
  other arithmetic  54.7 us (10%)
    ppermute x45, waiting for transfers between devices, swap(): return lax.ppermute(value, axis, [(i, i ^ bit) for i in range(size)])  117 us
    dot_general x36, matrix products, product(): jnp.einsum(einsum_form, left_op, right_op, preferred_element_type=f32)  117 us
    ppermute x30, waiting for transfers between devices, swap_f(): lax.ppermute(value, ('y', 'x'), [(i, i ^ dist) for i in range(count)])  72.8 us
    ppermute x45, starting transfers between devices, swap(): return lax.ppermute(value, axis, [(i, i ^ bit) for i in range(size)])  48.7 us
    ppermute x30, starting transfers between devices, swap_f(): lax.ppermute(value, ('y', 'x'), [(i, i ^ dist) for i in range(count)])  36.4 us
    unnamed x194, local copies, waits for them, and re-layouts  18.2 us
    another operation x56, other arithmetic, join(): jnp.stack([jnp.where(first, mine, other), jnp.where(first, other, mine)],...  12.8 us
  transfers between devices with their start and end apart: 75, of which 40 were waited for; matrix products, arithmetic and copies ran while one was open for 19% of the time, Pallas kernels for 0%

profile of v1, /device:TPU:0, one launch (start us, length us, event | category | flops | bytes accessed | tf_op | source)
XLA Modules:
  0.0 519.3 jit_solution(4504855303358312149)
XLA Ops:
  0.7 4.1 collective-permute-start.14
  28.5 3.6 collective-permute-start.1
  32.1 18.8 %collective-permute-done.8 = bf16[2,24,3072]{2,1,0:T(8,128)(2,1)S(1)} collective-permute-done((bf16[2,24,3072]{2,1,0:T(8,128)(2,1)S(1)}, bf16[2,24,3072]{2,1,0:T(8,128)(2,1)S(1)}, u32[]{:S(2)}, u32[]{:S(2)}) %collective-permute-start.8) | collective-permute-done | bytes 294944 | tf_op jit(solution)/shard_map/ppermute | solution.py:21
  58.1 8.2 %collective-permute-done.16 = bf16[4,96,384]{2,1,0:T(8,128)(2,1)S(1)} collective-permute-done((bf16[4,96,384]{2,1,0:T(8,128)(2,1)S(1)}, bf16[4,96,384]{2,1,0:T(8,128)(2,1)S(1)}, u32[]{:S(2)}, u32[]{:S(2)}) %collective-permute-start.16) | collective-permute-done | bytes 294944 | tf_op jit(solution)/shard_map/ppermute | solution.py:21
  79.8 6.2 %collective-permute-done.19 = bf16[2,4,96,384]{3,2,1,0:T(8,128)(2,1)S(1)} collective-permute-done((bf16[2,4,96,384]{3,2,1,0:T(8,128)(2,1)S(1)}, bf16[2,4,96,384]{3,2,1,0:T(8,128)(2,1)S(1)}, u32[]{:S(2)}, u32[]{:S(2)}) %collective-permute-start.19) | collective-permute-done | bytes 589856 | tf_op jit(solution)/shard_map/ppermute | solution.py:21
  92.3 6.3 %collective-permute-done.12 = bf16[2,4,24,1536]{3,2,1,0:T(8,128)(2,1)S(1)} collective-permute-done((bf16[2,4,24,1536]{3,2,1,0:T(8,128)(2,1)S(1)}, bf16[2,4,24,1536]{3,2,1,0:T(8,128)(2,1)S(1)}, u32[]{:S(2)}, u32[]{:S(2)}) %collective-permute-start.12) | collective-permute-done | bytes 589856 | tf_op jit(solution)/shard_map/ppermute | solution.py:21
  98.7 3.9 collective-permute-done.10
  103.9 5.0 collective-permute-done.3
  124.8 5.6 %convolution_convert_fusion = bf16[2304,8,128]{2,0,1:T(8,128)(2,1)S(1)} fusion(bf16[8,128,768]{2,1,0:T(8,128)(2,1)S(1)} %bitcast.636, bf16[768,3200]{1,0:T(8,128)(2,1)} %bitcast.574), kind=kOutput, calls=%fused_computation.17 | convolution fusion | flops 3626237952 | bytes 9830400 | tf_op jit(solution)/shard_map/gsd,de->gse/dot_general | solution.py:16
  137.9 3.5 fusion.118
  142.0 8.9 %multiply_convert_fusion = (bf16[8,128,3072]{2,1,0:T(8,128)(2,1)S(1)}, f32[8,128,3072]{2,1,0:T(8,128)}) fusion(bf16[768,3072,1]{1,0,2:T(8,128)(2,1)S(1)} %bitcast.609, f32[8,128,768]{2,1,0:T(8,128)S(1)} %get-tuple-element.239, f32[768]{0:T(1024)S(1)} %get-tuple-element.102, f32[768]{0:T(1024)S(1)} %get-tuple-element.103, f32[8,128]{1,0:T(8,128)S(1)} %add_rsqrt_fusion.1, ...), kind=kOutput, calls=%fused_computation.7 | convolution fusion | flops 4851499008 | bytes 26753024 | tf_op jit(solution)/shard_map/gsd,df->gsf/dot_general | solution.py:16
  151.0 5.4 %fusion.119 = (f32[8,128]{1,0:T(8,128)S(1)}, f32[8,128,768]{2,1,0:T(8,128)S(1)}) fusion(bf16[8,128,3072]{2,1,0:T(8,128)(2,1)S(1)} %get-tuple-element.240, bf16[3072,768,1]{1,0,2:T(8,128)(2,1)S(1)} %bitcast.603, f32[768]{0:T(1024)S(1)} %get-tuple-element.102, f32[768]{0:T(1024)S(1)} %get-tuple-element.103, f32[8,128]{1,0:T(8,128)S(1)} %add_rsqrt_fusion.1, ...), kind=kOutput, calls=%fused_computation.413 | convolution fusion | flops 4836555776 | bytes 17319936 | tf_op jit(solution)/shard_map/gsf,fd->gsd/dot_general | solution.py:16
  240.7 10.1 %bitcast_convert_fusion = bf16[3072,768]{1,0:T(8,128)(2,1)} fusion(bf16[8,128,3072]{2,1,0:T(8,128)(2,1)} %copy-done.72, f32[8,128,768]{2,1,0:T(8,128)S(1)} %subtract_multiply_fusion.1), kind=kOutput, calls=%fused_computation.9 | convolution fusion | flops 4834983936 | bytes 14155776 | tf_op jit(solution)/shard_map/gsf,gsd->fd/dot_general | solution.py:16
  250.8 11.6 %fusion.5 = bf16[8,128,3072]{2,1,0:T(8,128)(2,1)S(1)} fusion(f32[8,128,3072]{2,1,0:T(8,128)} %get-tuple-element.241, bf16[3072,768,1]{1,0,2:T(8,128)(2,1)S(1)} %bitcast.606, f32[8,128,768]{2,1,0:T(8,128)S(1)} %subtract_multiply_fusion.1), kind=kOutput, calls=%fused_computation.6 | convolution fusion | flops 4864081920 | bytes 26738688 | tf_op jit(solution)/shard_map/gsd,fd->gsf/dot_general | solution.py:16
  262.5 6.1 %multiply_reduce_fusion.2 = (bf16[768]{0:T(1024)(128)(2,1)S(1)}, f32[8,128]{1,0:T(8,128)S(1)}, f32[8,128]{1,0:T(8,128)S(1)}, bf16[768]{0:T(1024)(128)(2,1)S(1)}, f32[8,128,768]{2,1,0:T(8,128)S(1)}) fusion(f32[8,128,768]{2,1,0:T(8,128)S(1)} %copy-done.2, f32[8,128]{1,0:T(8,128)S(1)} %copy-done.67, f32[8,128]{1,0:T(8,128)S(1)} %copy-done.61, ...), kind=kOutput, calls=%fused_computation.35 | convolution fusion | flops 4839698432 | bytes 20469760 | tf_op jit(solution)/shard_map/gsf,df->gsd/dot_general | solution.py:16
  268.6 8.1 %bitcast_convert_fusion.1 = bf16[768,3072]{1,0:T(8,128)(2,1)} fusion(bf16[8,128,3072]{2,1,0:T(8,128)(2,1)S(1)} %fusion.5, f32[8,128,768]{2,1,0:T(8,128)S(1)} %copy-done.2, f32[768]{0:T(1024)S(1)} %copy-done.71, f32[768]{0:T(1024)S(1)} %copy-done.65, f32[8,128]{1,0:T(8,128)S(1)} %copy-done.67, f32[8,128]{1,0:T(8,128)S(1)} %copy-done.61), kind=kOutput, calls=%fused_computation.10 | convolution fusion | flops 4838129664 | bytes 14170112 | tf_op jit(solution)/shard_map/gsd,gsf->df/dot_general | solution.py:16
  283.0 6.4 %convolution_convert_fusion.1 = bf16[8,12,64,128]{3,2,1,0:T(8,128)(2,1)} fusion(bf16[8,128,12,64]{1,3,2,0:T(8,128)(2,1)S(1)} %bitcast.583, f32[8,12,128,128]{2,3,1,0:T(8,128)} %copy-done, f32[8,12,128]{2,1,0:T(8,128)S(1)} %copy-done.29, pred[8,128]{1,0:T(8,128)(4,1)S(1)} %copy-done.69), kind=kOutput, calls=%fused_computation.76 | convolution fusion | flops 208404480 | bytes 9487360 | tf_op jit(solution)/shard_map/ghqk,gqhe->gkhe/dot_general | solution.py:16
  289.4 6.1 %multiply_reduce_fusion = (f32[8,12,128]{2,1,0:T(8,128)S(1)}, f32[8,12,128,128]{2,3,1,0:T(8,128)S(1)}) fusion(f32[8,12,128,128]{2,3,1,0:T(8,128)} %copy-done, f32[8,12,128]{2,1,0:T(8,128)S(1)} %copy-done.29, pred[8,128]{1,0:T(8,128)(4,1)S(1)} %copy-done.69, bf16[8,128,12,64]{1,3,2,0:T(8,128)(2,1)S(1)} %bitcast.584, bf16[8,128,3,12,64]{1,4,3,2,0:T(8,128)(2,1)} %bitcast.615), kind=kOutput, calls=%fused_computation.13 | convolution fusion | flops 209178624 | bytes 15827968 | tf_op jit(solution)/shard_map/gqhe,gkhe->ghqk/dot_general | solution.py:16
  324.1 6.9 %bitcast_convert_fusion.2 = bf16[2304,768]{0,1:T(8,128)(2,1)S(1)} fusion(bf16[8,128,768]{2,1,0:T(8,128)(2,1)} %bitcast.635, bf16[8,128,768]{2,1,0:T(8,128)(2,1)} %copy.200, bf16[8,128,768]{2,1,0:T(8,128)(2,1)} %copy.199, bf16[8,128,768]{2,1,0:T(8,128)(2,1)} %copy.198), kind=kOutput, calls=%fused_computation.11 | convolution fusion | flops 3639803904 | bytes 9830400 | tf_op jit(solution)/shard_map/gsd,gse->de/dot_general | solution.py:16
  336.2 6.4 %add_convert_fusion = bf16[8,128,768]{2,1,0:T(8,128)(2,1)} fusion(f32[8,128,768]{2,1,0:T(8,128)S(1)} %copy-done.16, bf16[768,3200]{1,0:T(8,128)(2,1)S(1)} %bitcast.579, bf16[8,128,768]{2,1,0:T(8,128)(2,1)S(1)} %copy-done.18, bf16[8,128,768]{2,1,0:T(8,128)(2,1)} %copy.199, bf16[8,128,768]{2,1,0:T(8,128)(2,1)S(1)} %copy-done.19), kind=kOutput, calls=%fused_computation.36 | convolution fusion | flops 3639607296 | bytes 12976128 | tf_op jit(solution)/shard_map/gse,de->gsd/dot_general | solution.py:16
  342.6 18.2 %collective-permute-done.73 = bf16[2,32,8640]{2,1,0:T(8,128)(2,1)S(1)} collective-permute-done((bf16[2,32,8640]{2,1,0:T(8,128)(2,1)}, bf16[2,32,8640]{2,1,0:T(8,128)(2,1)S(1)}, u32[]{:S(2)}, u32[]{:S(2)}) %collective-permute-start.73) | collective-permute-done | bytes 1105952 | tf_op jit(solution)/shard_map/ppermute | solution.py:21
  375.4 7.2 %collective-permute-done.52 = bf16[96,3072]{1,0:T(8,128)(2,1)S(1)} collective-permute-done((bf16[96,3072]{1,0:T(8,128)(2,1)S(1)}, bf16[96,3072]{1,0:T(8,128)(2,1)S(1)}, u32[]{:S(2)}, u32[]{:S(2)}) %collective-permute-start.52) | collective-permute-done | bytes 589856 | tf_op jit(solution)/shard_map/ppermute | solution.py:73
  383.4 12.1 %collective-permute-done.54 = bf16[96,3072]{1,0:T(8,128)(2,1)S(1)} collective-permute-done((bf16[96,3072]{1,0:T(8,128)(2,1)S(1)}, bf16[96,3072]{1,0:T(8,128)(2,1)S(1)}, u32[]{:S(2)}, u32[]{:S(2)}) %collective-permute-start.54) | collective-permute-done | bytes 589856 | tf_op jit(solution)/shard_map/ppermute | solution.py:73
  399.5 8.5 %collective-permute-done.61 = bf16[384,768]{1,0:T(8,128)(2,1)S(1)} collective-permute-done((bf16[384,768]{1,0:T(8,128)(2,1)S(1)}, bf16[384,768]{1,0:T(8,128)(2,1)S(1)}, u32[]{:S(2)}, u32[]{:S(2)}) %collective-permute-start.61) | collective-permute-done | bytes 589856 | tf_op jit(solution)/shard_map/ppermute | solution.py:73
  408.8 12.1 %collective-permute-done.63 = bf16[384,768]{1,0:T(8,128)(2,1)S(1)} collective-permute-done((bf16[384,768]{1,0:T(8,128)(2,1)S(1)}, bf16[384,768]{1,0:T(8,128)(2,1)S(1)}, u32[]{:S(2)}, u32[]{:S(2)}) %collective-permute-start.63) | collective-permute-done | bytes 589856 | tf_op jit(solution)/shard_map/ppermute | solution.py:73
  424.4 9.4 %collective-permute-done.43 = bf16[96,3200]{1,0:T(8,128)(2,1)S(1)} collective-permute-done((bf16[96,3200]{1,0:T(8,128)(2,1)S(1)}, bf16[96,3200]{1,0:T(8,128)(2,1)S(1)}, u32[]{:S(2)}, u32[]{:S(2)}) %collective-permute-start.43) | collective-permute-done | bytes 614432 | tf_op jit(solution)/shard_map/ppermute | solution.py:73
  435.6 9.8 %collective-permute-done.45 = bf16[96,3200]{1,0:T(8,128)(2,1)S(1)} collective-permute-done((bf16[96,3200]{1,0:T(8,128)(2,1)S(1)}, bf16[96,3200]{1,0:T(8,128)(2,1)S(1)}, u32[]{:S(2)}, u32[]{:S(2)}) %collective-permute-start.45) | collective-permute-done | bytes 614432 | tf_op jit(solution)/shard_map/ppermute | solution.py:73
  452.1 5.8 %collective-permute-done.46 = bf16[2,24,3200]{2,1,0:T(8,128)(2,1)S(1)} collective-permute-done((bf16[2,24,3200]{2,1,0:T(8,128)(2,1)S(1)}, bf16[2,24,3200]{2,1,0:T(8,128)(2,1)S(1)}, u32[]{:S(2)}, u32[]{:S(2)}) %collective-permute-start.46) | collective-permute-done | bytes 307232 | tf_op jit(solution)/shard_map/ppermute | solution.py:21
  458.9 10.1 %collective-permute-done.56 = bf16[1,24,3072]{2,1,0:T(8,128)(2,1)S(1)} collective-permute-done((bf16[1,24,3072]{2,1,0:T(8,128)(2,1)S(1)}, bf16[1,24,3072]{2,1,0:T(8,128)(2,1)S(1)}, u32[]{:S(2)}, u32[]{:S(2)}) %collective-permute-start.56) | collective-permute-done | bytes 147488 | tf_op jit(solution)/shard_map/ppermute | solution.py:21
  472.3 8.0 %collective-permute-done.47 = bf16[1,24,3200]{2,1,0:T(8,128)(2,1)S(1)} collective-permute-done((bf16[1,24,3200]{2,1,0:T(8,128)(2,1)S(1)}, bf16[1,24,3200]{2,1,0:T(8,128)(2,1)S(1)}, u32[]{:S(2)}, u32[]{:S(2)}) %collective-permute-start.47) | collective-permute-done | bytes 153632 | tf_op jit(solution)/shard_map/ppermute | solution.py:21
  488.4 5.7 %collective-permute-done.58 = bf16[2,24,3072]{2,1,0:T(8,128)(2,1)S(1)} collective-permute-done((bf16[2,24,3072]{2,1,0:T(8,128)(2,1)S(1)}, bf16[2,24,3072]{2,1,0:T(8,128)(2,1)S(1)}, u32[]{:S(2)}, u32[]{:S(2)}) %collective-permute-start.58) | collective-permute-done | bytes 294944 | tf_op jit(solution)/shard_map/ppermute | solution.py:21
  494.3 6.1 %collective-permute-done.67 = bf16[2,96,768]{2,1,0:T(8,128)(2,1)S(1)} collective-permute-done((bf16[2,96,768]{2,1,0:T(8,128)(2,1)S(1)}, bf16[2,96,768]{2,1,0:T(8,128)(2,1)S(1)}, u32[]{:S(2)}, u32[]{:S(2)}) %collective-permute-start.67) | collective-permute-done | bytes 294944 | tf_op jit(solution)/shard_map/ppermute | solution.py:21
  (593 shorter events, 261.6 us)
Async XLA Ops:
  0.7 25.4 %collective-permute-start.14 = (bf16[1,96,768]{2,1,0:T(8,128)(2,1)}, bf16[1,96,768]{2,1,0:T(8,128)(2,1)S(1)}, u32[]{:S(2)}, u32[]{:S(2)}) collective-permute-start(bf16[1,96,768]{2,1,0:T(8,128)(2,1)} %bitcast.647), channel_id=1, source_target_pairs={{0,4},{2,6},{4,0},{6,2},{1,5},{3,7},{5,1},{7,3},{8,12},{10,14},{12... | collective-permute-start | bytes 442376 | tf_op jit(solution)/shard_map/ppermute | solution.py:21
  4.8 23.2 %collective-permute-start.7 = (bf16[1,24,3072]{2,1,0:T(8,128)(2,1)}, bf16[1,24,3072]{2,1,0:T(8,128)(2,1)S(1)}, u32[]{:S(2)}, u32[]{:S(2)}) collective-permute-start(bf16[1,24,3072]{2,1,0:T(8,128)(2,1)} %bitcast.648), channel_id=1, source_target_pairs={{0,4},{2,6},{4,0},{6,2},{1,5},{3,7},{5,1},{7,3},{8,12},{10,14},{12... | collective-permute-start | bytes 442376 | tf_op jit(solution)/shard_map/ppermute | solution.py:21
  9.6 18.8 %collective-permute-start = (bf16[1,24,3200]{2,1,0:T(8,128)(2,1)S(1)}, bf16[1,24,3200]{2,1,0:T(8,128)(2,1)S(1)}, u32[]{:S(2)}, u32[]{:S(2)}) collective-permute-start(bf16[1,24,3200]{2,1,0:T(8,128)(2,1)S(1)} %fusion.56), channel_id=1, source_target_pairs={{0,4},{2,6},{4,0},{6,2},{1,5},{3,7},{5,1},{7,3},{8,12},{10,14},{12... | collective-permute-start | bytes 460808 | tf_op jit(solution)/shard_map/ppermute | solution.py:21
  25.9 30.5 %collective-permute-start.27 = (bf16[1,96,2304]{2,1,0:T(8,128)(2,1)S(1)}, bf16[1,96,2304]{2,1,0:T(8,128)(2,1)S(1)}, u32[]{:S(2)}, u32[]{:S(2)}) collective-permute-start(bf16[1,96,2304]{2,1,0:T(8,128)(2,1)S(1)} %bitcast.631), channel_id=1, source_target_pairs={{0,4},{2,6},{4,0},{6,2},{1,5},{3,7},{5,1},{7,3},{8,12},{10,14},{12... | collective-permute-start | bytes 1327112 | tf_op jit(solution)/shard_map/ppermute | solution.py:21
  26.1 28.4 %collective-permute-start.15 = (bf16[2,96,768]{2,1,0:T(8,128)(2,1)S(1)}, bf16[2,96,768]{2,1,0:T(8,128)(2,1)S(1)}, u32[]{:S(2)}, u32[]{:S(2)}) collective-permute-start(bf16[2,96,768]{2,1,0:T(8,128)(2,1)S(1)} %maximum_bitcast_fusion.5), channel_id=1, source_target_pairs={{0,2},{2,0},{4,6},{6,4},{1,3},{3,1},{5,7},{7,5},{8,10},{10,8},{12,... | collective-permute-start | bytes 884744 | tf_op jit(solution)/shard_map/ppermute | solution.py:21
  28.1 22.8 %collective-permute-start.8 = (bf16[2,24,3072]{2,1,0:T(8,128)(2,1)S(1)}, bf16[2,24,3072]{2,1,0:T(8,128)(2,1)S(1)}, u32[]{:S(2)}, u32[]{:S(2)}) collective-permute-start(bf16[2,24,3072]{2,1,0:T(8,128)(2,1)S(1)} %maximum_bitcast_fusion.4), channel_id=1, source_target_pairs={{0,2},{2,0},{4,6},{6,4},{1,3},{3,1},{5,7},{7,5},{8,10},{10,8},{12,... | collective-permute-start | bytes 884744 | tf_op jit(solution)/shard_map/ppermute | solution.py:21
  28.5 26.8 %collective-permute-start.1 = (bf16[2,24,3200]{2,1,0:T(8,128)(2,1)S(1)}, bf16[2,24,3200]{2,1,0:T(8,128)(2,1)S(1)}, u32[]{:S(2)}, u32[]{:S(2)}) collective-permute-start(bf16[2,24,3200]{2,1,0:T(8,128)(2,1)S(1)} %maximum_bitcast_fusion.2), channel_id=1, source_target_pairs={{0,2},{2,0},{4,6},{6,4},{1,3},{3,1},{5,7},{7,5},{8,10},{10,8},{12,... | collective-permute-start | bytes 921608 | tf_op jit(solution)/shard_map/ppermute | solution.py:21
  69.3 33.3 %collective-permute-start.28 = (bf16[2,96,2304]{2,1,0:T(8,128)(2,1)S(1)}, bf16[2,96,2304]{2,1,0:T(8,128)(2,1)S(1)}, u32[]{:S(2)}, u32[]{:S(2)}) collective-permute-start(bf16[2,96,2304]{2,1,0:T(8,128)(2,1)S(1)} %maximum_bitcast_fusion.1), channel_id=1, source_target_pairs={{0,2},{2,0},{4,6},{6,4},{1,3},{3,1},{5,7},{7,5},{8,10},{10,8},{12,... | collective-permute-start | bytes 2654216 | tf_op jit(solution)/shard_map/ppermute | solution.py:21
  70.5 19.8 %collective-permute-start.17 = (bf16[2,4,96,384]{3,2,1,0:T(8,128)(2,1)S(1)}, bf16[2,4,96,384]{3,2,1,0:T(8,128)(2,1)S(1)}, u32[]{:S(2)}, u32[]{:S(2)}) collective-permute-start(bf16[2,4,96,384]{3,2,1,0:T(8,128)(2,1)S(1)} %pad_maximum_fusion.24), channel_id=1, source_target_pairs={{0,16},{16,0},{1,17},{17,1},{2,18},{18,2},{3,19},{19,3},{4,20},{20... | collective-permute-start | bytes 1769480 | tf_op jit(solution)/shard_map/ppermute | solution.py:21
  72.6 26.0 %collective-permute-start.12 = (bf16[2,4,24,1536]{3,2,1,0:T(8,128)(2,1)S(1)}, bf16[2,4,24,1536]{3,2,1,0:T(8,128)(2,1)S(1)}, u32[]{:S(2)}, u32[]{:S(2)}) collective-permute-start(bf16[2,4,24,1536]{3,2,1,0:T(8,128)(2,1)S(1)} %pad_maximum_fusion.22), channel_id=1, source_target_pairs={{0,8},{8,0},{1,9},{9,1},{2,10},{10,2},{3,11},{11,3},{4,12},{12,4},... | collective-permute-start | bytes 1769480 | tf_op jit(solution)/shard_map/ppermute | solution.py:21
  77.6 24.9 %collective-permute-start.10 = (bf16[2,4,24,1536]{3,2,1,0:T(8,128)(2,1)S(1)}, bf16[2,4,24,1536]{3,2,1,0:T(8,128)(2,1)S(1)}, u32[]{:S(2)}, u32[]{:S(2)}) collective-permute-start(bf16[2,4,24,1536]{3,2,1,0:T(8,128)(2,1)S(1)} %pad_maximum_fusion.21), channel_id=1, source_target_pairs={{0,16},{16,0},{1,17},{17,1},{2,18},{18,2},{3,19},{19,3},{4,20},{20... | collective-permute-start | bytes 1769480 | tf_op jit(solution)/shard_map/ppermute | solution.py:21
  86.0 22.9 %collective-permute-start.3 = (bf16[2,4,24,1536]{3,2,1,0:T(8,128)(2,1)S(1)}, bf16[2,4,24,1536]{3,2,1,0:T(8,128)(2,1)S(1)}, u32[]{:S(2)}, u32[]{:S(2)}) collective-permute-start(bf16[2,4,24,1536]{3,2,1,0:T(8,128)(2,1)S(1)} %pad_maximum_fusion.19), channel_id=1, source_target_pairs={{0,16},{16,0},{1,17},{17,1},{2,18},{18,2},{3,19},{19,3},{4,20},{20... | collective-permute-start | bytes 1769480 | tf_op jit(solution)/shard_map/ppermute | solution.py:21
  90.2 18.7 %collective-permute-start.5 = (bf16[2,4,24,1664]{3,2,1,0:T(8,128)(2,1)S(1)}, bf16[2,4,24,1664]{3,2,1,0:T(8,128)(2,1)S(1)}, u32[]{:S(2)}, u32[]{:S(2)}) collective-permute-start(bf16[2,4,24,1664]{3,2,1,0:T(8,128)(2,1)S(1)} %pad_maximum_fusion.16), channel_id=1, source_target_pairs={{0,8},{8,0},{1,9},{9,1},{2,10},{10,2},{3,11},{11,3},{4,12},{12,4},... | collective-permute-start | bytes 1916936 | tf_op jit(solution)/shard_map/ppermute | solution.py:21
  310.1 21.6 %collective-permute-start.72 = (bf16[1,32,8640]{2,1,0:T(8,128)(2,1)S(1)}, bf16[1,32,8640]{2,1,0:T(8,128)(2,1)}, u32[]{:S(2)}, u32[]{:S(2)}) collective-permute-start(bf16[1,32,8640]{2,1,0:T(8,128)(2,1)S(1)} %bitcast.630), channel_id=1, source_target_pairs={{0,4},{2,6},{4,0},{6,2},{1,5},{3,7},{5,1},{7,3},{8,12},{10,14},{12... | collective-permute-start | bytes 1658888 | tf_op jit(solution)/shard_map/ppermute | solution.py:21
  319.3 42.1 %collective-permute-start.51 = (bf16[4,96,3072]{2,1,0:T(8,128)(2,1)}, bf16[4,96,3072]{2,1,0:T(8,128)(2,1)}, u32[]{:S(2)}, u32[]{:S(2)}) collective-permute-start(bf16[4,96,3072]{2,1,0:T(8,128)(2,1)} %dynamic-slice_bitcast_fusion.2), channel_id=1, source_target_pairs={{0,1},{1,0},{2,3},{3,2},{4,5},{5,4},{6,7},{7,6},{8,9},{9,8},{10,11... | collective-permute-start | bytes 7077896 | tf_op jit(solution)/shard_map/ppermute | solution.py:21
  319.3 50.5 %collective-permute-start.60 = (bf16[4,384,768]{2,1,0:T(8,128)(2,1)}, bf16[4,384,768]{2,1,0:T(8,128)(2,1)}, u32[]{:S(2)}, u32[]{:S(2)}) collective-permute-start(bf16[4,384,768]{2,1,0:T(8,128)(2,1)} %dynamic-slice_bitcast_fusion.1), channel_id=1, source_target_pairs={{0,1},{1,0},{2,3},{3,2},{4,5},{5,4},{6,7},{7,6},{8,9},{9,8},{10,11... | collective-permute-start | bytes 7077896 | tf_op jit(solution)/shard_map/ppermute | solution.py:21
  333.9 26.9 %collective-permute-start.73 = (bf16[2,32,8640]{2,1,0:T(8,128)(2,1)}, bf16[2,32,8640]{2,1,0:T(8,128)(2,1)S(1)}, u32[]{:S(2)}, u32[]{:S(2)}) collective-permute-start(bf16[2,32,8640]{2,1,0:T(8,128)(2,1)} %maximum_bitcast_fusion), channel_id=1, source_target_pairs={{0,2},{2,0},{4,6},{6,4},{1,3},{3,1},{5,7},{7,5},{8,10},{10,8},{12,... | collective-permute-start | bytes 3317768 | tf_op jit(solution)/shard_map/ppermute | solution.py:21
  336.1 37.3 %collective-permute-start.42 = (bf16[4,96,3200]{2,1,0:T(8,128)(2,1)S(1)}, bf16[4,96,3200]{2,1,0:T(8,128)(2,1)S(1)}, u32[]{:S(2)}, u32[]{:S(2)}) collective-permute-start(bf16[4,96,3200]{2,1,0:T(8,128)(2,1)S(1)} %dynamic-slice_bitcast_fusion), channel_id=1, source_target_pairs={{0,1},{1,0},{2,3},{3,2},{4,5},{5,4},{6,7},{7,6},{8,9},{9,8},{10,11... | collective-permute-start | bytes 7372808 | tf_op jit(solution)/shard_map/ppermute | solution.py:21
  367.4 28.1 %collective-permute-start.54 = (bf16[96,3072]{1,0:T(8,128)(2,1)S(1)}, bf16[96,3072]{1,0:T(8,128)(2,1)S(1)}, u32[]{:S(2)}, u32[]{:S(2)}) collective-permute-start(bf16[96,3072]{1,0:T(8,128)(2,1)S(1)} %get-tuple-element.133), channel_id=1, source_target_pairs={{0,24},{8,16},{16,8},{24,0},{1,25},{9,17},{17,9},{25,1},{2,26},{10... | collective-permute-start | bytes 1769480 | tf_op jit(solution)/shard_map/ppermute | solution.py:73
  368.6 28.1 %collective-permute-start.53 = (bf16[96,3072]{1,0:T(8,128)(2,1)S(1)}, bf16[96,3072]{1,0:T(8,128)(2,1)S(1)}, u32[]{:S(2)}, u32[]{:S(2)}) collective-permute-start(bf16[96,3072]{1,0:T(8,128)(2,1)S(1)} %get-tuple-element.134), channel_id=1, source_target_pairs={{0,16},{8,24},{16,0},{24,8},{1,17},{9,25},{17,1},{25,9},{2,18},{10... | collective-permute-start | bytes 1769480 | tf_op jit(solution)/shard_map/ppermute | solution.py:73
  372.3 35.6 %collective-permute-start.61 = (bf16[384,768]{1,0:T(8,128)(2,1)S(1)}, bf16[384,768]{1,0:T(8,128)(2,1)S(1)}, u32[]{:S(2)}, u32[]{:S(2)}) collective-permute-start(bf16[384,768]{1,0:T(8,128)(2,1)S(1)} %get-tuple-element.129), channel_id=1, source_target_pairs={{0,8},{8,0},{16,24},{24,16},{1,9},{9,1},{17,25},{25,17},{2,10},{10... | collective-permute-start | bytes 1769480 | tf_op jit(solution)/shard_map/ppermute | solution.py:73
  373.4 47.5 %collective-permute-start.63 = (bf16[384,768]{1,0:T(8,128)(2,1)S(1)}, bf16[384,768]{1,0:T(8,128)(2,1)S(1)}, u32[]{:S(2)}, u32[]{:S(2)}) collective-permute-start(bf16[384,768]{1,0:T(8,128)(2,1)S(1)} %get-tuple-element.130), channel_id=1, source_target_pairs={{0,24},{8,16},{16,8},{24,0},{1,25},{9,17},{17,9},{25,1},{2,26},{10... | collective-permute-start | bytes 1769480 | tf_op jit(solution)/shard_map/ppermute | solution.py:73
  382.7 39.4 %collective-permute-start.62 = (bf16[384,768]{1,0:T(8,128)(2,1)S(1)}, bf16[384,768]{1,0:T(8,128)(2,1)S(1)}, u32[]{:S(2)}, u32[]{:S(2)}) collective-permute-start(bf16[384,768]{1,0:T(8,128)(2,1)S(1)} %get-tuple-element.131), channel_id=1, source_target_pairs={{0,16},{8,24},{16,0},{24,8},{1,17},{9,25},{17,1},{25,9},{2,18},{10... | collective-permute-start | bytes 1769480 | tf_op jit(solution)/shard_map/ppermute | solution.py:73
  395.6 38.3 %collective-permute-start.43 = (bf16[96,3200]{1,0:T(8,128)(2,1)S(1)}, bf16[96,3200]{1,0:T(8,128)(2,1)S(1)}, u32[]{:S(2)}, u32[]{:S(2)}) collective-permute-start(bf16[96,3200]{1,0:T(8,128)(2,1)S(1)} %get-tuple-element.126), channel_id=1, source_target_pairs={{0,8},{8,0},{16,24},{24,16},{1,9},{9,1},{17,25},{25,17},{2,10},{10... | collective-permute-start | bytes 1843208 | tf_op jit(solution)/shard_map/ppermute | solution.py:73
  396.8 48.6 %collective-permute-start.45 = (bf16[96,3200]{1,0:T(8,128)(2,1)S(1)}, bf16[96,3200]{1,0:T(8,128)(2,1)S(1)}, u32[]{:S(2)}, u32[]{:S(2)}) collective-permute-start(bf16[96,3200]{1,0:T(8,128)(2,1)S(1)} %get-tuple-element.127), channel_id=1, source_target_pairs={{0,24},{8,16},{16,8},{24,0},{1,25},{9,17},{17,9},{25,1},{2,26},{10... | collective-permute-start | bytes 1843208 | tf_op jit(solution)/shard_map/ppermute | solution.py:73
  408.0 38.6 %collective-permute-start.44 = (bf16[96,3200]{1,0:T(8,128)(2,1)S(1)}, bf16[96,3200]{1,0:T(8,128)(2,1)S(1)}, u32[]{:S(2)}, u32[]{:S(2)}) collective-permute-start(bf16[96,3200]{1,0:T(8,128)(2,1)S(1)} %get-tuple-element.128), channel_id=1, source_target_pairs={{0,16},{8,24},{16,0},{24,8},{1,17},{9,25},{17,1},{25,9},{2,18},{10... | collective-permute-start | bytes 1843208 | tf_op jit(solution)/shard_map/ppermute | solution.py:73
  420.9 79.7 %collective-permute-start.74 = (bf16[4,32,8640]{2,1,0:T(8,128)(2,1)S(1)}, bf16[4,32,8640]{2,1,0:T(8,128)(2,1)S(1)}, u32[]{:S(2)}, u32[]{:S(2)}) collective-permute-start(bf16[4,32,8640]{2,1,0:T(8,128)(2,1)S(1)} %bitcast.571), channel_id=1, source_target_pairs={{0,1},{1,0},{2,3},{3,2},{4,5},{5,4},{6,7},{7,6},{8,9},{9,8},{10,11... | collective-permute-start | bytes 6635528 | tf_op jit(solution)/shard_map/ppermute | solution.py:21
  422.0 26.8 %collective-permute-start.55 = (bf16[2,24,3072]{2,1,0:T(8,128)(2,1)S(1)}, bf16[2,24,3072]{2,1,0:T(8,128)(2,1)S(1)}, u32[]{:S(2)}, u32[]{:S(2)}) collective-permute-start(bf16[2,24,3072]{2,1,0:T(8,128)(2,1)S(1)} %dynamic-slice_bitcast_fusion.14), channel_id=1, source_target_pairs={{0,2},{2,0},{4,6},{6,4},{1,3},{3,1},{5,7},{7,5},{8,10},{10,8},{12,... | collective-permute-start | bytes 884744 | tf_op jit(solution)/shard_map/ppermute | solution.py:21
  448.9 20.1 %collective-permute-start.56 = (bf16[1,24,3072]{2,1,0:T(8,128)(2,1)S(1)}, bf16[1,24,3072]{2,1,0:T(8,128)(2,1)S(1)}, u32[]{:S(2)}, u32[]{:S(2)}) collective-permute-start(bf16[1,24,3072]{2,1,0:T(8,128)(2,1)S(1)} %constant_dynamic-slice_fusion.3), channel_id=1, source_target_pairs={{0,4},{2,6},{4,0},{6,2},{1,5},{3,7},{5,1},{7,3},{8,12},{10,14},{12... | collective-permute-start | bytes 442376 | tf_op jit(solution)/shard_map/ppermute | solution.py:21
  449.1 23.0 %collective-permute-start.65 = (bf16[1,96,768]{2,1,0:T(8,128)(2,1)S(1)}, bf16[1,96,768]{2,1,0:T(8,128)(2,1)S(1)}, u32[]{:S(2)}, u32[]{:S(2)}) collective-permute-start(bf16[1,96,768]{2,1,0:T(8,128)(2,1)S(1)} %constant_dynamic-slice_fusion.2), channel_id=1, source_target_pairs={{0,4},{2,6},{4,0},{6,2},{1,5},{3,7},{5,1},{7,3},{8,12},{10,14},{12... | collective-permute-start | bytes 442376 | tf_op jit(solution)/shard_map/ppermute | solution.py:21
  458.0 22.3 %collective-permute-start.47 = (bf16[1,24,3200]{2,1,0:T(8,128)(2,1)S(1)}, bf16[1,24,3200]{2,1,0:T(8,128)(2,1)S(1)}, u32[]{:S(2)}, u32[]{:S(2)}) collective-permute-start(bf16[1,24,3200]{2,1,0:T(8,128)(2,1)S(1)} %constant_dynamic-slice_fusion.4), channel_id=1, source_target_pairs={{0,4},{2,6},{4,0},{6,2},{1,5},{3,7},{5,1},{7,3},{8,12},{10,14},{12... | collective-permute-start | bytes 460808 | tf_op jit(solution)/shard_map/ppermute | solution.py:21
  487.8 22.2 %collective-permute-start.49 = (bf16[2,24,3200]{2,1,0:T(8,128)(2,1)S(1)}, bf16[2,24,3200]{2,1,0:T(8,128)(2,1)S(1)}, u32[]{:S(2)}, u32[]{:S(2)}) collective-permute-start(bf16[2,24,3200]{2,1,0:T(8,128)(2,1)S(1)} %maximum_bitcast_fusion.3), channel_id=1, source_target_pairs={{0,2},{2,0},{4,6},{6,4},{1,3},{3,1},{5,7},{7,5},{8,10},{10,8},{12,... | collective-permute-start | bytes 921608 | tf_op jit(solution)/shard_map/ppermute | solution.py:21
  (136 other events, 1367.3 us)

commit v2 on v1

v2 whole, which is shorter than its diff:
```python
import functools
import math

import jax
import jax.numpy as jnp
from jax import lax
from jax.experimental import pallas as pl
from jax.experimental.pallas import tpu as pltpu
from jax.sharding import Mesh
from jax.sharding import PartitionSpec as P

HEAD = 64
norm_eps = 1e-05
masked_score = -1000000000.0
bf16, f32 = jnp.bfloat16, jnp.float32
VMEM_CAP = 56 << 20


def tie(values, *after):
    return lax.optimization_barrier((values, after))[0]


def swap(value, axis, bit, then=()):
    size = lax.axis_size(axis)
    got = lax.ppermute(value, axis, [(i, i ^ bit) for i in range(size)])
    return tie(got, then) if then else got


def bit_of(axis, bit):
    return (lax.axis_index(axis) // bit) % 2


def join(mine, other, side, axis):
    first = side == 0
    return jnp.stack([jnp.where(first, mine, other), jnp.where(first, other, mine)], axis=axis)


def side_by_side(mine, other, side):
    both = jnp.concatenate([other, other], axis=-1)
    return lax.dynamic_update_slice_in_dim(both, mine, side * mine.shape[-1], axis=-1)


def part(value, side, axis):
    return lax.dynamic_index_in_dim(value, side, axis, keepdims=False)


def bits_down(size):
    return [1 << k for k in reversed(range(size.bit_length() - 1))]


class RowGather:
    def __init__(self, shard):
        rows, cols = shard.shape
        half = cols // 2
        c = lax.axis_index("c")
        keep = lax.dynamic_slice_in_dim(shard, c * half, half, 1)
        send = lax.dynamic_slice_in_dim(shard, (1 - c) * half, half, 1)
        self.state = join(keep, swap(send, "c", 1), c, 0).reshape(1, 2 * rows, half)

    def after(self, *others):
        self.state = tie(self.state, others)

    def far_z(self, *then):
        bits = bits_down(lax.axis_size("z"))
        for bit in bits[:-1]:
            self._along_z(bit, then)

    def near_z(self, *then):
        self._along_z(1, then)

    def _along_z(self, bit, then=()):
        got = self.state
        got = join(got, swap(got, "z", bit, then), bit_of("z", bit), 1)
        self.state = got.reshape((-1,) + got.shape[2:])

    def plane_first(self, *then):
        zhalf = self.state.shape[0] // 2
        one, two = self.state[:zhalf], self.state[zhalf:]
        got_one, got_two = swap(one, "x", 1, then), swap(two, "y", 1, then)
        self.state = join(one, got_one, lax.axis_index("x"), 0), join(two, got_two, lax.axis_index("y"), 0)

    def plane_second(self, *then):
        one, two = self.state
        got_one, got_two = swap(one, "y", 1, then), swap(two, "x", 1, then)
        one = join(one, got_one, lax.axis_index("y"), 0)
        two = join(two, got_two, lax.axis_index("x"), 1)
        both = jnp.concatenate([one, two], axis=2)
        self.state = both.reshape(-1, both.shape[-1])

    def sibling(self, *then):
        self.state = self.state, swap(self.state, "c", 1, then)


class RepGather:
    def __init__(self, message):
        self.state = message[None]

    far_z = RowGather.far_z
    near_z = RowGather.near_z
    after = RowGather.after

    def _along_z(self, bit, then=()):
        got = self.state
        got = join(got, swap(got, "z", bit, then), bit_of("z", bit), 1)
        self.state = got.reshape((-1,) + got.shape[2:])

    def sibling(self, *then):
        self.state = join(self.state, swap(self.state, "c", 1, then), lax.axis_index("c"), 1)


def swap_f(value, dist, then=()):
    count = lax.axis_size("y") * lax.axis_size("x")
    got = lax.ppermute(value, ("y", "x"), [(i, i ^ dist) for i in range(count)])
    return tie(got, then) if then else got


def in_order(parts):
    y, x = lax.axis_index("y"), lax.axis_index("x")
    row0 = [jnp.where(x == 0, parts[0], parts[1]), jnp.where(x == 0, parts[1], parts[0])]
    row1 = [jnp.where(x == 0, parts[2], parts[3]), jnp.where(x == 0, parts[3], parts[2])]
    top, low = jnp.stack(row0), jnp.stack(row1)
    return jnp.concatenate([jnp.where(y == 0, top, low), jnp.where(y == 0, low, top)])


def gather_f(value, *then):
    return in_order([value] + [swap_f(value, d, then) for d in (1, 2, 3)])


def sum_f(value):
    got = [value] + [swap_f(value, d) for d in (1, 2, 3)]
    return (got[0] + got[1]) + (got[2] + got[3])


def add(*terms):
    total = terms[0].astype(f32)
    for term in terms[1:]:
        total = total + term.astype(f32)
    return total.astype(bf16)


class RowReduce:
    def __init__(self):
        self.parts = []

    def after(self, *others):
        self.state = tie(self.state, others)

    def core(self, pair, *then):
        self.parts.append((pair[0], swap(pair[1], "c", 1, then)))

    def after_core(self, *others):
        self.parts = tie(self.parts, others)

    def chip_direct(self):
        count = lax.axis_size("y") * lax.axis_size("x")
        mine, got = (p.reshape((count, -1) + p.shape[-1:]) for p in self.parts[0])
        self.state = [add(mine[d], got[d]) for d in range(count)]

    def plane_direct(self, *then):
        got = [swap_f(self.state[d], d, then) for d in (1, 2, 3)]
        plane = add(self.state[0], *got)
        zsize = lax.axis_size("z")
        self.state = plane.reshape(zsize, plane.shape[0] // zsize, plane.shape[1])

    def chip(self):
        count = lax.axis_size("y") * lax.axis_size("x")

        def some(blocks, right):
            out = []
            for d in blocks:
                cuts = []
                for mine, got in self.parts:
                    half = (mine.shape[-1] // 256) * 128
                    cut = slice(half, None) if right else slice(None, half)
                    mine = mine.reshape((count, -1) + mine.shape[-1:])
                    got = got.reshape(mine.shape)
                    cuts.append(add(mine[d][:, cut], got[d][:, cut]))
                out.append(jnp.concatenate(cuts, axis=-1))
            return jnp.stack(out)

        self.state = some((0, 2), False), some((1, 3), False), some((0, 1), True), some((2, 3), True)

    def plane_first(self, *then):
        keep_left, send_left, keep_right, send_right = self.state
        got_left, got_right = swap(send_left, "x", 1, then), swap(send_right, "y", 1, then)
        self.state = (
            add(keep_left[0], got_left[0]), add(keep_left[1], got_left[1]),
            add(keep_right[0], got_right[0]), add(keep_right[1], got_right[1]),
        )

    def plane_second(self, *then):
        keep_left, send_left, keep_right, send_right = self.state
        got_left, got_right = swap(send_left, "y", 1, then), swap(send_right, "x", 1, then)
        plane = jnp.concatenate([add(keep_left, got_left), add(keep_right, got_right)], axis=-1)
        zsize = lax.axis_size("z")
        self.state = plane.reshape(zsize, plane.shape[0] // zsize, plane.shape[1])

    def near_z(self, *then):
        self._along_z(1, then)

    def far_z(self, *then):
        for bit in reversed(bits_down(lax.axis_size("z"))[:-1]):
            self._along_z(bit, then)

    def _along_z(self, bit, then=()):
        side = bit_of("z", bit)
        pairs = self.state.reshape((-1, 2) + self.state.shape[1:])
        other = swap(part(pairs, 1 - side, 1), "z", bit, then)
        self.state = add(part(pairs, side, 1), other)

    def back_far(self, *then):
        self.back = RepGather(self.state[0])
        self.back.far_z(*then)
        self.state = self.back.state

    def back_near(self, *then):
        self.back.state = self.state
        self.back.near_z(*then)
        self.state = self.back.state

    def back_core(self, *then):
        mine = self.state.reshape(-1, self.state.shape[-1])
        both = join(mine, swap(mine, "c", 1, then), lax.axis_index("c"), 0)
        self.state = both.reshape(-1, both.shape[-1])


def ungroup(reduced, sizes):
    halves = [(size // 256) * 128 for size in sizes]
    left, right, arrays = 0, sum(halves), []
    for size, half in zip(sizes, halves, strict=True):
        arrays.append(jnp.concatenate([reduced[:, left : left + half], reduced[:, right : right + size - half]], axis=-1))
        left, right = left + half, right + size - half
    return arrays


def product(left_op, right_op, einsum_form):
    return jnp.einsum(einsum_form, left_op, right_op, preferred_element_type=f32)


def normalize(summed_in, gain_row, bias_row):
    row_mean = jnp.mean(summed_in, axis=-1, keepdims=True)
    centered = summed_in - row_mean
    inv_dev = lax.rsqrt(jnp.mean(centered * centered, axis=-1, keepdims=True) + norm_eps)
    unit_rows = centered * inv_dev
    return (unit_rows * gain_row + bias_row, unit_rows, inv_dev)


def norm_back(upstream, unit_rows, inv_dev, gain_row):
    scaled = upstream * gain_row
    grad_in = inv_dev * (
        scaled
        - jnp.mean(scaled, axis=-1, keepdims=True)
        - unit_rows * jnp.mean(scaled * unit_rows, axis=-1, keepdims=True)
    )
    sums = tuple(range(upstream.ndim - 1))
    return (grad_in, jnp.sum(upstream * unit_rows, axis=sums), jnp.sum(upstream, axis=sums))


def gelu_pair(inner_pre):
    cumul = 0.5 * (1.0 + lax.erf(inner_pre * 0.7071067811865476))
    return (
        inner_pre * cumul,
        cumul + inner_pre * jnp.exp(-0.5 * inner_pre * inner_pre) * 0.3989422804014327,
    )


def masked_scores(query_rows, key_rows, key_mask):
    raw_scores = product(query_rows, key_rows, "gqhe,gkhe->ghqk") * (1.0 / math.sqrt(HEAD))
    return jnp.where(key_mask[:, None, None, :], raw_scores, masked_score)


def attend(query_rows, key_rows, value_rows, key_mask):
    scores = masked_scores(query_rows, key_rows, key_mask)
    row_max = jnp.max(scores, axis=-1, keepdims=True)
    log_total = row_max + jnp.log(jnp.sum(jnp.exp(scores - row_max), axis=-1, keepdims=True))
    softmax_w = jnp.exp(scores - log_total).astype(bf16)
    mixed_heads = product(softmax_w, value_rows, "ghqk,gkhe->gqhe").astype(bf16)
    return (mixed_heads, log_total)


def attend_back(query_rows, key_rows, value_rows, key_mask, log_total, grad_mixed):
    scores = masked_scores(query_rows, key_rows, key_mask)
    softmax_w = jnp.exp(scores - log_total)
    grad_value = product(softmax_w.astype(bf16), grad_mixed, "ghqk,gqhe->gkhe")
    grad_probs = product(grad_mixed, value_rows, "gqhe,gkhe->ghqk")
    grad_scores = (
        softmax_w * (grad_probs - jnp.sum(softmax_w * grad_probs, axis=-1, keepdims=True))
    ).astype(bf16)
    inv_root = 1.0 / math.sqrt(HEAD)
    grad_query = product(grad_scores, key_rows, "ghqk,gkhe->gqhe") * inv_root
    grad_key = product(grad_scores, query_rows, "ghqk,gqhe->gkhe") * inv_root
    return (grad_query, grad_key, grad_value)


def split_heads(packed, head_count):
    stacked = packed.reshape(packed.shape[0], packed.shape[1], 3, head_count, HEAD)
    return (stacked[:, :, 0], stacked[:, :, 1], stacked[:, :, 2])


def dot(a, b):
    return lax.dot_general(a, b, (((1,), (0,)), ((), ())), preferred_element_type=f32)


def dot_nt(a, b):
    return lax.dot_general(a, b, (((1,), (1,)), ((), ())), preferred_element_type=f32)


def dot_tn(a, b):
    return lax.dot_general(a, b, (((0,), (0,)), ((), ())), preferred_element_type=f32)


def norm_back_rows(upstream, unit_rows, inv_dev, gain_row):
    scaled = upstream * gain_row
    return inv_dev * (
        scaled
        - jnp.mean(scaled, axis=-1, keepdims=True)
        - unit_rows * jnp.mean(scaled * unit_rows, axis=-1, keepdims=True)
    )


def pair_of(value, low_half):
    zero = jnp.zeros_like(value)
    return jnp.concatenate([jnp.where(low_half, value, zero), jnp.where(low_half, zero, value)], axis=0)


def pair_probs(keys, queries_two, key_ok):
    scores = jnp.where(key_ok, dot_nt(keys, queries_two), masked_score)
    e = jnp.exp(scores - jnp.max(scores, axis=0, keepdims=True))
    return e * (1.0 / jnp.sum(e, axis=0, keepdims=True))


def cost(flops, moved):
    return pl.CostEstimate(flops=flops, bytes_accessed=moved, transcendentals=0)


def attend_kernel(counts_ref, x_ref, w_ref, packed_ref, mixed_ref, *, seg):
    step = pl.program_id(0)
    rows, width = x_ref.shape
    packed_ref[...] = dot(x_ref[...], w_ref[...]).astype(bf16)
    low_half = lax.broadcasted_iota(jnp.int32, (seg, 2 * HEAD), 1) < HEAD
    key_at = lax.broadcasted_iota(jnp.int32, (seg, 2 * seg), 0)
    for s in range(rows // seg):
        key_ok = key_at < counts_ref[step * (rows // seg) + s]
        r = pl.ds(s * seg, seg)
        for p in range(width // (2 * HEAD)):
            col = p * 2 * HEAD
            q = packed_ref[r, pl.ds(col, 2 * HEAD)] * jnp.asarray(HEAD**-0.5, bf16)
            k = packed_ref[r, pl.ds(width + col, 2 * HEAD)]
            v = packed_ref[r, pl.ds(2 * width + col, 2 * HEAD)]
            probs = pair_probs(k, pair_of(q, low_half), key_ok).astype(bf16)
            both = dot_tn(probs, v)
            mixed_ref[r, pl.ds(col, 2 * HEAD)] = jnp.where(low_half, both[:seg], both[seg:]).astype(bf16)


def attend_call(counts, x, w_qkv, rows=256):
    total, width = x.shape
    return pl.pallas_call(
        functools.partial(attend_kernel, seg=total // counts.shape[0]),
        grid_spec=pltpu.PrefetchScalarGridSpec(
            num_scalar_prefetch=1,
            grid=(total // rows,),
            in_specs=[
                pl.BlockSpec((rows, width), lambda i, n: (i, 0)),
                pl.BlockSpec((width, 3 * width), lambda i, n: (0, 0)),
            ],
            out_specs=[
                pl.BlockSpec((rows, 3 * width), lambda i, n: (i, 0)),
                pl.BlockSpec((rows, width), lambda i, n: (i, 0)),
            ],
        ),
        out_shape=[
            jax.ShapeDtypeStruct((total, 3 * width), bf16),
            jax.ShapeDtypeStruct((total, width), bf16),
        ],
        compiler_params=pltpu.CompilerParams(vmem_limit_bytes=VMEM_CAP),
        cost_estimate=cost(8 * total * width * width, 16 << 20),
        name="attend",
    )(counts, x, w_qkv)


def attend_back_kernel(counts_ref, packed_ref, grad_ref, out_ref, *, seg):
    step = pl.program_id(0)
    rows, width = grad_ref.shape
    low_half = lax.broadcasted_iota(jnp.int32, (seg, 2 * HEAD), 1) < HEAD
    key_at = lax.broadcasted_iota(jnp.int32, (seg, 2 * seg), 0)
    root = jnp.asarray(HEAD**-0.5, bf16)
    for s in range(rows // seg):
        key_ok = key_at < counts_ref[step * (rows // seg) + s]
        r = pl.ds(s * seg, seg)
        for p in range(width // (2 * HEAD)):
            col = p * 2 * HEAD
            q_two = pair_of(packed_ref[r, pl.ds(col, 2 * HEAD)] * root, low_half)
            k = packed_ref[r, pl.ds(width + col, 2 * HEAD)]
            v = packed_ref[r, pl.ds(2 * width + col, 2 * HEAD)]
            g_two = pair_of(grad_ref[r, pl.ds(col, 2 * HEAD)], low_half)
            probs = pair_probs(k, q_two, key_ok)
            grad_v = dot(probs.astype(bf16), g_two)
            grad_p = dot_nt(v, g_two)
            weighted = probs * grad_p
            grad_s = (weighted - probs * jnp.sum(weighted, axis=0, keepdims=True)).astype(bf16)
            grad_k = dot(grad_s, q_two)
            both = dot_tn(grad_s, k) * (HEAD**-0.5)
            out_ref[r, pl.ds(col, 2 * HEAD)] = jnp.where(low_half, both[:seg], both[seg:]).astype(bf16)
            out_ref[r, pl.ds(width + col, 2 * HEAD)] = grad_k.astype(bf16)
            out_ref[r, pl.ds(2 * width + col, 2 * HEAD)] = grad_v.astype(bf16)


def attend_back_call(counts, packed, grad_mixed, rows=256):
    total, width = grad_mixed.shape
    return pl.pallas_call(
        functools.partial(attend_back_kernel, seg=total // counts.shape[0]),
        grid_spec=pltpu.PrefetchScalarGridSpec(
            num_scalar_prefetch=1,
            grid=(total // rows,),
            in_specs=[
                pl.BlockSpec((rows, 3 * width), lambda i, n: (i, 0)),
                pl.BlockSpec((rows, width), lambda i, n: (i, 0)),
            ],
            out_specs=pl.BlockSpec((rows, 3 * width), lambda i, n: (i, 0)),
        ),
        out_shape=jax.ShapeDtypeStruct((total, 3 * width), bf16),
        compiler_params=pltpu.CompilerParams(vmem_limit_bytes=VMEM_CAP),
        cost_estimate=cost(16 * total * width * width, 16 << 20),
        name="attend_back",
    )(counts, packed, grad_mixed)


def whole(shape):
    return pl.BlockSpec(shape, lambda *i: (0,) * len(shape))


def rows_of(rows, cols):
    return pl.BlockSpec((rows, cols), lambda i, *n: (i, 0))


def finish_kernel(counts_ref, x_ref, mixed_ref, out_ref, up_ref, down_ref, rows_ref,
                  z1_ref, z2_ref, act_ref, slope_ref, hidden_ref, cls_ref, *, tile, seg):
    step = pl.program_id(0)
    rows, width = x_ref.shape
    z1 = x_ref[...].astype(f32) + dot(mixed_ref[...], out_ref[...])
    z1_ref[...] = z1
    first, _, _ = normalize(z1, rows_ref[0:1], rows_ref[2:3])
    low = first.astype(bf16)
    total = first
    for t in range(up_ref.shape[1] // tile):
        cols = pl.ds(t * tile, tile)
        act, slope = gelu_pair(dot(low, up_ref[:, cols]))
        act = act.astype(bf16)
        act_ref[:, cols] = act
        slope_ref[:, cols] = slope.astype(bf16)
        total = total + dot(act, down_ref[cols, :])
    z2_ref[...] = total
    normed = normalize(total, rows_ref[1:2], rows_ref[3:4])[0]
    at = lax.broadcasted_iota(jnp.int32, (seg, width), 0)
    for s in range(rows // seg):
        here = step * (rows // seg) + s
        block = normed[s * seg : (s + 1) * seg]
        cls_ref[pl.ds(here, 1), :] = block[0:1]
        hidden_ref[s * seg : (s + 1) * seg] = jnp.where(at < counts_ref[here], block, 0.0).astype(bf16)


def pack_kernel(wide_ref, *refs):
    small, o_ref = refs[:-1], refs[-1]
    cols = wide_ref.shape[1]
    o_ref[:, :cols] = wide_ref[...]
    turned, at = 0.0, 0
    for ref in small:
        count = ref.shape[0]
        shape = (count, 128)
        one = lax.broadcasted_iota(jnp.int32, shape, 1) == lax.broadcasted_iota(jnp.int32, shape, 0) + at
        turned = turned + dot_tn(ref[...], one.astype(bf16))
        at += count
    o_ref[:, cols:] = turned.astype(bf16)


def pack_call(wide, small):
    return pl.pallas_call(
        pack_kernel,
        out_shape=jax.ShapeDtypeStruct((wide.shape[0], wide.shape[1] + 128), bf16),
        name="pack",
    )(wide, *small)


def turn_kernel(w_ref, o_ref):
    o_ref[...] = w_ref[...].astype(f32).T


def turn_call(w, at):
    return pl.pallas_call(
        turn_kernel,
        grid=(1,),
        in_specs=[pl.BlockSpec((w.shape[0], 128), lambda i: (0, at))],
        out_specs=whole((128, w.shape[0])),
        out_shape=jax.ShapeDtypeStruct((128, w.shape[0]), f32),
        name="turn",
    )(w)


def up_out_specs(width, ff):
    return [
        pl.BlockSpec((width, width), lambda i, *n: (0, 3)),
        pl.BlockSpec((width, ff), lambda i, *n: (0, 0)),
    ]


def finish_call(counts, x, mixed, w_first, w_up, w_down, small, rows=256, tile=768):
    total, width = x.shape
    ff = w_down.shape[0]
    groups = counts.shape[0]
    narrow, wide = rows_of(rows, width), rows_of(rows, ff)
    return pl.pallas_call(
        functools.partial(finish_kernel, tile=tile, seg=total // groups),
        grid_spec=pltpu.PrefetchScalarGridSpec(
            num_scalar_prefetch=1,
            grid=(total // rows,),
            in_specs=[
                narrow, narrow,
                *up_out_specs(width, ff), whole(w_down.shape),
                whole(small.shape),
            ],
            out_specs=[narrow, narrow, wide, wide, narrow, whole((groups, width))],
        ),
        out_shape=[
            jax.ShapeDtypeStruct((total, width), f32),
            jax.ShapeDtypeStruct((total, width), f32),
            jax.ShapeDtypeStruct((total, ff), bf16),
            jax.ShapeDtypeStruct((total, ff), bf16),
            jax.ShapeDtypeStruct((total, width), bf16),
            jax.ShapeDtypeStruct((groups, width), f32),
        ],
        compiler_params=pltpu.CompilerParams(vmem_limit_bytes=VMEM_CAP),
        cost_estimate=cost(2 * total * width * (width + 2 * ff), 40 << 20),
        name="finish",
    )(counts, x, mixed, w_first, w_up, w_down, small)


def finish_back_kernel(counts_ref, cot_ref, cls_ref, z1_ref, z2_ref, slope_ref, out_ref, up_ref, down_ref,
                       rows_ref,
                       outer_ref, inner_ref, resid_ref, attended_ref, mixed_ref, low_ref, sums_ref, *, tile, seg):
    step = pl.program_id(0)
    rows, width = cot_ref.shape

    @pl.when(step == 0)
    def _():
        sums_ref[...] = jnp.zeros_like(sums_ref)

    at = lax.broadcasted_iota(jnp.int32, (seg, width), 0)
    parts = []
    for s in range(rows // seg):
        here = step * (rows // seg) + s
        block = cot_ref[s * seg : (s + 1) * seg].astype(f32)
        block = jnp.where(at == 0, cls_ref[pl.ds(here, 1), :], block)
        parts.append(jnp.where(at < counts_ref[here], block, 0.0))
    g = jnp.concatenate(parts, axis=0)
    _, unit_two, inv_two = normalize(z2_ref[...], rows_ref[1:2], rows_ref[3:4])
    grad_two = norm_back_rows(g, unit_two, inv_two, rows_ref[1:2])
    outer = grad_two.astype(bf16)
    outer_ref[...] = outer
    sums_ref[1:2] += jnp.sum(g * unit_two, axis=0, keepdims=True)
    sums_ref[3:4] += jnp.sum(g, axis=0, keepdims=True)
    first_grad = grad_two
    for t in range(up_ref.shape[1] // tile):
        cols = pl.ds(t * tile, tile)
        inner = (dot_nt(outer, down_ref[cols, :]) * slope_ref[:, cols].astype(f32)).astype(bf16)
        inner_ref[:, cols] = inner
        first_grad = first_grad + dot_nt(inner, up_ref[:, cols])
    first, unit_one, inv_one = normalize(z1_ref[...], rows_ref[0:1], rows_ref[2:3])
    low_ref[...] = first.astype(bf16)
    grad_one = norm_back_rows(first_grad, unit_one, inv_one, rows_ref[0:1])
    resid_ref[...] = grad_one
    sums_ref[0:1] += jnp.sum(first_grad * unit_one, axis=0, keepdims=True)
    sums_ref[2:3] += jnp.sum(first_grad, axis=0, keepdims=True)
    attended = grad_one.astype(bf16)
    attended_ref[...] = attended
    mixed_ref[...] = dot_nt(attended, out_ref[...]).astype(bf16)


def finish_back_call(counts, cot, cls_grad, z1, z2, slope, w_first, w_up, w_down, small, rows=256, tile=768):
    total, width = cot.shape
    ff = w_down.shape[0]
    groups = counts.shape[0]
    narrow, wide = rows_of(rows, width), rows_of(rows, ff)
    return pl.pallas_call(
        functools.partial(finish_back_kernel, tile=tile, seg=total // groups),
        grid_spec=pltpu.PrefetchScalarGridSpec(
            num_scalar_prefetch=1,
            grid=(total // rows,),
            in_specs=[
                narrow, whole((groups, width)), narrow, narrow, wide,
                *up_out_specs(width, ff), whole(w_down.shape),
                whole(small.shape),
            ],
            out_specs=[narrow, wide, narrow, narrow, narrow, narrow, whole((16, width))],
        ),
        out_shape=[
            jax.ShapeDtypeStruct((total, width), bf16),
            jax.ShapeDtypeStruct((total, ff), bf16),
            jax.ShapeDtypeStruct((total, width), f32),
            jax.ShapeDtypeStruct((total, width), bf16),
            jax.ShapeDtypeStruct((total, width), bf16),
            jax.ShapeDtypeStruct((total, width), bf16),
            jax.ShapeDtypeStruct((16, width), f32),
        ],
        compiler_params=pltpu.CompilerParams(vmem_limit_bytes=VMEM_CAP),
        cost_estimate=cost(2 * total * width * (width + 2 * ff), 40 << 20),
        name="finish_back",
    )(counts, cot, cls_grad, z1, z2, slope, w_first, w_up, w_down, small)


def row_blocks_kernel(ids_ref, a_ref, b_ref, *refs, count):
    extra, (mine_ref, send_ref, turned_ref) = refs[:-3], refs[-3:]
    c, f = ids_ref[0], ids_ref[1]
    half = turned_ref.shape[0] // 2
    unit = half // count

    def place(ref, value):
        for block in range(count):
            for h in range(2):
                to = pl.multiple_of((h ^ c) * half + (block ^ f) * unit, 16)
                ref[pl.ds(to, unit), :] = value[(block * 2 + h) * unit : (block * 2 + h + 1) * unit]

    @pl.when(pl.program_id(0) == 0)
    def _():
        place(turned_ref, a_ref[...].T)

    tile = b_ref.shape[1]
    result = dot(turned_ref[...], b_ref[...]).astype(bf16)
    mine_ref[:, :tile] = result[:half]
    send_ref[:, :tile] = result[half:]
    if extra:
        sums_ref, = extra
        low = sums_ref[...].astype(bf16)
        lanes = lax.broadcasted_iota(jnp.int32, (low.shape[0], 128), 1)
        eye = (lax.broadcasted_iota(jnp.int32, (low.shape[0], 128), 0) == lanes).astype(bf16)
        turned = dot_tn(low, eye).astype(bf16)
        for block in range(count):
            for h in range(2):
                value = turned[(block * 2 + h) * unit : (block * 2 + h + 1) * unit]
                to = pl.multiple_of((block ^ f) * unit, 16)

                @pl.when(h == c)
                def _():
                    mine_ref[pl.ds(to, unit), tile:] = value

                @pl.when(h != c)
                def _():
                    send_ref[pl.ds(to, unit), tile:] = value


def row_blocks_call(ids, a, b, count, sums=None, tile=768):
    total, width = a.shape
    cols = b.shape[1]
    full = cols if sums is None else cols + 128
    step = tile if sums is None else full
    out = pl.BlockSpec((width // 2, step), lambda i, n: (0, i))
    more = [] if sums is None else [sums]
    return pl.pallas_call(
        functools.partial(row_blocks_kernel, count=count),
        grid_spec=pltpu.PrefetchScalarGridSpec(
            num_scalar_prefetch=1,
            grid=(cols // tile,),
            in_specs=[whole(a.shape), pl.BlockSpec((total, tile), lambda i, n: (0, i))] + [whole(m.shape) for m in more],
            out_specs=[out, out],
            scratch_shapes=[pltpu.VMEM((width, total), bf16)],
        ),
        out_shape=[jax.ShapeDtypeStruct((width // 2, full), bf16)] * 2,
        compiler_params=pltpu.CompilerParams(vmem_limit_bytes=VMEM_CAP),
        cost_estimate=cost(2 * total * width * cols * 2, 16 << 20),
        name="row_blocks",
    )(ids, a, b, *more)


def wide_blocks_kernel(ids_ref, a_ref, b_ref, mine_ref, send_ref):
    c = ids_ref[0]
    half = b_ref.shape[1] // 2

    def rows_at(h):
        at = pl.multiple_of(h * half, 128)
        return dot_tn(b_ref[:, pl.ds(at, half)], a_ref[...]).astype(bf16)

    mine_ref[0] = rows_at(c)
    send_ref[0] = rows_at(1 - c)


def wide_blocks_call(ids, a, b, count):
    total, width = a.shape
    block = b.shape[1] // count
    out = pl.BlockSpec((1, block // 2, width), lambda i, n: (i ^ n[1], 0, 0))
    return pl.pallas_call(
        wide_blocks_kernel,
        grid_spec=pltpu.PrefetchScalarGridSpec(
            num_scalar_prefetch=1,
            grid=(count,),
            in_specs=[whole(a.shape), pl.BlockSpec((total, block), lambda i, n: (0, i))],
            out_specs=[out, out],
        ),
        out_shape=[jax.ShapeDtypeStruct((count, block // 2, width), bf16)] * 2,
        compiler_params=pltpu.CompilerParams(vmem_limit_bytes=VMEM_CAP),
        cost_estimate=cost(2 * total * width * b.shape[1] * 2, 16 << 20),
        name="wide_blocks",
    )(ids, a, b)


def token_grad_kernel(resid_ref, g_ref, w_ref, o_ref):
    o_ref[...] = (resid_ref[...] + dot_nt(g_ref[...], w_ref[...])).astype(bf16)


def token_grad_call(resid, g, w_qkv, rows=256):
    total, width = resid.shape
    return pl.pallas_call(
        token_grad_kernel,
        grid=(total // rows,),
        in_specs=[rows_of(rows, width), rows_of(rows, 3 * width), whole((width, 3 * width))],
        out_specs=rows_of(rows, width),
        out_shape=jax.ShapeDtypeStruct((total, width), bf16),
        compiler_params=pltpu.CompilerParams(vmem_limit_bytes=VMEM_CAP),
        cost_estimate=cost(12 * total * width * width, 16 << 20),
        name="token_grad",
    )(resid, g, w_qkv)


def cross_message(cse_qkv, cse_out, cse_up, cse_down, fsize, f):
    rows, width = cse_qkv.shape[0], cse_out.shape[1]
    ff = cse_up.shape[1]
    slim = width // fsize
    cols = jnp.concatenate(
        [
            cse_qkv.reshape(rows, 3, fsize, slim).transpose(2, 0, 1, 3).reshape(fsize, rows, 3 * slim),
            cse_up.reshape(rows, fsize, ff // fsize).transpose(1, 0, 2),
        ],
        axis=-1,
    )
    mine = in_order([part(cols, f, 0)] + [swap_f(part(cols, f ^ d, 0), d) for d in (1, 2, 3)])
    flat = mine.reshape(fsize * rows, -1)
    frows = cse_down.shape[0]
    out_flat = jnp.concatenate([cse_out[:, k * slim : (k + 1) * slim] for k in range(fsize)], axis=0)
    return jnp.concatenate([flat, cse_down, out_flat], axis=-1)


def unpack_kernel(m_ref, qkv_ref, out_ref, up_ref, down_ref, *, fsize):
    reps, frows, _ = m_ref.shape
    rows = frows // fsize
    width, a = qkv_ref.shape
    b, slim = a + up_ref.shape[1], width // fsize
    for r in range(reps):
        for k in range(fsize):
            at, here = k * reps * rows + r * rows, slice(k * rows, (k + 1) * rows)
            qkv_ref[at : at + rows, :] = m_ref[r, here, :a]
            up_ref[at : at + rows, :] = m_ref[r, here, a:b]
        down_ref[r * frows : (r + 1) * frows, :] = m_ref[r, :, b : b + width]
        out = [m_ref[r, k * rows : (k + 1) * rows, b + width :] for k in range(fsize)]
        out_ref[r * rows : (r + 1) * rows, :] = jnp.concatenate(out, axis=-1)


def cross_unpack(gathered, width, ff, fsize):
    reps, frows = gathered.shape[:2]
    slim = width // fsize
    if frows // fsize % 8:
        return cross_unpack_small(gathered, width, ff, fsize)
    shapes = [(width, 3 * slim), (slim, width), (width, ff // fsize), (ff // fsize, width)]
    return pl.pallas_call(
        functools.partial(unpack_kernel, fsize=fsize),
        out_shape=[jax.ShapeDtypeStruct(shape, bf16) for shape in shapes],
        compiler_params=pltpu.CompilerParams(vmem_limit_bytes=VMEM_CAP),
        name="unpack",
    )(gathered)


def cross_unpack_small(gathered, width, ff, fsize):
    slim = width // fsize
    reps, frows = gathered.shape[:2]
    rows = frows // fsize
    a, b = 3 * slim, 3 * slim + ff // fsize
    by_row = gathered[:, :, :b].reshape(reps, fsize, rows, b).transpose(1, 0, 2, 3).reshape(-1, b)
    qkv = by_row[:, :a]
    up = by_row[:, a:]
    down = gathered[:, :, b : b + width].reshape(-1, width)
    out = gathered[:, :, b + width :].reshape(reps, fsize, rows, slim).transpose(0, 2, 1, 3).reshape(-1, width)
    return qkv, out, up, down


def cross_block(cls_in, cotan, weights, gains, biases, fsize, f):
    qkv, out, up, down = weights
    segs, width = cls_in.shape
    slim = width // fsize
    heads = slim // HEAD
    packed = product(cls_in[None], qkv, "gsd,de->gse").astype(bf16)
    queries, keys, values = split_heads(packed, heads)
    every = jnp.ones((1, segs), jnp.bool_)
    mixed, log_total = attend(queries, keys, values, every)
    mixed = mixed.reshape(segs, slim)
    attended = sum_f(product(mixed, out, "sd,de->se"))
    first, unit_one, inv_one = normalize(cls_in.astype(f32) + attended, gains[0], biases[0])
    first_low = first.astype(bf16)
    activated, slope = gelu_pair(product(first_low, up, "sd,df->sf"))
    act_low = activated.astype(bf16)
    outer = sum_f(product(act_low, down, "sf,fd->sd"))
    cls_out, unit_two, inv_two = normalize(first + outer, gains[1], biases[1])

    grad_two, gain_two, bias_two = norm_back(cotan, unit_two, inv_two, gains[1])
    grad_outer = grad_two.astype(bf16)
    grad_inner = (product(grad_outer, down, "sd,fd->sf") * slope).astype(bf16)
    grad_first = grad_two + sum_f(product(grad_inner, up, "sf,df->sd"))
    grad_one, gain_one, bias_one = norm_back(grad_first, unit_one, inv_one, gains[0])
    grad_attended = grad_one.astype(bf16)
    grad_mixed = product(grad_attended, out, "se,de->sd").astype(bf16)
    grad_q, grad_k, grad_v = attend_back(
        queries, keys, values, every, log_total, grad_mixed.reshape(1, segs, heads, HEAD)
    )
    grad_packed = jnp.concatenate(
        [grad_q.reshape(segs, slim), grad_k.reshape(segs, slim), grad_v.reshape(segs, slim)], axis=-1
    ).astype(bf16)
    grad_in = grad_one + sum_f(product(grad_packed, qkv, "se,de->sd"))

    def own(value):
        return lax.dynamic_slice_in_dim(value, f * slim, slim, value.ndim - 1)

    sums = jnp.stack([gain_one, gain_two, bias_one, bias_two])
    pieces = {
        "packed": grad_packed,
        "inner": grad_inner,
        "act": act_low,
        "outer": grad_outer,
        "attended": grad_attended,
        "mixed": mixed,
        "own_in": own(cls_in),
        "own_low": own(first_low),
        "own_grad": own(grad_in).astype(bf16),
        "sums": jnp.pad(own(sums), ((0, segs - 4), (0, 0))).astype(bf16),
    }
    return cls_out, grad_in, pieces


def doc_message(spread, pieces, fsize, width):
    segs = spread.shape[1]
    slim = width // fsize
    qkv_cols = spread[:, :, : 3 * slim].reshape(fsize, segs, 3, slim).transpose(1, 2, 0, 3)
    parts = {"packed": qkv_cols.reshape(segs, 3 * width), "inner": spread[:, :, 3 * slim :].transpose(1, 0, 2).reshape(segs, -1)}
    parts = {**pieces, **parts}
    ends, at = {}, 0
    for name, value in parts.items():
        ends[name] = (at, at + value.shape[1])
        at += value.shape[1] + -value.shape[1] % 128
    parts = {k: jnp.pad(v, ((0, 0), (0, -v.shape[1] % 128))) for k, v in parts.items()}
    return jnp.concatenate(list(parts.values()), axis=-1), ends


def cross_grads(docs, ends):
    flat = docs.reshape(-1, docs.shape[-1])
    cut = {name: flat[:, a:b] for name, (a, b) in ends.items()}
    g_qkv = product(cut["own_in"], cut["packed"], "rd,re->de")
    g_out = product(cut["mixed"], cut["attended"], "rd,re->de")
    g_up = product(cut["own_low"], cut["inner"], "rd,re->de")
    g_down = product(cut["act"], cut["outer"], "rd,re->de")
    part_of = {name: docs[:, :, ends[name][0] : ends[name][1]].astype(f32) for name in ("own_grad", "sums")}
    g_pos = jnp.sum(part_of["own_grad"], axis=0)
    g_sums = jnp.sum(part_of["sums"][:, :4], axis=0)
    return g_qkv, g_out, g_up, g_down, g_sums[0:2], g_sums[2:4], g_pos


def per_device(
    tokens, counts, cotangent,
    swe_qkv, swe_out, swe_up, swe_down, swe_gains, swe_biases,
    cse_qkv, cse_out, cse_up, cse_down, cse_gains, cse_biases, positions,
):
    docs_here, local_len, width = tokens.shape
    ff = swe_up.shape[1]
    seg_here = counts.shape[1]
    groups = docs_here * seg_here
    fsize = lax.axis_size("y") * lax.axis_size("x")
    f = lax.axis_index("y") * lax.axis_size("x") + lax.axis_index("x")
    c = lax.axis_index("c")
    ids = jnp.stack([c, f])
    segs = fsize * seg_here
    x = tokens.reshape(-1, width)
    cot = cotangent.reshape(-1, width)
    lens = counts.reshape(groups)

    small = [swe_gains, swe_biases, cse_gains, cse_biases, positions]
    count_small = sum(v.shape[0] for v in small)
    packed_up = pack_call(swe_up, small)
    w_up = lax.all_gather(packed_up, ("y", "x", "z", "c"), axis=0, tiled=True)
    first = RowGather(tie(jnp.concatenate([swe_qkv, swe_out], axis=-1), packed_up))
    first.far_z()
    down = RowGather(tie(swe_down, first.state))
    first.near_z()
    first.after(down.state)
    down.after(first.state)
    turned = first.state
    first.plane_first()
    down.far_z()
    message = cross_message(*tie((cse_qkv, cse_out, cse_up, cse_down), turned), fsize, f)
    down.after(first.state)
    first.after(down.state, message)
    first.plane_second()
    down.near_z()
    first.after(down.state)
    down.after(first.state)
    first.sibling()
    w_first = side_by_side(*first.state, c)
    down.plane_first(w_first)
    packed, mixed = attend_call(lens, x, tie(w_first, down.state))
    down.plane_second(packed)
    w_up = tie(w_up, packed, down.state)
    down.after(w_up)
    cross = lax.all_gather(tie(message, w_up), ("z", "c"), axis=0)
    down.sibling()
    w_down = side_by_side(*down.state, c)
    rows = turn_call(w_up, ff // 128)
    gains, biases, cross_gains, cross_biases, pos = (
        rows[0:2], rows[2:4], rows[4:6], rows[6:8], rows[8:count_small]
    )
    z1, z2, act, slope, hidden, cls_rows = finish_call(lens, x, mixed, w_first, w_up, w_down, rows)
    cross_w = cross_unpack(cross, width, ff, fsize)

    pos_here = lax.dynamic_slice_in_dim(pos, f * seg_here, seg_here, 0)
    cls_here = (cls_rows + pos_here).astype(bf16)
    cls_cot = cot.reshape(groups, -1, width)[:, 0]
    both = gather_f(jnp.concatenate([cls_here, cls_cot], axis=-1), cross_w).reshape(segs, 2 * width)
    cls_out, cls_grad, pieces = cross_block(
        both[:, :width], both[:, width:].astype(f32), cross_w, cross_gains, cross_biases, fsize, f,
    )
    cls_out = lax.dynamic_slice_in_dim(cls_out, f * seg_here, seg_here, 0)
    cls_here_grad = lax.dynamic_slice_in_dim(cls_grad, f * seg_here, seg_here, 0)

    spread = tie(jnp.concatenate([pieces["packed"], pieces["inner"]], axis=-1), cls_grad)
    outer, inner, resid, attended, grad_mixed, low, sums = finish_back_call(
        lens, cot, tie(cls_here_grad, spread), z1, z2, slope, w_first, w_up, w_down, rows
    )
    spread = gather_f(spread, outer)
    layer_out = hidden.reshape(groups, -1, width).at[:, 0].set(tie(cls_out.astype(bf16), outer))
    message, ends = doc_message(tie(spread, outer), pieces, fsize, width)
    docs = lax.all_gather(message, ("z", "c"), axis=0)
    red_down, red_up, red_qkv = RowReduce(), RowReduce(), RowReduce()
    g_down = wide_blocks_call(ids, tie(outer, message), act, fsize)
    g_out = row_blocks_call(ids, tie(mixed, g_down), attended, fsize, sums)
    red_down.core(g_down, g_out)
    red_down.chip()
    g_up = row_blocks_call(ids, tie(low, red_down.state), inner, fsize)
    red_down.plane_first(g_up)
    red_up.core(g_out, g_up)
    red_up.core(tie(g_up, red_down.state))
    red_up.chip()
    red_down.after(red_up.state)
    grad_packed = attend_back_call(lens, packed, tie(grad_mixed, red_up.state, red_down.state))
    red_down.plane_second(grad_packed)
    red_up.plane_first(grad_packed)
    red_down.after(grad_packed, red_up.state)
    red_up.after(red_down.state)
    g_qkv = row_blocks_call(ids, x, tie(grad_packed, red_up.state, red_down.state), fsize)
    red_up.plane_second(g_qkv)
    red_down.near_z(g_qkv)
    red_qkv.core(tie(g_qkv, red_up.state, red_down.state))
    red_qkv.chip_direct()
    red_down.far_z(red_qkv.state)
    red_up.near_z(red_qkv.state)
    red_up.after(red_qkv.state, red_down.state)
    red_down.after(red_up.state)
    token_grad = token_grad_call(tie(resid, red_qkv.state, red_down.state, red_up.state), grad_packed, w_first)
    red_down.back_far(token_grad)
    red_up.far_z(token_grad)
    others = cross_grads(tie(docs, token_grad), ends)
    red_qkv.plane_direct(token_grad)
    red_down.back_near()
    red_up.back_far()

    def step(*moves):
        states = lax.optimization_barrier([r.state for r in (red_qkv, red_up, red_down)])
        for r, state in zip((red_qkv, red_up, red_down), states, strict=True):
            r.state = state
        for move in moves:
            move()

    red_qkv.near_z()
    step(red_qkv.far_z, red_up.back_near, red_down.back_core)
    red_qkv.back_far()
    step(red_qkv.back_near, red_up.back_core)
    done_out, done_up = ungroup(red_up.state.astype(f32), (width + 128, ff))
    done_down = red_down.state.astype(f32)
    red_qkv.back_core(layer_out, done_out, done_up, done_down)
    done_qkv = red_qkv.state.astype(f32)
    small_grads = done_out[:, width : width + 4].T
    return (
        layer_out.reshape(tokens.shape),
        token_grad.reshape(tokens.shape),
        done_qkv,
        done_out[:, :width],
        done_up,
        done_down,
        small_grads[0:2],
        small_grads[2:4],
    ) + others


def solution(mesh):
    fsize, rsize = mesh.shape["fsdp"], mesh.shape["rep"]
    fine = Mesh(mesh.devices.reshape(2, fsize // 2, rsize // 2, 2), ("y", "x", "z", "c"))
    fs, rep = ("y", "x"), ("z", "c")
    every = fs + rep
    by_rows, by_cols = P(every, None), P(None, every)
    block = (by_rows,) * 4 + (by_cols,) * 2
    grads = (P(fs, None),) * 4 + (P(None, fs),) * 2
    return jax.shard_map(
        per_device,
        mesh=fine,
        in_specs=(P(rep, fs, None), P(rep, fs), P(rep, fs, None)) + block + block + (by_cols,),
        out_specs=(P(rep, fs, None),) * 2 + grads + grads + (P(None, fs),),
        check_vma=False,
    )
```

time: 527 us -> 432 us (0.82)
  Pallas kernels: 0 us -> 129 us
  matrix products: 117 us -> 18.1 us
  waiting for transfers between devices: 190 us -> 140 us
  local copies, waits for them, and re-layouts: 68.8 us -> 19.3 us
  other arithmetic: 54.7 us -> 35 us
  starting transfers between devices: 85.1 us -> 67.8 us
  between operations: 3.65 us -> 15.7 us
    pallas_call x0 -> x12, Pallas kernels: none -> 129 us  [the longest x3 24.4 us: row_blocks_call(): pl.pallas_call(functools.partial(row_blocks_kernel, count=count), grid_sp...]
    dot_general x36 -> x18, matrix products: 117 us -> 18.1 us  [product(): jnp.einsum(einsum_form, left_op, right_op, preferred_element_type=f32)]
    ppermute x75 -> x67, waiting for transfers between devices: 190 us -> 139 us  [the longest x43 122 us: swap(): got = lax.ppermute(value, axis, [(i, i ^ bit) for i in range(size)])]
    ppermute x75 -> x67, starting transfers between devices: 85.1 us -> 67.4 us  [the longest x43 39.2 us: swap(): got = lax.ppermute(value, axis, [(i, i ^ bit) for i in range(size)])]
    reshape x14 -> x8, local copies, waits for them, and re-layouts: 14.3 us -> 0.89 us  [the longest x4 0.46 us: cross_message(): cse_qkv.reshape(rows, 3, fsize, slim).transpose(2, 0, 1, 3)]
    unnamed x194 -> x86, local copies, waits for them, and re-layouts: 18.2 us -> 7.16 us
    another operation x56 -> x34, other arithmetic: 12.8 us -> 3.46 us  [join(): jnp.stack([jnp.where(first, mine, other), jnp.where(first, other, mine)],...]
    concatenate x6 -> x12, other arithmetic: 2.42 us -> 10.3 us  [the longest x2 4.1 us: ungroup(): jnp.concatenate([reduced[:, left:left + half], reduced[:, right:right + s...]
  transfers between devices with their start and end apart: 75 -> 70, of which waited for: 40 -> 45; matrix products, arithmetic and copies ran while one was open for 19% -> 12% of each run, Pallas kernels for 0% -> 28%
where the time goes in v2:
time: 432 us; the launch traced here: 424 us
  waiting for transfers between devices  140 us (32%)
  Pallas kernels  129 us (30%)
  starting transfers between devices  67.8 us (16%)
  other arithmetic  35 us (8%)
  local copies, waits for them, and re-layouts  19.3 us (4%)
  matrix products  18.1 us (4%)
  between operations  15.7 us (4%)
    ppermute x43, waiting for transfers between devices, swap(): got = lax.ppermute(value, axis, [(i, i ^ bit) for i in range(size)])  122 us
    ppermute x43, starting transfers between devices, swap(): got = lax.ppermute(value, axis, [(i, i ^ bit) for i in range(size)])  39.2 us
    ppermute x24, starting transfers between devices, swap_f(): got = lax.ppermute(value, ('y', 'x'), [(i, i ^ dist) for i in range(count)])  28.2 us
    pallas_call x3, Pallas kernels, row_blocks_call(): pl.pallas_call(functools.partial(row_blocks_kernel, count=count), grid_sp...  24.4 us
    pallas_call x1, Pallas kernels, finish_call(): pl.pallas_call(functools.partial(finish_kernel, tile=tile, seg=total // g...  23.8 us
    pallas_call x1, Pallas kernels, finish_back_call(): pl.pallas_call(functools.partial(finish_back_kernel, tile=tile, seg=total...  23.4 us
    dot_general x18, matrix products, product(): jnp.einsum(einsum_form, left_op, right_op, preferred_element_type=f32)  18.1 us
    pallas_call x1, Pallas kernels, attend_back_call(): pl.pallas_call(functools.partial(attend_back_kernel, seg=total // counts....  17.9 us
  transfers between devices with their start and end apart: 70, of which 45 were waited for; matrix products, arithmetic and copies ran while one was open for 12% of the time, Pallas kernels for 28%

profile of v2, /device:TPU:0, one launch (start us, length us, event | category | flops | bytes accessed | tf_op | source)
XLA Modules:
  0.0 424.4 jit_solution(17032230361607024166)
XLA Ops:
  12.9 4.0 collective-permute-start.1
  16.9 7.3 %collective-permute-done.1 = bf16[1,48,1536]{2,1,0:T(8,128)(2,1)S(1)} collective-permute-done((bf16[1,48,1536]{2,1,0:T(8,128)(2,1)S(1)}, bf16[1,48,1536]{2,1,0:T(8,128)(2,1)S(1)}, u32[]{:S(2)}, u32[]{:S(2)}) %collective-permute-start.1) | collective-permute-done | bytes 147488 | tf_op jit(solution)/shard_map/ppermute | solution.py:25
  25.7 8.2 %collective-permute-done.2 = bf16[2,48,1536]{2,1,0:T(8,128)(2,1)S(1)} collective-permute-done((bf16[2,48,1536]{2,1,0:T(8,128)(2,1)S(1)}, bf16[2,48,1536]{2,1,0:T(8,128)(2,1)S(1)}, u32[]{:S(2)}, u32[]{:S(2)}) %collective-permute-start.2) | collective-permute-done | bytes 294944 | tf_op jit(solution)/shard_map/ppermute | solution.py:25
  47.7 3.7 collective-permute-done.5
  57.4 6.2 %collective-permute-done.12 = bf16[2,192,384]{2,1,0:T(8,128)(2,1)S(1)} collective-permute-done((bf16[2,192,384]{2,1,0:T(8,128)(2,1)S(1)}, bf16[2,192,384]{2,1,0:T(8,128)(2,1)S(1)}, u32[]{:S(2)}, u32[]{:S(2)}) %collective-permute-start.12) | collective-permute-done | bytes 294944 | tf_op jit(solution)/shard_map/ppermute | solution.py:25
  63.8 6.4 %collective-permute-done.10 = bf16[2,2,48,1536]{3,2,1,0:T(8,128)(2,1)S(1)} collective-permute-done((bf16[2,2,48,1536]{3,2,1,0:T(8,128)(2,1)S(1)}, bf16[2,2,48,1536]{3,2,1,0:T(8,128)(2,1)S(1)}, u32[]{:S(2)}, u32[]{:S(2)}) %collective-permute-start.10) | collective-permute-done | bytes 589856 | tf_op jit(solution)/shard_map/ppermute | solution.py:25
  78.2 9.8 %collective-permute-done.15 = bf16[2,192,384]{2,1,0:T(8,128)(2,1)S(1)} collective-permute-done((bf16[2,192,384]{2,1,0:T(8,128)(2,1)S(1)}, bf16[2,192,384]{2,1,0:T(8,128)(2,1)S(1)}, u32[]{:S(2)}, u32[]{:S(2)}) %collective-permute-start.15) | collective-permute-done | bytes 294944 | tf_op jit(solution)/shard_map/ppermute | solution.py:25
  91.0 12.6 %attend.1 = (bf16[1024,2304]{1,0:T(8,128)(2,1)}, bf16[1024,768]{1,0:T(8,128)(2,1)}) custom-call(s32[8]{0:T(128)} %bitcast.394, bf16[1024,768]{1,0:T(8,128)(2,1)} %bitcast.389, bf16[768,3072]{1,0:T(8,128)(2,1)} %copy-done.1), custom_call_target="tpu_custom_call" | custom-call | flops 4831838208 | bytes 16777216 | tf_op jit(solution)/shard_map/attend/pallas_call | solution.py:357
  111.2 3.1 pad_maximum_fusion.1
  116.8 23.8 %finish.1 = (f32[1024,768]{1,0:T(8,128)}, f32[1024,768]{1,0:T(8,128)}, bf16[1024,3072]{1,0:T(8,128)(2,1)}, bf16[1024,3072]{1,0:T(8,128)(2,1)}, bf16[1024,768]{1,0:T(8,128)(2,1)}, /*index=5*/f32[8,768]{1,0:T(8,128)}) custom-call(s32[8]{0:T(128)} %bitcast.395, bf16[1024,768]{1,0:T(8,128)(2,1)} %bitcast.390, ...), custom_call_target="tpu_custom_call" | custom-call | flops 10871635968 | bytes 41943040 | tf_op jit(solution)/shard_map/finish/pallas_call | solution.py:511
  145.4 4.8 %unpack.1 = (bf16[768,576]{1,0:T(8,128)(2,1)}, bf16[192,768]{1,0:T(8,128)(2,1)}, bf16[768,768]{1,0:T(8,128)(2,1)}, bf16[768,768]{1,0:T(8,128)(2,1)}) custom-call(bf16[8,96,2304]{2,1,0:T(8,128)(2,1)} %bitcast.360), custom_call_target="tpu_custom_call" | custom-call | tf_op jit(solution)/shard_map/unpack/pallas_call | solution.py:761
  196.6 23.4 %finish_back.1 = (bf16[1024,768]{1,0:T(8,128)(2,1)}, bf16[1024,3072]{1,0:T(8,128)(2,1)}, f32[1024,768]{1,0:T(8,128)}, bf16[1024,768]{1,0:T(8,128)(2,1)}, bf16[10...) custom-call(s32[8]{0:T(128)} %bitcast.396, bf16[1024,768]{1,0:T(8,128)(2,1)} %bitcast.388, ...), custom_call_target="tpu_custom_call" | custom-call | flops 10871635968 | bytes 41943040 | tf_op jit(solution)/shard_map/finish_back/pallas_call | solution.py:583
  221.5 9.4 %wide_blocks.1 = (bf16[4,384,768]{2,1,0:T(8,128)(2,1)}, bf16[4,384,768]{2,1,0:T(8,128)(2,1)}) custom-call(s32[2]{0:T(128)} %pad_add_fusion.ids_ref, bf16[1024,768]{1,0:T(8,128)(2,1)} %get-tuple-element.177.a_ref, bf16[1024,3072]{1,0:T(8,128)(2,1)} %get-tuple-element.178.b_ref), custom_call_target="tpu_custom_call" | custom-call | flops 9663676416 | bytes 16777216 | tf_op jit(solution)/shard_map/wide_blocks/pallas_call | solution.py:689
  230.9 5.7 %row_blocks.3 = (bf16[384,896]{1,0:T(8,128)(2,1)}, bf16[384,896]{1,0:T(8,128)(2,1)}) custom-call(s32[2]{0:T(128)} %pad_add_fusion.ids_ref, bf16[1024,768]{1,0:T(8,128)(2,1)} %get-tuple-element.181.mixed_ref.a_ref, bf16[1024,768]{1,0:T(8,128)(2,1)} %get-tuple-element.182.b_ref, f32[16,768]{1,0:T(8,128)} %get-tuple-element.183.refs_0_), custom_call_target="tpu_custom_call" | custom-call | flops 2415919104 | bytes 16777216 | tf_op jit(solution)/shard_map/row_blocks/pallas_call | solution.py:657
  239.5 10.2 %row_blocks.4 = (bf16[384,3072]{1,0:T(8,128)(2,1)}, bf16[384,3072]{1,0:T(8,128)(2,1)}) custom-call(s32[2]{0:T(128)} %pad_add_fusion.ids_ref, bf16[1024,768]{1,0:T(8,128)(2,1)} %get-tuple-element.188.a_ref, bf16[1024,3072]{1,0:T(8,128)(2,1)} %get-tuple-element.189.b_ref), custom_call_target="tpu_custom_call" | custom-call | flops 9663676416 | bytes 16777216 | tf_op jit(solution)/shard_map/row_blocks/pallas_call | solution.py:657
  249.7 3.3 collective-permute-done.39
  271.8 17.9 %attend_back.1.b_ref.g_ref = bf16[1024,2304]{1,0:T(8,128)(2,1)} custom-call(s32[8]{0:T(128)} %bitcast.397, bf16[1024,2304]{1,0:T(8,128)(2,1)} %get-tuple-element.149.packed_ref, bf16[1024,768]{1,0:T(8,128)(2,1)} %get-tuple-element.201.grad_ref), custom_call_target="tpu_custom_call" | custom-call | flops 9663676416 | bytes 16777216 | tf_op jit(solution)/shard_map/attend_back/pallas_call | solution.py:410
  289.7 4.0 collective-permute-done.44
  296.9 8.5 %row_blocks.5 = (bf16[384,2304]{1,0:T(8,128)(2,1)}, bf16[384,2304]{1,0:T(8,128)(2,1)}) custom-call(s32[2]{0:T(128)} %pad_add_fusion.ids_ref, bf16[1024,768]{1,0:T(8,128)(2,1)} %bitcast.391, bf16[1024,2304]{1,0:T(8,128)(2,1)} %attend_back.1.b_ref.g_ref), custom_call_target="tpu_custom_call" | custom-call | flops 7247757312 | bytes 16777216 | tf_op jit(solution)/shard_map/row_blocks/pallas_call | solution.py:657
  305.4 5.0 %collective-permute-done.46 = bf16[2,96,768]{2,1,0:T(8,128)(2,1)S(1)} collective-permute-done((bf16[2,96,768]{2,1,0:T(8,128)(2,1)S(1)}, bf16[2,96,768]{2,1,0:T(8,128)(2,1)S(1)}, u32[]{:S(2)}, u32[]{:S(2)}) %collective-permute-start.46) | collective-permute-done | bytes 294944 | tf_op jit(solution)/shard_map/ppermute | solution.py:25
  314.0 3.2 collective-permute-done.47
  321.1 6.8 %collective-permute-done.51 = bf16[2,24,3968]{2,1,0:T(8,128)(2,1)S(1)} collective-permute-done((bf16[2,24,3968]{2,1,0:T(8,128)(2,1)S(1)}, bf16[2,24,3968]{2,1,0:T(8,128)(2,1)S(1)}, u32[]{:S(2)}, u32[]{:S(2)}) %collective-permute-start.51) | collective-permute-done | bytes 380960 | tf_op jit(solution)/shard_map/ppermute | solution.py:25
  328.2 8.7 %token_grad.1 = bf16[1024,768]{1,0:T(8,128)(2,1)} custom-call(f32[1024,768]{1,0:T(8,128)} %get-tuple-element.223.resid_ref, bf16[1024,2304]{1,0:T(8,128)(2,1)} %attend_back.1.b_ref.g_ref, bf16[768,3072]{1,0:T(8,128)(2,1)} %copy-done.1), custom_call_target="tpu_custom_call" | custom-call | flops 7247757312 | bytes 16777216 | tf_op jit(solution)/shard_map/token_grad/pallas_call | solution.py:710
  339.9 3.4 fusion
  351.4 6.5 %collective-permute-done.56 = bf16[1,24,3968]{2,1,0:T(8,128)(2,1)S(1)} collective-permute-done((bf16[1,24,3968]{2,1,0:T(8,128)(2,1)S(1)}, bf16[1,24,3968]{2,1,0:T(8,128)(2,1)S(1)}, u32[]{:S(2)}, u32[]{:S(2)}) %collective-permute-start.56) | collective-permute-done | bytes 190496 | tf_op jit(solution)/shard_map/ppermute | solution.py:25
  360.3 7.1 %collective-permute-done.57 = bf16[1,24,3968]{2,1,0:T(8,128)(2,1)S(1)} collective-permute-done((bf16[1,24,3968]{2,1,0:T(8,128)(2,1)S(1)}, bf16[1,24,3968]{2,1,0:T(8,128)(2,1)S(1)}, u32[]{:S(2)}, u32[]{:S(2)}) %collective-permute-start.57) | collective-permute-done | bytes 190496 | tf_op jit(solution)/shard_map/ppermute | solution.py:25
  371.0 5.3 %collective-permute-done.55 = bf16[2,24,2304]{2,1,0:T(8,128)(2,1)S(1)} collective-permute-done((bf16[2,24,2304]{2,1,0:T(8,128)(2,1)S(1)}, bf16[2,24,2304]{2,1,0:T(8,128)(2,1)S(1)}, u32[]{:S(2)}, u32[]{:S(2)}) %collective-permute-start.55) | collective-permute-done | bytes 221216 | tf_op jit(solution)/shard_map/ppermute | solution.py:25
  378.8 4.9 %collective-permute-done.60 = bf16[1,24,2304]{2,1,0:T(8,128)(2,1)S(1)} collective-permute-done((bf16[1,24,2304]{2,1,0:T(8,128)(2,1)S(1)}, bf16[1,24,2304]{2,1,0:T(8,128)(2,1)S(1)}, u32[]{:S(2)}, u32[]{:S(2)}) %collective-permute-start.60) | collective-permute-done | bytes 110624 | tf_op jit(solution)/shard_map/ppermute | solution.py:25
  386.6 3.8 collective-permute-done.61
  390.4 7.0 %collective-permute-done.62 = bf16[2,24,3968]{2,1,0:T(8,128)(2,1)S(1)} collective-permute-done((bf16[2,24,3968]{2,1,0:T(8,128)(2,1)S(1)}, bf16[2,24,3968]{2,1,0:T(8,128)(2,1)S(1)}, u32[]{:S(2)}, u32[]{:S(2)}) %collective-permute-start.62) | collective-permute-done | bytes 380960 | tf_op jit(solution)/shard_map/ppermute | solution.py:25
  400.1 4.1 collective-permute-done.64
  411.0 3.2 pad_maximum_fusion.2
  (415 shorter events, 167.2 us)
Async XLA Ops:
  7.2 99.0 %all-gather.6.cloned.1.call-start = ((), (), s32[]{:S(2)}) async-start(), calls=%async_computation | async-start | bytes 5068800 | tf_op jit(solution)/shard_map/all_gather | solution.py:882
  12.9 11.3 %collective-permute-start.1 = (bf16[1,48,1536]{2,1,0:T(8,128)(2,1)S(1)}, bf16[1,48,1536]{2,1,0:T(8,128)(2,1)S(1)}, u32[]{:S(2)}, u32[]{:S(2)}) collective-permute-start(bf16[1,48,1536]{2,1,0:T(8,128)(2,1)S(1)} %bitcast.379), channel_id=1, source_target_pairs={{0,4},{2,6},{4,0},{6,2},{1,5},{3,7},{5,1},{7,3},{8,12},{10,14},{12... | collective-permute-start | bytes 442376 | tf_op jit(solution)/shard_map/ppermute | solution.py:25
  24.4 121.0 %all-gather.8.cloned.1.call-start = ((), (), s32[]{:S(2)}) async-start(), calls=%async_computation.1 | async-start | bytes 3981312 | tf_op jit(solution)/shard_map/all_gather | solution.py:906
  35.0 12.6 %collective-permute-start.6 = (bf16[1,192,384]{2,1,0:T(8,128)(2,1)S(1)}, bf16[1,192,384]{2,1,0:T(8,128)(2,1)S(1)}, u32[]{:S(2)}, u32[]{:S(2)}) collective-permute-start(bf16[1,192,384]{2,1,0:T(8,128)(2,1)S(1)} %bitcast.377), channel_id=1, source_target_pairs={{0,4},{2,6},{4,0},{6,2},{1,5},{3,7},{5,1},{7,3},{8,12},{10,14},{12... | collective-permute-start | bytes 442376 | tf_op jit(solution)/shard_map/ppermute | solution.py:25
  55.1 15.1 %collective-permute-start.10 = (bf16[2,2,48,1536]{3,2,1,0:T(8,128)(2,1)S(1)}, bf16[2,2,48,1536]{3,2,1,0:T(8,128)(2,1)S(1)}, u32[]{:S(2)}, u32[]{:S(2)}) collective-permute-start(bf16[2,2,48,1536]{3,2,1,0:T(8,128)(2,1)S(1)} %get-tuple-element.141), channel_id=1, source_target_pairs={{0,16},{16,0},{1,17},{17,1},{2,18},{18,2},{3,19},{19,3},{4,20},{20... | collective-permute-start | bytes 1769480 | tf_op jit(solution)/shard_map/ppermute | solution.py:25
  56.6 15.8 %collective-permute-start.11 = (bf16[2,2,48,1536]{3,2,1,0:T(8,128)(2,1)S(1)}, bf16[2,2,48,1536]{3,2,1,0:T(8,128)(2,1)S(1)}, u32[]{:S(2)}, u32[]{:S(2)}) collective-permute-start(bf16[2,2,48,1536]{3,2,1,0:T(8,128)(2,1)S(1)} %get-tuple-element.142), channel_id=1, source_target_pairs={{0,8},{8,0},{1,9},{9,1},{2,10},{10,2},{3,11},{11,3},{4,12},{12,4},... | collective-permute-start | bytes 1769480 | tf_op jit(solution)/shard_map/ppermute | solution.py:25
  72.9 15.2 %collective-permute-start.15 = (bf16[2,192,384]{2,1,0:T(8,128)(2,1)S(1)}, bf16[2,192,384]{2,1,0:T(8,128)(2,1)S(1)}, u32[]{:S(2)}, u32[]{:S(2)}) collective-permute-start(bf16[2,192,384]{2,1,0:T(8,128)(2,1)S(1)} %get-tuple-element.368), channel_id=1, source_target_pairs={{0,16},{16,0},{1,17},{17,1},{2,18},{18,2},{3,19},{19,3},{4,20},{20... | collective-permute-start | bytes 884744 | tf_op jit(solution)/shard_map/ppermute | solution.py:25
  74.4 15.5 %collective-permute-start.14 = (bf16[2,192,384]{2,1,0:T(8,128)(2,1)S(1)}, bf16[2,192,384]{2,1,0:T(8,128)(2,1)S(1)}, u32[]{:S(2)}, u32[]{:S(2)}) collective-permute-start(bf16[2,192,384]{2,1,0:T(8,128)(2,1)S(1)} %get-tuple-element.369), channel_id=1, source_target_pairs={{0,8},{8,0},{1,9},{9,1},{2,10},{10,2},{3,11},{11,3},{4,12},{12,4},... | collective-permute-start | bytes 884744 | tf_op jit(solution)/shard_map/ppermute | solution.py:25
  90.2 15.2 %collective-permute-start.17 = (bf16[2,2,192,384]{3,2,1,0:T(8,128)(2,1)S(1)}, bf16[2,2,192,384]{3,2,1,0:T(8,128)(2,1)S(1)}, u32[]{:S(2)}, u32[]{:S(2)}) collective-permute-start(bf16[2,2,192,384]{3,2,1,0:T(8,128)(2,1)S(1)} %pad_maximum_fusion.18), channel_id=1, source_target_pairs={{0,8},{8,0},{1,9},{9,1},{2,10},{10,2},{3,11},{11,3},{4,12},{12,4},... | collective-permute-start | bytes 1769480 | tf_op jit(solution)/shard_map/ppermute | solution.py:25
  90.9 14.6 %collective-permute-start.16 = (bf16[2,2,192,384]{3,2,1,0:T(8,128)(2,1)S(1)}, bf16[2,2,192,384]{3,2,1,0:T(8,128)(2,1)S(1)}, u32[]{:S(2)}, u32[]{:S(2)}) collective-permute-start(bf16[2,2,192,384]{3,2,1,0:T(8,128)(2,1)S(1)} %pad_maximum_fusion.17), channel_id=1, source_target_pairs={{0,16},{16,0},{1,17},{17,1},{2,18},{18,2},{3,19},{19,3},{4,20},{20... | collective-permute-start | bytes 1769480 | tf_op jit(solution)/shard_map/ppermute | solution.py:25
  106.2 230.8 %all-gather.10.cloned.1.call-start = ((), (), s32[]{:S(2)}) async-start(), calls=%async_computation.2 | async-start | bytes 5160960 | tf_op jit(solution)/shard_map/all_gather | solution.py:933
  193.1 27.0 %collective-permute-start.35 = (bf16[32,1344]{1,0:T(8,128)(2,1)S(1)}, bf16[32,1344]{1,0:T(8,128)(2,1)S(1)}, u32[]{:S(2)}, u32[]{:S(2)}) collective-permute-start(bf16[32,1344]{1,0:T(8,128)(2,1)S(1)} %concatenate.97), channel_id=1, source_target_pairs={{0,16},{8,24},{16,0},{24,8},{1,17},{9,25},{17,1},{25,9},{2,18},{10... | collective-permute-start | bytes 258056 | tf_op jit(solution)/shard_map/ppermute | solution.py:113
  194.6 25.5 %collective-permute-start.36 = (bf16[32,1344]{1,0:T(8,128)(2,1)S(1)}, bf16[32,1344]{1,0:T(8,128)(2,1)S(1)}, u32[]{:S(2)}, u32[]{:S(2)}) collective-permute-start(bf16[32,1344]{1,0:T(8,128)(2,1)S(1)} %concatenate.97), channel_id=1, source_target_pairs={{0,24},{8,16},{16,8},{24,0},{1,25},{9,17},{17,9},{25,1},{2,26},{10... | collective-permute-start | bytes 258056 | tf_op jit(solution)/shard_map/ppermute | solution.py:113
  196.1 24.0 %collective-permute-start.34 = (bf16[32,1344]{1,0:T(8,128)(2,1)S(1)}, bf16[32,1344]{1,0:T(8,128)(2,1)S(1)}, u32[]{:S(2)}, u32[]{:S(2)}) collective-permute-start(bf16[32,1344]{1,0:T(8,128)(2,1)S(1)} %concatenate.97), channel_id=1, source_target_pairs={{0,8},{8,0},{16,24},{24,16},{1,9},{9,1},{17,25},{25,17},{2,10},{10... | collective-permute-start | bytes 258056 | tf_op jit(solution)/shard_map/ppermute | solution.py:113
  237.2 15.8 %collective-permute-start.39 = (bf16[2,384,384]{2,1,0:T(8,128)(2,1)S(1)}, bf16[2,384,384]{2,1,0:T(8,128)(2,1)S(1)}, u32[]{:S(2)}, u32[]{:S(2)}) collective-permute-start(bf16[2,384,384]{2,1,0:T(8,128)(2,1)S(1)} %pad_maximum_fusion.19), channel_id=1, source_target_pairs={{0,8},{8,0},{1,9},{9,1},{2,10},{10,2},{3,11},{11,3},{4,12},{12,4},... | collective-permute-start | bytes 1769480 | tf_op jit(solution)/shard_map/ppermute | solution.py:25
  238.9 15.5 %collective-permute-start.40 = (bf16[2,384,384]{2,1,0:T(8,128)(2,1)S(1)}, bf16[2,384,384]{2,1,0:T(8,128)(2,1)S(1)}, u32[]{:S(2)}, u32[]{:S(2)}) collective-permute-start(bf16[2,384,384]{2,1,0:T(8,128)(2,1)S(1)} %pad_maximum_fusion.20), channel_id=1, source_target_pairs={{0,16},{16,0},{1,17},{17,1},{2,18},{18,2},{3,19},{19,3},{4,20},{20... | collective-permute-start | bytes 1769480 | tf_op jit(solution)/shard_map/ppermute | solution.py:25
  267.5 26.5 %collective-permute-start.42 = (bf16[2,96,1920]{2,1,0:T(8,128)(2,1)S(1)}, bf16[2,96,1920]{2,1,0:T(8,128)(2,1)S(1)}, u32[]{:S(2)}, u32[]{:S(2)}) collective-permute-start(bf16[2,96,1920]{2,1,0:T(8,128)(2,1)S(1)} %pad_maximum_fusion.12), channel_id=1, source_target_pairs={{0,8},{8,0},{1,9},{9,1},{2,10},{10,2},{3,11},{11,3},{4,12},{12,4},... | collective-permute-start | bytes 2211848 | tf_op jit(solution)/shard_map/ppermute | solution.py:25
  268.0 26.1 %collective-permute-start.43 = (bf16[2,96,2048]{2,1,0:T(8,128)(2,1)S(1)}, bf16[2,96,2048]{2,1,0:T(8,128)(2,1)S(1)}, u32[]{:S(2)}, u32[]{:S(2)}) collective-permute-start(bf16[2,96,2048]{2,1,0:T(8,128)(2,1)S(1)} %pad_maximum_fusion.8), channel_id=1, source_target_pairs={{0,16},{16,0},{1,17},{17,1},{2,18},{18,2},{3,19},{19,3},{4,20},{20... | collective-permute-start | bytes 2359304 | tf_op jit(solution)/shard_map/ppermute | solution.py:25
  269.6 24.2 %collective-permute-start.44 = (bf16[384,384]{1,0:T(8,128)(2,1)S(1)}, bf16[384,384]{1,0:T(8,128)(2,1)S(1)}, u32[]{:S(2)}, u32[]{:S(2)}) collective-permute-start(bf16[384,384]{1,0:T(8,128)(2,1)S(1)} %copy-done.18), channel_id=1, source_target_pairs={{0,16},{16,0},{1,17},{17,1},{2,18},{18,2},{3,19},{19,3},{4,20},{20... | collective-permute-start | bytes 884744 | tf_op jit(solution)/shard_map/ppermute | solution.py:25
  270.1 23.6 %collective-permute-start.45 = (bf16[384,384]{1,0:T(8,128)(2,1)S(1)}, bf16[384,384]{1,0:T(8,128)(2,1)S(1)}, u32[]{:S(2)}, u32[]{:S(2)}) collective-permute-start(bf16[384,384]{1,0:T(8,128)(2,1)S(1)} %get-tuple-element.200), channel_id=1, source_target_pairs={{0,8},{8,0},{1,9},{9,1},{2,10},{10,2},{3,11},{11,3},{4,12},{12,4},... | collective-permute-start | bytes 884744 | tf_op jit(solution)/shard_map/ppermute | solution.py:25
  294.4 18.9 %collective-permute-start.49 = (bf16[96,1920]{1,0:T(8,128)(2,1)S(1)}, bf16[96,1920]{1,0:T(8,128)(2,1)S(1)}, u32[]{:S(2)}, u32[]{:S(2)}) collective-permute-start(bf16[96,1920]{1,0:T(8,128)(2,1)S(1)} %get-tuple-element.208), channel_id=1, source_target_pairs={{0,16},{16,0},{1,17},{17,1},{2,18},{18,2},{3,19},{19,3},{4,20},{20... | collective-permute-start | bytes 1105928 | tf_op jit(solution)/shard_map/ppermute | solution.py:25
  295.9 17.5 %collective-permute-start.50 = (bf16[96,2048]{1,0:T(8,128)(2,1)S(1)}, bf16[96,2048]{1,0:T(8,128)(2,1)S(1)}, u32[]{:S(2)}, u32[]{:S(2)}) collective-permute-start(bf16[96,2048]{1,0:T(8,128)(2,1)S(1)} %get-tuple-element.210), channel_id=1, source_target_pairs={{0,8},{8,0},{1,9},{9,1},{2,10},{10,2},{3,11},{11,3},{4,12},{12,4},... | collective-permute-start | bytes 1179656 | tf_op jit(solution)/shard_map/ppermute | solution.py:25
  296.5 14.0 %collective-permute-start.46 = (bf16[2,96,768]{2,1,0:T(8,128)(2,1)S(1)}, bf16[2,96,768]{2,1,0:T(8,128)(2,1)S(1)}, u32[]{:S(2)}, u32[]{:S(2)}) collective-permute-start(bf16[2,96,768]{2,1,0:T(8,128)(2,1)S(1)} %dynamic-slice_bitcast_fusion.1), channel_id=1, source_target_pairs={{0,2},{2,0},{4,6},{6,4},{1,3},{3,1},{5,7},{7,5},{8,10},{10,8},{12,... | collective-permute-start | bytes 884744 | tf_op jit(solution)/shard_map/ppermute | solution.py:25
  310.6 17.3 %collective-permute-start.48 = (bf16[1,96,768]{2,1,0:T(8,128)(2,1)S(1)}, bf16[1,96,768]{2,1,0:T(8,128)(2,1)S(1)}, u32[]{:S(2)}, u32[]{:S(2)}) collective-permute-start(bf16[1,96,768]{2,1,0:T(8,128)(2,1)S(1)} %constant_dynamic-slice_fusion.2), channel_id=1, source_target_pairs={{0,4},{2,6},{4,0},{6,2},{1,5},{3,7},{5,1},{7,3},{8,12},{10,14},{12... | collective-permute-start | bytes 442376 | tf_op jit(solution)/shard_map/ppermute | solution.py:25
  313.6 14.3 %collective-permute-start.51 = (bf16[2,24,3968]{2,1,0:T(8,128)(2,1)S(1)}, bf16[2,24,3968]{2,1,0:T(8,128)(2,1)S(1)}, u32[]{:S(2)}, u32[]{:S(2)}) collective-permute-start(bf16[2,24,3968]{2,1,0:T(8,128)(2,1)S(1)} %dynamic-slice_bitcast_fusion), channel_id=1, source_target_pairs={{0,2},{2,0},{4,6},{6,4},{1,3},{3,1},{5,7},{7,5},{8,10},{10,8},{12,... | collective-permute-start | bytes 1142792 | tf_op jit(solution)/shard_map/ppermute | solution.py:25
  317.6 50.0 %collective-permute-start.54 = (bf16[96,2304]{1,0:T(8,128)(2,1)S(1)}, bf16[96,2304]{1,0:T(8,128)(2,1)S(1)}, u32[]{:S(2)}, u32[]{:S(2)}) collective-permute-start(bf16[96,2304]{1,0:T(8,128)(2,1)S(1)} %get-tuple-element.308), channel_id=1, source_target_pairs={{0,24},{8,16},{16,8},{24,0},{1,25},{9,17},{17,9},{25,1},{2,26},{10... | collective-permute-start | bytes 1327112 | tf_op jit(solution)/shard_map/ppermute | solution.py:113
  319.2 48.4 %collective-permute-start.53 = (bf16[96,2304]{1,0:T(8,128)(2,1)S(1)}, bf16[96,2304]{1,0:T(8,128)(2,1)S(1)}, u32[]{:S(2)}, u32[]{:S(2)}) collective-permute-start(bf16[96,2304]{1,0:T(8,128)(2,1)S(1)} %get-tuple-element.309), channel_id=1, source_target_pairs={{0,16},{8,24},{16,0},{24,8},{1,17},{9,25},{17,1},{25,9},{2,18},{10... | collective-permute-start | bytes 1327112 | tf_op jit(solution)/shard_map/ppermute | solution.py:113
  320.6 47.0 %collective-permute-start.52 = (bf16[96,2304]{1,0:T(8,128)(2,1)S(1)}, bf16[96,2304]{1,0:T(8,128)(2,1)}, u32[]{:S(2)}, u32[]{:S(2)}) collective-permute-start(bf16[96,2304]{1,0:T(8,128)(2,1)S(1)} %get-tuple-element.310), channel_id=1, source_target_pairs={{0,8},{8,0},{16,24},{24,16},{1,9},{9,1},{17,25},{25,17},{2,10},{10... | collective-permute-start | bytes 1327112 | tf_op jit(solution)/shard_map/ppermute | solution.py:113
  328.1 23.3 %collective-permute-start.58 = (bf16[1,96,768]{2,1,0:T(8,128)(2,1)S(1)}, bf16[1,96,768]{2,1,0:T(8,128)(2,1)S(1)}, u32[]{:S(2)}, u32[]{:S(2)}) collective-permute-start(bf16[1,96,768]{2,1,0:T(8,128)(2,1)S(1)} %add_convert_fusion.26), channel_id=1, source_target_pairs={{0,4},{2,6},{4,0},{6,2},{1,5},{3,7},{5,1},{7,3},{8,12},{10,14},{12... | collective-permute-start | bytes 442376 | tf_op jit(solution)/shard_map/ppermute | solution.py:25
  346.4 11.5 %collective-permute-start.56 = (bf16[1,24,3968]{2,1,0:T(8,128)(2,1)S(1)}, bf16[1,24,3968]{2,1,0:T(8,128)(2,1)S(1)}, u32[]{:S(2)}, u32[]{:S(2)}) collective-permute-start(bf16[1,24,3968]{2,1,0:T(8,128)(2,1)S(1)} %constant_dynamic-slice_fusion.1), channel_id=1, source_target_pairs={{0,4},{2,6},{4,0},{6,2},{1,5},{3,7},{5,1},{7,3},{8,12},{10,14},{12... | collective-permute-start | bytes 571400 | tf_op jit(solution)/shard_map/ppermute | solution.py:25
  358.1 12.7 %collective-permute-start.59 = (bf16[2,96,768]{2,1,0:T(8,128)(2,1)S(1)}, bf16[2,96,768]{2,1,0:T(8,128)(2,1)S(1)}, u32[]{:S(2)}, u32[]{:S(2)}) collective-permute-start(bf16[2,96,768]{2,1,0:T(8,128)(2,1)S(1)} %maximum_bitcast_fusion.7), channel_id=1, source_target_pairs={{0,2},{2,0},{4,6},{6,4},{1,3},{3,1},{5,7},{7,5},{8,10},{10,8},{12,... | collective-permute-start | bytes 884744 | tf_op jit(solution)/shard_map/ppermute | solution.py:25
  384.6 12.8 %collective-permute-start.62 = (bf16[2,24,3968]{2,1,0:T(8,128)(2,1)S(1)}, bf16[2,24,3968]{2,1,0:T(8,128)(2,1)S(1)}, u32[]{:S(2)}, u32[]{:S(2)}) collective-permute-start(bf16[2,24,3968]{2,1,0:T(8,128)(2,1)S(1)} %maximum_bitcast_fusion.2), channel_id=1, source_target_pairs={{0,2},{2,0},{4,6},{6,4},{1,3},{3,1},{5,7},{7,5},{8,10},{10,8},{12,... | collective-permute-start | bytes 1142792 | tf_op jit(solution)/shard_map/ppermute | solution.py:25
  (77 other events, 633.5 us)
Sparse Core Ops, SparseCore 0:
  24.5 76.9 all-gather.5
  106.3 39.0 all-gather.7
  258.8 49.4 all-gather.9

commit v3 on v2

--- a/solution.py
+++ b/solution.py
@@ -165,33 +165,33 @@
     def chip(self):
         count = lax.axis_size("y") * lax.axis_size("x")
 
-        def some(blocks, right):
+        def some(blocks, lower):
             out = []
             for d in blocks:
                 cuts = []
                 for mine, got in self.parts:
-                    half = (mine.shape[-1] // 256) * 128
-                    cut = slice(half, None) if right else slice(None, half)
                     mine = mine.reshape((count, -1) + mine.shape[-1:])
                     got = got.reshape(mine.shape)
-                    cuts.append(add(mine[d][:, cut], got[d][:, cut]))
+                    half = mine.shape[1] // 2
+                    cut = slice(half, None) if lower else slice(None, half)
+                    cuts.append(add(mine[d, cut], got[d, cut]))
                 out.append(jnp.concatenate(cuts, axis=-1))
             return jnp.stack(out)
 
         self.state = some((0, 2), False), some((1, 3), False), some((0, 1), True), some((2, 3), True)
 
     def plane_first(self, *then):
-        keep_left, send_left, keep_right, send_right = self.state
-        got_left, got_right = swap(send_left, "x", 1, then), swap(send_right, "y", 1, then)
+        keep_upper, send_upper, keep_lower, send_lower = self.state
+        got_upper, got_lower = swap(send_upper, "x", 1, then), swap(send_lower, "y", 1, then)
         self.state = (
-            add(keep_left[0], got_left[0]), add(keep_left[1], got_left[1]),
-            add(keep_right[0], got_right[0]), add(keep_right[1], got_right[1]),
+            add(keep_upper[0], got_upper[0]), add(keep_upper[1], got_upper[1]),
+            add(keep_lower[0], got_lower[0]), add(keep_lower[1], got_lower[1]),
         )
 
     def plane_second(self, *then):
-        keep_left, send_left, keep_right, send_right = self.state
-        got_left, got_right = swap(send_left, "y", 1, then), swap(send_right, "x", 1, then)
-        plane = jnp.concatenate([add(keep_left, got_left), add(keep_right, got_right)], axis=-1)
+        keep_upper, send_upper, keep_lower, send_lower = self.state
+        got_upper, got_lower = swap(send_upper, "y", 1, then), swap(send_lower, "x", 1, then)
+        plane = jnp.concatenate([add(keep_upper, got_upper), add(keep_lower, got_lower)], axis=0)
         zsize = lax.axis_size("z")
         self.state = plane.reshape(zsize, plane.shape[0] // zsize, plane.shape[1])
 
@@ -222,15 +222,6 @@
         mine = self.state.reshape(-1, self.state.shape[-1])
         both = join(mine, swap(mine, "c", 1, then), lax.axis_index("c"), 0)
         self.state = both.reshape(-1, both.shape[-1])
-
-
-def ungroup(reduced, sizes):
-    halves = [(size // 256) * 128 for size in sizes]
-    left, right, arrays = 0, sum(halves), []
-    for size, half in zip(sizes, halves, strict=True):
-        arrays.append(jnp.concatenate([reduced[:, left : left + half], reduced[:, right : right + size - half]], axis=-1))
-        left, right = left + half, right + size - half
-    return arrays
 
 
 def product(left_op, right_op, einsum_form):
@@ -845,17 +836,19 @@
     return jnp.concatenate(list(parts.values()), axis=-1), ends
 
 
-def cross_grads(docs, ends):
+def cross_grads(docs, ends, names):
     flat = docs.reshape(-1, docs.shape[-1])
-    cut = {name: flat[:, a:b] for name, (a, b) in ends.items()}
-    g_qkv = product(cut["own_in"], cut["packed"], "rd,re->de")
-    g_out = product(cut["mixed"], cut["attended"], "rd,re->de")
-    g_up = product(cut["own_low"], cut["inner"], "rd,re->de")
-    g_down = product(cut["act"], cut["outer"], "rd,re->de")
-    part_of = {name: docs[:, :, ends[name][0] : ends[name][1]].astype(f32) for name in ("own_grad", "sums")}
-    g_pos = jnp.sum(part_of["own_grad"], axis=0)
-    g_sums = jnp.sum(part_of["sums"][:, :4], axis=0)
-    return g_qkv, g_out, g_up, g_down, g_sums[0:2], g_sums[2:4], g_pos
+
+    def cut(name):
+        return flat[:, slice(*ends[name])]
+
+    pairs = {"qkv": ("own_in", "packed"), "out": ("mixed", "attended"), "up": ("own_low", "inner"), "down": ("act", "outer")}
+    grads = {k: product(cut(pairs[k][0]), cut(pairs[k][1]), "rd,re->de") for k in names if k in pairs}
+    if "rest" in names:
+        grads["positions"] = jnp.sum(docs[:, :, slice(*ends["own_grad"])].astype(f32), axis=0)
+        sums = jnp.sum(docs[:, :4, slice(*ends["sums"])].astype(f32), axis=0)
+        grads["gains"], grads["biases"] = sums[0:2], sums[2:4]
+    return grads
 
 
 def per_device(
@@ -957,39 +950,41 @@
     red_up.after(red_qkv.state, red_down.state)
     red_down.after(red_up.state)
     token_grad = token_grad_call(tie(resid, red_qkv.state, red_down.state, red_up.state), grad_packed, w_first)
-    red_down.back_far(token_grad)
-    red_up.far_z(token_grad)
-    others = cross_grads(tie(docs, token_grad), ends)
-    red_qkv.plane_direct(token_grad)
-    red_down.back_near()
-    red_up.back_far()
-
-    def step(*moves):
-        states = lax.optimization_barrier([r.state for r in (red_qkv, red_up, red_down)])
-        for r, state in zip((red_qkv, red_up, red_down), states, strict=True):
-            r.state = state
-        for move in moves:
-            move()
-
+    others = cross_grads(tie(docs, token_grad), ends, ("up", "qkv"))
+    red_qkv.plane_direct(token_grad, others)
+    lead = red_qkv.state
+    others |= cross_grads(tie(docs, lead), ends, ("down", "out", "rest"))
+    red_down.back_far(token_grad, lead)
+    red_up.far_z(token_grad, lead)
     red_qkv.near_z()
-    step(red_qkv.far_z, red_up.back_near, red_down.back_core)
+    lead = red_qkv.state
+    red_down.back_near(lead)
+    red_up.back_far(lead)
+    red_qkv.far_z()
+    lead = red_qkv.state
+    red_down.back_core(lead)
+    red_up.back_near(lead)
     red_qkv.back_far()
-    step(red_qkv.back_near, red_up.back_core)
-    done_out, done_up = ungroup(red_up.state.astype(f32), (width + 128, ff))
+    lead = red_qkv.state
+    red_up.back_core(lead)
     done_down = red_down.state.astype(f32)
-    red_qkv.back_core(layer_out, done_out, done_up, done_down)
+    red_qkv.back_near()
+    red_qkv.after(done_down, layer_out, others)
+    red_qkv.back_core()
+    done_up = red_up.state.astype(f32)
     done_qkv = red_qkv.state.astype(f32)
-    small_grads = done_out[:, width : width + 4].T
+    pick = (jnp.arange(128)[None, :] == jnp.arange(4)[:, None]).astype(bf16)
+    small_grads = product(pick, red_up.state[:, width : width + 128], "kc,rc->kr")
     return (
         layer_out.reshape(tokens.shape),
         token_grad.reshape(tokens.shape),
         done_qkv,
-        done_out[:, :width],
-        done_up,
+        done_up[:, :width],
+        done_up[:, width + 128 :],
         done_down,
         small_grads[0:2],
         small_grads[2:4],
-    ) + others
+    ) + tuple(others[k] for k in ("qkv", "out", "up", "down", "gains", "biases", "positions"))
 
 
 def solution(mesh):

time: 432 us -> 418 us (0.968)
  waiting for transfers between devices: 140 us -> 127 us
  other arithmetic: 35 us -> 29.5 us
    ppermute x43, waiting for transfers between devices: 122 us -> 109 us  [swap(): got = lax.ppermute(value, axis, [(i, i ^ bit) for i in range(size)])]
    dot_general x18 -> x19, matrix products: 18.1 us -> 18.2 us  [product(): jnp.einsum(einsum_form, left_op, right_op, preferred_element_type=f32)]
  transfers between devices with their start and end apart: 70 -> 70, of which waited for: 45 -> 43; matrix products, arithmetic and copies ran while one was open for 12% -> 9% of each run, Pallas kernels for 28% -> 29%
where the time goes in v3:
time: 418 us; the launch traced here: 411 us
  Pallas kernels  129 us (31%)
  waiting for transfers between devices  127 us (30%)
  starting transfers between devices  70.3 us (17%)
  other arithmetic  29.5 us (7%)
  local copies, waits for them, and re-layouts  21.4 us (5%)
  matrix products  18.2 us (4%)
  between operations  15.4 us (4%)
    ppermute x43, waiting for transfers between devices, swap(): got = lax.ppermute(value, axis, [(i, i ^ bit) for i in range(size)])  109 us
    ppermute x43, starting transfers between devices, swap(): got = lax.ppermute(value, axis, [(i, i ^ bit) for i in range(size)])  41.7 us
    ppermute x24, starting transfers between devices, swap_f(): got = lax.ppermute(value, ('y', 'x'), [(i, i ^ dist) for i in range(count)])  28.2 us
    pallas_call x3, Pallas kernels, row_blocks_call(): pl.pallas_call(functools.partial(row_blocks_kernel, count=count), grid_sp...  24.4 us
    pallas_call x1, Pallas kernels, finish_call(): pl.pallas_call(functools.partial(finish_kernel, tile=tile, seg=total // g...  23.8 us
    pallas_call x1, Pallas kernels, finish_back_call(): pl.pallas_call(functools.partial(finish_back_kernel, tile=tile, seg=total...  23.5 us
    dot_general x19, matrix products, product(): jnp.einsum(einsum_form, left_op, right_op, preferred_element_type=f32)  18.2 us
    pallas_call x1, Pallas kernels, attend_back_call(): pl.pallas_call(functools.partial(attend_back_kernel, seg=total // counts....  17.9 us
  transfers between devices with their start and end apart: 70, of which 43 were waited for; matrix products, arithmetic and copies ran while one was open for 9% of the time, Pallas kernels for 29%

profile of v3, /device:TPU:0, one launch (start us, length us, event | category | flops | bytes accessed | tf_op | source)
XLA Modules:
  0.0 410.6 jit_solution(8566048661927447357)
XLA Ops:
  12.9 4.0 collective-permute-start.1
  16.9 7.3 %collective-permute-done.1 = bf16[1,48,1536]{2,1,0:T(8,128)(2,1)S(1)} collective-permute-done((bf16[1,48,1536]{2,1,0:T(8,128)(2,1)S(1)}, bf16[1,48,1536]{2,1,0:T(8,128)(2,1)S(1)}, u32[]{:S(2)}, u32[]{:S(2)}) %collective-permute-start.1) | collective-permute-done | bytes 147488 | tf_op jit(solution)/shard_map/ppermute | solution.py:25
  25.7 8.2 %collective-permute-done.2 = bf16[2,48,1536]{2,1,0:T(8,128)(2,1)S(1)} collective-permute-done((bf16[2,48,1536]{2,1,0:T(8,128)(2,1)S(1)}, bf16[2,48,1536]{2,1,0:T(8,128)(2,1)S(1)}, u32[]{:S(2)}, u32[]{:S(2)}) %collective-permute-start.2) | collective-permute-done | bytes 294944 | tf_op jit(solution)/shard_map/ppermute | solution.py:25
  47.7 3.7 collective-permute-done.5
  57.4 6.2 %collective-permute-done.12 = bf16[2,192,384]{2,1,0:T(8,128)(2,1)S(1)} collective-permute-done((bf16[2,192,384]{2,1,0:T(8,128)(2,1)S(1)}, bf16[2,192,384]{2,1,0:T(8,128)(2,1)S(1)}, u32[]{:S(2)}, u32[]{:S(2)}) %collective-permute-start.12) | collective-permute-done | bytes 294944 | tf_op jit(solution)/shard_map/ppermute | solution.py:25
  63.8 6.4 %collective-permute-done.10 = bf16[2,2,48,1536]{3,2,1,0:T(8,128)(2,1)S(1)} collective-permute-done((bf16[2,2,48,1536]{3,2,1,0:T(8,128)(2,1)S(1)}, bf16[2,2,48,1536]{3,2,1,0:T(8,128)(2,1)S(1)}, u32[]{:S(2)}, u32[]{:S(2)}) %collective-permute-start.10) | collective-permute-done | bytes 589856 | tf_op jit(solution)/shard_map/ppermute | solution.py:25
  78.3 9.7 %collective-permute-done.15 = bf16[2,192,384]{2,1,0:T(8,128)(2,1)S(1)} collective-permute-done((bf16[2,192,384]{2,1,0:T(8,128)(2,1)S(1)}, bf16[2,192,384]{2,1,0:T(8,128)(2,1)S(1)}, u32[]{:S(2)}, u32[]{:S(2)}) %collective-permute-start.15) | collective-permute-done | bytes 294944 | tf_op jit(solution)/shard_map/ppermute | solution.py:25
  91.0 12.6 %attend.1 = (bf16[1024,2304]{1,0:T(8,128)(2,1)}, bf16[1024,768]{1,0:T(8,128)(2,1)}) custom-call(s32[8]{0:T(128)} %bitcast.407, bf16[1024,768]{1,0:T(8,128)(2,1)} %bitcast.402, bf16[768,3072]{1,0:T(8,128)(2,1)} %copy-done), custom_call_target="tpu_custom_call" | custom-call | flops 4831838208 | bytes 16777216 | tf_op jit(solution)/shard_map/attend/pallas_call | solution.py:348
  111.2 3.1 pad_maximum_fusion.1
  116.8 23.8 %finish.1 = (f32[1024,768]{1,0:T(8,128)}, f32[1024,768]{1,0:T(8,128)}, bf16[1024,3072]{1,0:T(8,128)(2,1)}, bf16[1024,3072]{1,0:T(8,128)(2,1)}, bf16[1024,768]{1,0:T(8,128)(2,1)}, /*index=5*/f32[8,768]{1,0:T(8,128)}) custom-call(s32[8]{0:T(128)} %bitcast.408, bf16[1024,768]{1,0:T(8,128)(2,1)} %bitcast.403, ...), custom_call_target="tpu_custom_call" | custom-call | flops 10871635968 | bytes 41943040 | tf_op jit(solution)/shard_map/finish/pallas_call | solution.py:502
  145.4 4.8 %unpack.1 = (bf16[768,576]{1,0:T(8,128)(2,1)}, bf16[192,768]{1,0:T(8,128)(2,1)}, bf16[768,768]{1,0:T(8,128)(2,1)}, bf16[768,768]{1,0:T(8,128)(2,1)}) custom-call(bf16[8,96,2304]{2,1,0:T(8,128)(2,1)} %bitcast.372), custom_call_target="tpu_custom_call" | custom-call | tf_op jit(solution)/shard_map/unpack/pallas_call | solution.py:752
  175.6 2.7 collective-permute-done.30
  197.1 23.5 %finish_back.1 = (bf16[1024,768]{1,0:T(8,128)(2,1)}, bf16[1024,3072]{1,0:T(8,128)(2,1)}, f32[1024,768]{1,0:T(8,128)}, bf16[1024,768]{1,0:T(8,128)(2,1)}, bf16[10...) custom-call(s32[8]{0:T(128)} %bitcast.409, bf16[1024,768]{1,0:T(8,128)(2,1)} %bitcast.401, ...), custom_call_target="tpu_custom_call" | custom-call | flops 10871635968 | bytes 41943040 | tf_op jit(solution)/shard_map/finish_back/pallas_call | solution.py:574
  228.2 9.4 %wide_blocks.1 = (bf16[4,384,768]{2,1,0:T(8,128)(2,1)}, bf16[4,384,768]{2,1,0:T(8,128)(2,1)}) custom-call(s32[2]{0:T(128)} %pad_add_fusion.ids_ref, bf16[1024,768]{1,0:T(8,128)(2,1)} %get-tuple-element.177.a_ref, bf16[1024,3072]{1,0:T(8,128)(2,1)} %get-tuple-element.178.b_ref), custom_call_target="tpu_custom_call" | custom-call | flops 9663676416 | bytes 16777216 | tf_op jit(solution)/shard_map/wide_blocks/pallas_call | solution.py:680
  237.6 5.7 %row_blocks.3 = (bf16[384,896]{1,0:T(8,128)(2,1)}, bf16[384,896]{1,0:T(8,128)(2,1)}) custom-call(s32[2]{0:T(128)} %pad_add_fusion.ids_ref, bf16[1024,768]{1,0:T(8,128)(2,1)} %get-tuple-element.181.mixed_ref.a_ref, bf16[1024,768]{1,0:T(8,128)(2,1)} %get-tuple-element.182.b_ref, f32[16,768]{1,0:T(8,128)} %get-tuple-element.183.refs_0_), custom_call_target="tpu_custom_call" | custom-call | flops 2415919104 | bytes 16777216 | tf_op jit(solution)/shard_map/row_blocks/pallas_call | solution.py:648
  245.9 10.2 %row_blocks.4 = (bf16[384,3072]{1,0:T(8,128)(2,1)}, bf16[384,3072]{1,0:T(8,128)(2,1)}) custom-call(s32[2]{0:T(128)} %pad_add_fusion.ids_ref, bf16[1024,768]{1,0:T(8,128)(2,1)} %get-tuple-element.188.a_ref, bf16[1024,3072]{1,0:T(8,128)(2,1)} %get-tuple-element.189.b_ref), custom_call_target="tpu_custom_call" | custom-call | flops 9663676416 | bytes 16777216 | tf_op jit(solution)/shard_map/row_blocks/pallas_call | solution.py:648
  256.0 3.4 collective-permute-done.39
  264.3 3.5 collective-permute-done.37
  276.7 17.9 %attend_back.1.b_ref.g_ref = bf16[1024,2304]{1,0:T(8,128)(2,1)} custom-call(s32[8]{0:T(128)} %bitcast.410, bf16[1024,2304]{1,0:T(8,128)(2,1)} %get-tuple-element.149.packed_ref, bf16[1024,768]{1,0:T(8,128)(2,1)} %get-tuple-element.201.grad_ref), custom_call_target="tpu_custom_call" | custom-call | flops 9663676416 | bytes 16777216 | tf_op jit(solution)/shard_map/attend_back/pallas_call | solution.py:401
  294.6 3.6 collective-permute-done.44
  301.2 8.5 %row_blocks.5 = (bf16[384,2304]{1,0:T(8,128)(2,1)}, bf16[384,2304]{1,0:T(8,128)(2,1)}) custom-call(s32[2]{0:T(128)} %pad_add_fusion.ids_ref, bf16[1024,768]{1,0:T(8,128)(2,1)} %bitcast.404, bf16[1024,2304]{1,0:T(8,128)(2,1)} %attend_back.1.b_ref.g_ref), custom_call_target="tpu_custom_call" | custom-call | flops 7247757312 | bytes 16777216 | tf_op jit(solution)/shard_map/row_blocks/pallas_call | solution.py:648
  309.7 6.4 %collective-permute-done.46 = bf16[2,96,768]{2,1,0:T(8,128)(2,1)S(1)} collective-permute-done((bf16[2,96,768]{2,1,0:T(8,128)(2,1)S(1)}, bf16[2,96,768]{2,1,0:T(8,128)(2,1)S(1)}, u32[]{:S(2)}, u32[]{:S(2)}) %collective-permute-start.46) | collective-permute-done | bytes 294944 | tf_op jit(solution)/shard_map/ppermute | solution.py:25
  325.6 6.8 %collective-permute-done.51 = bf16[2,24,3968]{2,1,0:T(8,128)(2,1)S(1)} collective-permute-done((bf16[2,24,3968]{2,1,0:T(8,128)(2,1)S(1)}, bf16[2,24,3968]{2,1,0:T(8,128)(2,1)S(1)}, u32[]{:S(2)}, u32[]{:S(2)}) %collective-permute-start.51) | collective-permute-done | bytes 380960 | tf_op jit(solution)/shard_map/ppermute | solution.py:25
  332.6 8.7 %token_grad.1 = bf16[1024,768]{1,0:T(8,128)(2,1)} custom-call(f32[1024,768]{1,0:T(8,128)} %get-tuple-element.223.resid_ref, bf16[1024,2304]{1,0:T(8,128)(2,1)} %attend_back.1.b_ref.g_ref, bf16[768,3072]{1,0:T(8,128)(2,1)} %copy-done), custom_call_target="tpu_custom_call" | custom-call | flops 7247757312 | bytes 16777216 | tf_op jit(solution)/shard_map/token_grad/pallas_call | solution.py:701
  341.4 3.0 collective-permute-start.63
  344.3 3.0 fusion.2
  347.3 3.4 fusion
  352.0 3.0 fusion.20
  362.5 9.6 %collective-permute-done.55 = bf16[2,24,2304]{2,1,0:T(8,128)(2,1)S(1)} collective-permute-done((bf16[2,24,2304]{2,1,0:T(8,128)(2,1)S(1)}, bf16[2,24,2304]{2,1,0:T(8,128)(2,1)S(1)}, u32[]{:S(2)}, u32[]{:S(2)}) %collective-permute-start.55) | collective-permute-done | bytes 221216 | tf_op jit(solution)/shard_map/ppermute | solution.py:25
  375.3 6.7 %collective-permute-done.60 = bf16[2,96,768]{2,1,0:T(8,128)(2,1)S(1)} collective-permute-done((bf16[2,96,768]{2,1,0:T(8,128)(2,1)S(1)}, bf16[2,96,768]{2,1,0:T(8,128)(2,1)S(1)}, u32[]{:S(2)}, u32[]{:S(2)}) %collective-permute-start.60) | collective-permute-done | bytes 294944 | tf_op jit(solution)/shard_map/ppermute | solution.py:25
  382.6 5.8 %collective-permute-done.57 = bf16[1,24,2304]{2,1,0:T(8,128)(2,1)S(1)} collective-permute-done((bf16[1,24,2304]{2,1,0:T(8,128)(2,1)S(1)}, bf16[1,24,2304]{2,1,0:T(8,128)(2,1)S(1)}, u32[]{:S(2)}, u32[]{:S(2)}) %collective-permute-start.57) | collective-permute-done | bytes 110624 | tf_op jit(solution)/shard_map/ppermute | solution.py:25
  390.6 3.9 collective-permute-done.58
  (398 shorter events, 156.6 us)
Async XLA Ops:
  7.2 99.0 %all-gather.6.cloned.1.call-start = ((), (), s32[]{:S(2)}) async-start(), calls=%async_computation | async-start | bytes 5068800 | tf_op jit(solution)/shard_map/all_gather | solution.py:875
  24.4 121.0 %all-gather.8.cloned.1.call-start = ((), (), s32[]{:S(2)}) async-start(), calls=%async_computation.1 | async-start | bytes 3981312 | tf_op jit(solution)/shard_map/all_gather | solution.py:899
  35.0 12.6 %collective-permute-start.6 = (bf16[1,192,384]{2,1,0:T(8,128)(2,1)S(1)}, bf16[1,192,384]{2,1,0:T(8,128)(2,1)S(1)}, u32[]{:S(2)}, u32[]{:S(2)}) collective-permute-start(bf16[1,192,384]{2,1,0:T(8,128)(2,1)S(1)} %bitcast.390), channel_id=1, source_target_pairs={{0,4},{2,6},{4,0},{6,2},{1,5},{3,7},{5,1},{7,3},{8,12},{10,14},{12... | collective-permute-start | bytes 442376 | tf_op jit(solution)/shard_map/ppermute | solution.py:25
  55.1 15.1 %collective-permute-start.10 = (bf16[2,2,48,1536]{3,2,1,0:T(8,128)(2,1)S(1)}, bf16[2,2,48,1536]{3,2,1,0:T(8,128)(2,1)S(1)}, u32[]{:S(2)}, u32[]{:S(2)}) collective-permute-start(bf16[2,2,48,1536]{3,2,1,0:T(8,128)(2,1)S(1)} %get-tuple-element.141), channel_id=1, source_target_pairs={{0,16},{16,0},{1,17},{17,1},{2,18},{18,2},{3,19},{19,3},{4,20},{20... | collective-permute-start | bytes 1769480 | tf_op jit(solution)/shard_map/ppermute | solution.py:25
  56.6 15.8 %collective-permute-start.11 = (bf16[2,2,48,1536]{3,2,1,0:T(8,128)(2,1)S(1)}, bf16[2,2,48,1536]{3,2,1,0:T(8,128)(2,1)S(1)}, u32[]{:S(2)}, u32[]{:S(2)}) collective-permute-start(bf16[2,2,48,1536]{3,2,1,0:T(8,128)(2,1)S(1)} %get-tuple-element.142), channel_id=1, source_target_pairs={{0,8},{8,0},{1,9},{9,1},{2,10},{10,2},{3,11},{11,3},{4,12},{12,4},... | collective-permute-start | bytes 1769480 | tf_op jit(solution)/shard_map/ppermute | solution.py:25
  72.9 15.2 %collective-permute-start.15 = (bf16[2,192,384]{2,1,0:T(8,128)(2,1)S(1)}, bf16[2,192,384]{2,1,0:T(8,128)(2,1)S(1)}, u32[]{:S(2)}, u32[]{:S(2)}) collective-permute-start(bf16[2,192,384]{2,1,0:T(8,128)(2,1)S(1)} %get-tuple-element.317), channel_id=1, source_target_pairs={{0,16},{16,0},{1,17},{17,1},{2,18},{18,2},{3,19},{19,3},{4,20},{20... | collective-permute-start | bytes 884744 | tf_op jit(solution)/shard_map/ppermute | solution.py:25
  74.4 15.5 %collective-permute-start.14 = (bf16[2,192,384]{2,1,0:T(8,128)(2,1)S(1)}, bf16[2,192,384]{2,1,0:T(8,128)(2,1)S(1)}, u32[]{:S(2)}, u32[]{:S(2)}) collective-permute-start(bf16[2,192,384]{2,1,0:T(8,128)(2,1)S(1)} %get-tuple-element.318), channel_id=1, source_target_pairs={{0,8},{8,0},{1,9},{9,1},{2,10},{10,2},{3,11},{11,3},{4,12},{12,4},... | collective-permute-start | bytes 884744 | tf_op jit(solution)/shard_map/ppermute | solution.py:25
  90.2 15.2 %collective-permute-start.17 = (bf16[2,2,192,384]{3,2,1,0:T(8,128)(2,1)S(1)}, bf16[2,2,192,384]{3,2,1,0:T(8,128)(2,1)S(1)}, u32[]{:S(2)}, u32[]{:S(2)}) collective-permute-start(bf16[2,2,192,384]{3,2,1,0:T(8,128)(2,1)S(1)} %pad_maximum_fusion.16), channel_id=1, source_target_pairs={{0,8},{8,0},{1,9},{9,1},{2,10},{10,2},{3,11},{11,3},{4,12},{12,4},... | collective-permute-start | bytes 1769480 | tf_op jit(solution)/shard_map/ppermute | solution.py:25
  90.9 14.6 %collective-permute-start.16 = (bf16[2,2,192,384]{3,2,1,0:T(8,128)(2,1)S(1)}, bf16[2,2,192,384]{3,2,1,0:T(8,128)(2,1)S(1)}, u32[]{:S(2)}, u32[]{:S(2)}) collective-permute-start(bf16[2,2,192,384]{3,2,1,0:T(8,128)(2,1)S(1)} %pad_maximum_fusion.15), channel_id=1, source_target_pairs={{0,16},{16,0},{1,17},{17,1},{2,18},{18,2},{3,19},{19,3},{4,20},{20... | collective-permute-start | bytes 1769480 | tf_op jit(solution)/shard_map/ppermute | solution.py:25
  106.2 235.2 %all-gather.10.cloned.1.call-start = ((), (), s32[]{:S(2)}) async-start(), calls=%async_computation.2 | async-start | bytes 5160960 | tf_op jit(solution)/shard_map/all_gather | solution.py:926
  193.6 27.1 %collective-permute-start.35 = (bf16[32,1344]{1,0:T(8,128)(2,1)S(1)}, bf16[32,1344]{1,0:T(8,128)(2,1)S(1)}, u32[]{:S(2)}, u32[]{:S(2)}) collective-permute-start(bf16[32,1344]{1,0:T(8,128)(2,1)S(1)} %concatenate.91), channel_id=1, source_target_pairs={{0,16},{8,24},{16,0},{24,8},{1,17},{9,25},{17,1},{25,9},{2,18},{10... | collective-permute-start | bytes 258056 | tf_op jit(solution)/shard_map/ppermute | solution.py:113
  195.1 25.6 %collective-permute-start.36 = (bf16[32,1344]{1,0:T(8,128)(2,1)S(1)}, bf16[32,1344]{1,0:T(8,128)(2,1)S(1)}, u32[]{:S(2)}, u32[]{:S(2)}) collective-permute-start(bf16[32,1344]{1,0:T(8,128)(2,1)S(1)} %concatenate.91), channel_id=1, source_target_pairs={{0,24},{8,16},{16,8},{24,0},{1,25},{9,17},{17,9},{25,1},{2,26},{10... | collective-permute-start | bytes 258056 | tf_op jit(solution)/shard_map/ppermute | solution.py:113
  196.6 24.2 %collective-permute-start.34 = (bf16[32,1344]{1,0:T(8,128)(2,1)S(1)}, bf16[32,1344]{1,0:T(8,128)(2,1)S(1)}, u32[]{:S(2)}, u32[]{:S(2)}) collective-permute-start(bf16[32,1344]{1,0:T(8,128)(2,1)S(1)} %concatenate.91), channel_id=1, source_target_pairs={{0,8},{8,0},{16,24},{24,16},{1,9},{9,1},{17,25},{25,17},{2,10},{10... | collective-permute-start | bytes 258056 | tf_op jit(solution)/shard_map/ppermute | solution.py:113
  243.6 15.8 %collective-permute-start.39 = (bf16[2,192,768]{2,1,0:T(8,128)(2,1)S(1)}, bf16[2,192,768]{2,1,0:T(8,128)(2,1)S(1)}, u32[]{:S(2)}, u32[]{:S(2)}) collective-permute-start(bf16[2,192,768]{2,1,0:T(8,128)(2,1)S(1)} %pad_maximum_fusion.17), channel_id=1, source_target_pairs={{0,8},{8,0},{1,9},{9,1},{2,10},{10,2},{3,11},{11,3},{4,12},{12,4},... | collective-permute-start | bytes 1769480 | tf_op jit(solution)/shard_map/ppermute | solution.py:25
  245.2 15.5 %collective-permute-start.40 = (bf16[2,192,768]{2,1,0:T(8,128)(2,1)S(1)}, bf16[2,192,768]{2,1,0:T(8,128)(2,1)S(1)}, u32[]{:S(2)}, u32[]{:S(2)}) collective-permute-start(bf16[2,192,768]{2,1,0:T(8,128)(2,1)S(1)} %pad_maximum_fusion.18), channel_id=1, source_target_pairs={{0,16},{16,0},{1,17},{17,1},{2,18},{18,2},{3,19},{19,3},{4,20},{20... | collective-permute-start | bytes 1769480 | tf_op jit(solution)/shard_map/ppermute | solution.py:25
  272.3 26.1 %collective-permute-start.42 = (bf16[2,48,3968]{2,1,0:T(8,128)(2,1)S(1)}, bf16[2,48,3968]{2,1,0:T(8,128)(2,1)S(1)}, u32[]{:S(2)}, u32[]{:S(2)}) collective-permute-start(bf16[2,48,3968]{2,1,0:T(8,128)(2,1)S(1)} %pad_maximum_fusion.6), channel_id=1, source_target_pairs={{0,8},{8,0},{1,9},{9,1},{2,10},{10,2},{3,11},{11,3},{4,12},{12,4},... | collective-permute-start | bytes 2285576 | tf_op jit(solution)/shard_map/ppermute | solution.py:25
  273.0 25.6 %collective-permute-start.43 = (bf16[2,48,3968]{2,1,0:T(8,128)(2,1)S(1)}, bf16[2,48,3968]{2,1,0:T(8,128)(2,1)S(1)}, u32[]{:S(2)}, u32[]{:S(2)}) collective-permute-start(bf16[2,48,3968]{2,1,0:T(8,128)(2,1)S(1)} %pad_maximum_fusion.8), channel_id=1, source_target_pairs={{0,16},{16,0},{1,17},{17,1},{2,18},{18,2},{3,19},{19,3},{4,20},{20... | collective-permute-start | bytes 2285576 | tf_op jit(solution)/shard_map/ppermute | solution.py:25
  274.5 23.6 %collective-permute-start.44 = (bf16[192,768]{1,0:T(8,128)(2,1)S(1)}, bf16[192,768]{1,0:T(8,128)(2,1)S(1)}, u32[]{:S(2)}, u32[]{:S(2)}) collective-permute-start(bf16[192,768]{1,0:T(8,128)(2,1)S(1)} %copy-done.16), channel_id=1, source_target_pairs={{0,16},{16,0},{1,17},{17,1},{2,18},{18,2},{3,19},{19,3},{4,20},{20... | collective-permute-start | bytes 884744 | tf_op jit(solution)/shard_map/ppermute | solution.py:25
  275.1 23.1 %collective-permute-start.45 = (bf16[192,768]{1,0:T(8,128)(2,1)S(1)}, bf16[192,768]{1,0:T(8,128)(2,1)S(1)}, u32[]{:S(2)}, u32[]{:S(2)}) collective-permute-start(bf16[192,768]{1,0:T(8,128)(2,1)S(1)} %copy-done.15), channel_id=1, source_target_pairs={{0,8},{8,0},{1,9},{9,1},{2,10},{10,2},{3,11},{11,3},{4,12},{12,4},... | collective-permute-start | bytes 884744 | tf_op jit(solution)/shard_map/ppermute | solution.py:25
  298.8 18.9 %collective-permute-start.49 = (bf16[48,3968]{1,0:T(8,128)(2,1)S(1)}, bf16[48,3968]{1,0:T(8,128)(2,1)S(1)}, u32[]{:S(2)}, u32[]{:S(2)}) collective-permute-start(bf16[48,3968]{1,0:T(8,128)(2,1)S(1)} %get-tuple-element.208), channel_id=1, source_target_pairs={{0,16},{16,0},{1,17},{17,1},{2,18},{18,2},{3,19},{19,3},{4,20},{20... | collective-permute-start | bytes 1142792 | tf_op jit(solution)/shard_map/ppermute | solution.py:25
  300.3 17.3 %collective-permute-start.50 = (bf16[48,3968]{1,0:T(8,128)(2,1)S(1)}, bf16[48,3968]{1,0:T(8,128)(2,1)S(1)}, u32[]{:S(2)}, u32[]{:S(2)}) collective-permute-start(bf16[48,3968]{1,0:T(8,128)(2,1)S(1)} %get-tuple-element.210), channel_id=1, source_target_pairs={{0,8},{8,0},{1,9},{9,1},{2,10},{10,2},{3,11},{11,3},{4,12},{12,4},... | collective-permute-start | bytes 1142792 | tf_op jit(solution)/shard_map/ppermute | solution.py:25
  300.9 15.2 %collective-permute-start.46 = (bf16[2,96,768]{2,1,0:T(8,128)(2,1)S(1)}, bf16[2,96,768]{2,1,0:T(8,128)(2,1)S(1)}, u32[]{:S(2)}, u32[]{:S(2)}) collective-permute-start(bf16[2,96,768]{2,1,0:T(8,128)(2,1)S(1)} %dynamic-slice_bitcast_fusion.1), channel_id=1, source_target_pairs={{0,2},{2,0},{4,6},{6,4},{1,3},{3,1},{5,7},{7,5},{8,10},{10,8},{12,... | collective-permute-start | bytes 884744 | tf_op jit(solution)/shard_map/ppermute | solution.py:25
  316.2 16.1 %collective-permute-start.48 = (bf16[1,96,768]{2,1,0:T(8,128)(2,1)S(1)}, bf16[1,96,768]{2,1,0:T(8,128)(2,1)S(1)}, u32[]{:S(2)}, u32[]{:S(2)}) collective-permute-start(bf16[1,96,768]{2,1,0:T(8,128)(2,1)S(1)} %constant_dynamic-slice_fusion.2), channel_id=1, source_target_pairs={{0,4},{2,6},{4,0},{6,2},{1,5},{3,7},{5,1},{7,3},{8,12},{10,14},{12... | collective-permute-start | bytes 442376 | tf_op jit(solution)/shard_map/ppermute | solution.py:25
  318.0 14.4 %collective-permute-start.51 = (bf16[2,24,3968]{2,1,0:T(8,128)(2,1)S(1)}, bf16[2,24,3968]{2,1,0:T(8,128)(2,1)S(1)}, u32[]{:S(2)}, u32[]{:S(2)}) collective-permute-start(bf16[2,24,3968]{2,1,0:T(8,128)(2,1)S(1)} %dynamic-slice_bitcast_fusion), channel_id=1, source_target_pairs={{0,2},{2,0},{4,6},{6,4},{1,3},{3,1},{5,7},{7,5},{8,10},{10,8},{12,... | collective-permute-start | bytes 1142792 | tf_op jit(solution)/shard_map/ppermute | solution.py:25
  322.0 28.7 %collective-permute-start.54 = (bf16[96,2304]{1,0:T(8,128)(2,1)S(1)}, bf16[96,2304]{1,0:T(8,128)(2,1)S(1)}, u32[]{:S(2)}, u32[]{:S(2)}) collective-permute-start(bf16[96,2304]{1,0:T(8,128)(2,1)S(1)} %get-tuple-element.273), channel_id=1, source_target_pairs={{0,24},{8,16},{16,8},{24,0},{1,25},{9,17},{17,9},{25,1},{2,26},{10... | collective-permute-start | bytes 1327112 | tf_op jit(solution)/shard_map/ppermute | solution.py:113
  323.6 27.1 %collective-permute-start.53 = (bf16[96,2304]{1,0:T(8,128)(2,1)S(1)}, bf16[96,2304]{1,0:T(8,128)(2,1)S(1)}, u32[]{:S(2)}, u32[]{:S(2)}) collective-permute-start(bf16[96,2304]{1,0:T(8,128)(2,1)S(1)} %get-tuple-element.274), channel_id=1, source_target_pairs={{0,16},{8,24},{16,0},{24,8},{1,17},{9,25},{17,1},{25,9},{2,18},{10... | collective-permute-start | bytes 1327112 | tf_op jit(solution)/shard_map/ppermute | solution.py:113
  325.0 25.7 %collective-permute-start.52 = (bf16[96,2304]{1,0:T(8,128)(2,1)S(1)}, bf16[96,2304]{1,0:T(8,128)(2,1)}, u32[]{:S(2)}, u32[]{:S(2)}) collective-permute-start(bf16[96,2304]{1,0:T(8,128)(2,1)S(1)} %get-tuple-element.275), channel_id=1, source_target_pairs={{0,8},{8,0},{16,24},{24,16},{1,9},{9,1},{17,25},{25,17},{2,10},{10... | collective-permute-start | bytes 1327112 | tf_op jit(solution)/shard_map/ppermute | solution.py:113
  332.5 27.1 %collective-permute-start.59 = (bf16[1,96,768]{2,1,0:T(8,128)(2,1)S(1)}, bf16[1,96,768]{2,1,0:T(8,128)(2,1)S(1)}, u32[]{:S(2)}, u32[]{:S(2)}) collective-permute-start(bf16[1,96,768]{2,1,0:T(8,128)(2,1)S(1)} %add_convert_fusion.30), channel_id=1, source_target_pairs={{0,4},{2,6},{4,0},{6,2},{1,5},{3,7},{5,1},{7,3},{8,12},{10,14},{12... | collective-permute-start | bytes 442376 | tf_op jit(solution)/shard_map/ppermute | solution.py:25
  341.4 15.8 %collective-permute-start.63 = (bf16[1,24,3968]{2,1,0:T(8,128)(2,1)S(1)}, bf16[1,24,3968]{2,1,0:T(8,128)(2,1)S(1)}, u32[]{:S(2)}, u32[]{:S(2)}) collective-permute-start(bf16[1,24,3968]{2,1,0:T(8,128)(2,1)S(1)} %constant_dynamic-slice_fusion), channel_id=1, source_target_pairs={{0,4},{2,6},{4,0},{6,2},{1,5},{3,7},{5,1},{7,3},{8,12},{10,14},{12... | collective-permute-start | bytes 571400 | tf_op jit(solution)/shard_map/ppermute | solution.py:25
  359.6 12.6 %collective-permute-start.64 = (bf16[1,24,3968]{2,1,0:T(8,128)(2,1)S(1)}, bf16[1,24,3968]{2,1,0:T(8,128)(2,1)S(1)}, u32[]{:S(2)}, u32[]{:S(2)}) collective-permute-start(bf16[1,24,3968]{2,1,0:T(8,128)(2,1)S(1)} %add_convert_fusion.29), channel_id=1, source_target_pairs={{0,4},{2,6},{4,0},{6,2},{1,5},{3,7},{5,1},{7,3},{8,12},{10,14},{12... | collective-permute-start | bytes 571400 | tf_op jit(solution)/shard_map/ppermute | solution.py:25
  361.6 20.3 %collective-permute-start.60 = (bf16[2,96,768]{2,1,0:T(8,128)(2,1)S(1)}, bf16[2,96,768]{2,1,0:T(8,128)(2,1)S(1)}, u32[]{:S(2)}, u32[]{:S(2)}) collective-permute-start(bf16[2,96,768]{2,1,0:T(8,128)(2,1)S(1)} %maximum_bitcast_fusion.7), channel_id=1, source_target_pairs={{0,2},{2,0},{4,6},{6,4},{1,3},{3,1},{5,7},{7,5},{8,10},{10,8},{12,... | collective-permute-start | bytes 884744 | tf_op jit(solution)/shard_map/ppermute | solution.py:25
  372.8 17.7 %collective-permute-start.65 = (bf16[2,24,3968]{2,1,0:T(8,128)(2,1)S(1)}, bf16[2,24,3968]{2,1,0:T(8,128)(2,1)S(1)}, u32[]{:S(2)}, u32[]{:S(2)}) collective-permute-start(bf16[2,24,3968]{2,1,0:T(8,128)(2,1)S(1)} %maximum_bitcast_fusion.4), channel_id=1, source_target_pairs={{0,2},{2,0},{4,6},{6,4},{1,3},{3,1},{5,7},{7,5},{8,10},{10,8},{12,... | collective-permute-start | bytes 1142792 | tf_op jit(solution)/shard_map/ppermute | solution.py:25
  (72 other events, 503.5 us)
Sparse Core Ops, SparseCore 0:
  24.5 76.9 all-gather.5
  106.3 39.0 all-gather.7
  264.5 49.9 all-gather.9

commit v4 on v3

--- a/solution.py
+++ b/solution.py
@@ -943,20 +943,19 @@
     g_qkv = row_blocks_call(ids, x, tie(grad_packed, red_up.state, red_down.state), fsize)
     red_up.plane_second(g_qkv)
     red_down.near_z(g_qkv)
-    red_qkv.core(tie(g_qkv, red_up.state, red_down.state))
+    red_qkv.core(tie(g_qkv, red_up.state))
     red_qkv.chip_direct()
-    red_down.far_z(red_qkv.state)
-    red_up.near_z(red_qkv.state)
-    red_up.after(red_qkv.state, red_down.state)
-    red_down.after(red_up.state)
-    token_grad = token_grad_call(tie(resid, red_qkv.state, red_down.state, red_up.state), grad_packed, w_first)
+    token_grad = token_grad_call(tie(resid, red_qkv.state), grad_packed, w_first)
+    red_down.far_z(token_grad)
+    red_up.near_z(token_grad)
     others = cross_grads(tie(docs, token_grad), ends, ("up", "qkv"))
     red_qkv.plane_direct(token_grad, others)
     lead = red_qkv.state
-    others |= cross_grads(tie(docs, lead), ends, ("down", "out", "rest"))
+    later = cross_grads(tie(docs, lead), ends, ("down", "out", "rest"))
+    others |= later
     red_down.back_far(token_grad, lead)
     red_up.far_z(token_grad, lead)
-    red_qkv.near_z()
+    red_qkv.near_z(later)
     lead = red_qkv.state
     red_down.back_near(lead)
     red_up.back_far(lead)

time: 418 us -> 411 us (0.983)
  waiting for transfers between devices: 127 us -> 117 us
    ppermute x43, waiting for transfers between devices: 109 us -> 99.2 us  [swap(): got = lax.ppermute(value, axis, [(i, i ^ bit) for i in range(size)])]
  transfers between devices with their start and end apart: 70 -> 70, of which waited for: 43 -> 41; matrix products, arithmetic and copies ran while one was open for 9% -> 10% of each run, Pallas kernels for 29% -> 29%
where the time goes in v4:
time: 411 us; the launch traced here: 404 us
  Pallas kernels  129 us (31%)
  waiting for transfers between devices  117 us (28%)
  starting transfers between devices  72.5 us (18%)
  other arithmetic  30.5 us (7%)
  local copies, waits for them, and re-layouts  21.4 us (5%)
  matrix products  18.2 us (4%)
  between operations  15.4 us (4%)
    ppermute x43, waiting for transfers between devices, swap(): got = lax.ppermute(value, axis, [(i, i ^ bit) for i in range(size)])  99.2 us
    ppermute x43, starting transfers between devices, swap(): got = lax.ppermute(value, axis, [(i, i ^ bit) for i in range(size)])  43.9 us
    ppermute x24, starting transfers between devices, swap_f(): got = lax.ppermute(value, ('y', 'x'), [(i, i ^ dist) for i in range(count)])  28.2 us
    pallas_call x3, Pallas kernels, row_blocks_call(): pl.pallas_call(functools.partial(row_blocks_kernel, count=count), grid_sp...  24.4 us
    pallas_call x1, Pallas kernels, finish_call(): pl.pallas_call(functools.partial(finish_kernel, tile=tile, seg=total // g...  23.8 us
    pallas_call x1, Pallas kernels, finish_back_call(): pl.pallas_call(functools.partial(finish_back_kernel, tile=tile, seg=total...  23.5 us
    dot_general x19, matrix products, product(): jnp.einsum(einsum_form, left_op, right_op, preferred_element_type=f32)  18.2 us
    pallas_call x1, Pallas kernels, attend_back_call(): pl.pallas_call(functools.partial(attend_back_kernel, seg=total // counts....  17.9 us
  transfers between devices with their start and end apart: 70, of which 41 were waited for; matrix products, arithmetic and copies ran while one was open for 10% of the time, Pallas kernels for 29%

profile of v4, /device:TPU:0, one launch (start us, length us, event | category | flops | bytes accessed | tf_op | source)
XLA Modules:
  0.0 403.8 jit_solution(12800761754038806388)
XLA Ops:
  12.9 4.0 collective-permute-start.1
  16.9 7.3 %collective-permute-done.1 = bf16[1,48,1536]{2,1,0:T(8,128)(2,1)S(1)} collective-permute-done((bf16[1,48,1536]{2,1,0:T(8,128)(2,1)S(1)}, bf16[1,48,1536]{2,1,0:T(8,128)(2,1)S(1)}, u32[]{:S(2)}, u32[]{:S(2)}) %collective-permute-start.1) | collective-permute-done | bytes 147488 | tf_op jit(solution)/shard_map/ppermute | solution.py:25
  25.7 8.2 %collective-permute-done.2 = bf16[2,48,1536]{2,1,0:T(8,128)(2,1)S(1)} collective-permute-done((bf16[2,48,1536]{2,1,0:T(8,128)(2,1)S(1)}, bf16[2,48,1536]{2,1,0:T(8,128)(2,1)S(1)}, u32[]{:S(2)}, u32[]{:S(2)}) %collective-permute-start.2) | collective-permute-done | bytes 294944 | tf_op jit(solution)/shard_map/ppermute | solution.py:25
  47.7 3.7 collective-permute-done.5
  57.4 6.2 %collective-permute-done.12 = bf16[2,192,384]{2,1,0:T(8,128)(2,1)S(1)} collective-permute-done((bf16[2,192,384]{2,1,0:T(8,128)(2,1)S(1)}, bf16[2,192,384]{2,1,0:T(8,128)(2,1)S(1)}, u32[]{:S(2)}, u32[]{:S(2)}) %collective-permute-start.12) | collective-permute-done | bytes 294944 | tf_op jit(solution)/shard_map/ppermute | solution.py:25
  63.8 6.4 %collective-permute-done.10 = bf16[2,2,48,1536]{3,2,1,0:T(8,128)(2,1)S(1)} collective-permute-done((bf16[2,2,48,1536]{3,2,1,0:T(8,128)(2,1)S(1)}, bf16[2,2,48,1536]{3,2,1,0:T(8,128)(2,1)S(1)}, u32[]{:S(2)}, u32[]{:S(2)}) %collective-permute-start.10) | collective-permute-done | bytes 589856 | tf_op jit(solution)/shard_map/ppermute | solution.py:25
  78.3 9.7 %collective-permute-done.15 = bf16[2,192,384]{2,1,0:T(8,128)(2,1)S(1)} collective-permute-done((bf16[2,192,384]{2,1,0:T(8,128)(2,1)S(1)}, bf16[2,192,384]{2,1,0:T(8,128)(2,1)S(1)}, u32[]{:S(2)}, u32[]{:S(2)}) %collective-permute-start.15) | collective-permute-done | bytes 294944 | tf_op jit(solution)/shard_map/ppermute | solution.py:25
  91.0 12.6 %attend.1 = (bf16[1024,2304]{1,0:T(8,128)(2,1)}, bf16[1024,768]{1,0:T(8,128)(2,1)}) custom-call(s32[8]{0:T(128)} %bitcast.407, bf16[1024,768]{1,0:T(8,128)(2,1)} %bitcast.402, bf16[768,3072]{1,0:T(8,128)(2,1)} %copy-done), custom_call_target="tpu_custom_call" | custom-call | flops 4831838208 | bytes 16777216 | tf_op jit(solution)/shard_map/attend/pallas_call | solution.py:348
  111.2 3.1 pad_maximum_fusion.1
  116.8 23.8 %finish.1 = (f32[1024,768]{1,0:T(8,128)}, f32[1024,768]{1,0:T(8,128)}, bf16[1024,3072]{1,0:T(8,128)(2,1)}, bf16[1024,3072]{1,0:T(8,128)(2,1)}, bf16[1024,768]{1,0:T(8,128)(2,1)}, /*index=5*/f32[8,768]{1,0:T(8,128)}) custom-call(s32[8]{0:T(128)} %bitcast.408, bf16[1024,768]{1,0:T(8,128)(2,1)} %bitcast.403, ...), custom_call_target="tpu_custom_call" | custom-call | flops 10871635968 | bytes 41943040 | tf_op jit(solution)/shard_map/finish/pallas_call | solution.py:502
  145.4 4.8 %unpack.1 = (bf16[768,576]{1,0:T(8,128)(2,1)}, bf16[192,768]{1,0:T(8,128)(2,1)}, bf16[768,768]{1,0:T(8,128)(2,1)}, bf16[768,768]{1,0:T(8,128)(2,1)}) custom-call(bf16[8,96,2304]{2,1,0:T(8,128)(2,1)} %bitcast.372), custom_call_target="tpu_custom_call" | custom-call | tf_op jit(solution)/shard_map/unpack/pallas_call | solution.py:752
  175.6 2.7 collective-permute-done.30
  188.9 2.7 collective-permute-done.33
  197.1 23.5 %finish_back.1 = (bf16[1024,768]{1,0:T(8,128)(2,1)}, bf16[1024,3072]{1,0:T(8,128)(2,1)}, f32[1024,768]{1,0:T(8,128)}, bf16[1024,768]{1,0:T(8,128)(2,1)}, bf16[10...) custom-call(s32[8]{0:T(128)} %bitcast.409, bf16[1024,768]{1,0:T(8,128)(2,1)} %bitcast.401, ...), custom_call_target="tpu_custom_call" | custom-call | flops 10871635968 | bytes 41943040 | tf_op jit(solution)/shard_map/finish_back/pallas_call | solution.py:574
  228.2 9.4 %wide_blocks.1 = (bf16[4,384,768]{2,1,0:T(8,128)(2,1)}, bf16[4,384,768]{2,1,0:T(8,128)(2,1)}) custom-call(s32[2]{0:T(128)} %pad_add_fusion.ids_ref, bf16[1024,768]{1,0:T(8,128)(2,1)} %get-tuple-element.176.a_ref, bf16[1024,3072]{1,0:T(8,128)(2,1)} %get-tuple-element.177.b_ref), custom_call_target="tpu_custom_call" | custom-call | flops 9663676416 | bytes 16777216 | tf_op jit(solution)/shard_map/wide_blocks/pallas_call | solution.py:680
  237.6 5.7 %row_blocks.3 = (bf16[384,896]{1,0:T(8,128)(2,1)}, bf16[384,896]{1,0:T(8,128)(2,1)}) custom-call(s32[2]{0:T(128)} %pad_add_fusion.ids_ref, bf16[1024,768]{1,0:T(8,128)(2,1)} %get-tuple-element.180.mixed_ref.a_ref, bf16[1024,768]{1,0:T(8,128)(2,1)} %get-tuple-element.181.b_ref, f32[16,768]{1,0:T(8,128)} %get-tuple-element.182.refs_0_), custom_call_target="tpu_custom_call" | custom-call | flops 2415919104 | bytes 16777216 | tf_op jit(solution)/shard_map/row_blocks/pallas_call | solution.py:648
  245.9 10.2 %row_blocks.4 = (bf16[384,3072]{1,0:T(8,128)(2,1)}, bf16[384,3072]{1,0:T(8,128)(2,1)}) custom-call(s32[2]{0:T(128)} %pad_add_fusion.ids_ref, bf16[1024,768]{1,0:T(8,128)(2,1)} %get-tuple-element.187.a_ref, bf16[1024,3072]{1,0:T(8,128)(2,1)} %get-tuple-element.188.b_ref), custom_call_target="tpu_custom_call" | custom-call | flops 9663676416 | bytes 16777216 | tf_op jit(solution)/shard_map/row_blocks/pallas_call | solution.py:648
  256.0 3.4 collective-permute-done.39
  264.3 3.5 collective-permute-done.37
  276.7 17.9 %attend_back.1.b_ref.g_ref = bf16[1024,2304]{1,0:T(8,128)(2,1)} custom-call(s32[8]{0:T(128)} %bitcast.410, bf16[1024,2304]{1,0:T(8,128)(2,1)} %get-tuple-element.148.packed_ref, bf16[1024,768]{1,0:T(8,128)(2,1)} %get-tuple-element.200.grad_ref), custom_call_target="tpu_custom_call" | custom-call | flops 9663676416 | bytes 16777216 | tf_op jit(solution)/shard_map/attend_back/pallas_call | solution.py:401
  294.6 3.6 collective-permute-done.44
  301.2 8.5 %row_blocks.5 = (bf16[384,2304]{1,0:T(8,128)(2,1)}, bf16[384,2304]{1,0:T(8,128)(2,1)}) custom-call(s32[2]{0:T(128)} %pad_add_fusion.ids_ref, bf16[1024,768]{1,0:T(8,128)(2,1)} %bitcast.404, bf16[1024,2304]{1,0:T(8,128)(2,1)} %attend_back.1.b_ref.g_ref), custom_call_target="tpu_custom_call" | custom-call | flops 7247757312 | bytes 16777216 | tf_op jit(solution)/shard_map/row_blocks/pallas_call | solution.py:648
  309.7 6.3 %collective-permute-done.54 = bf16[2,96,768]{2,1,0:T(8,128)(2,1)S(1)} collective-permute-done((bf16[2,96,768]{2,1,0:T(8,128)(2,1)S(1)}, bf16[2,96,768]{2,1,0:T(8,128)(2,1)S(1)}, u32[]{:S(2)}, u32[]{:S(2)}) %collective-permute-start.54) | collective-permute-done | bytes 294944 | tf_op jit(solution)/shard_map/ppermute | solution.py:25
  323.6 8.7 %token_grad.1 = bf16[1024,768]{1,0:T(8,128)(2,1)} custom-call(f32[1024,768]{1,0:T(8,128)} %get-tuple-element.213.resid_ref, bf16[1024,2304]{1,0:T(8,128)(2,1)} %attend_back.1.b_ref.g_ref, bf16[768,3072]{1,0:T(8,128)(2,1)} %copy-done), custom_call_target="tpu_custom_call" | custom-call | flops 7247757312 | bytes 16777216 | tf_op jit(solution)/shard_map/token_grad/pallas_call | solution.py:701
  335.6 3.0 fusion.2
  338.6 3.4 fusion
  343.3 3.0 fusion.20
  355.1 9.7 %collective-permute-done.50 = bf16[2,24,2304]{2,1,0:T(8,128)(2,1)S(1)} collective-permute-done((bf16[2,24,2304]{2,1,0:T(8,128)(2,1)S(1)}, bf16[2,24,2304]{2,1,0:T(8,128)(2,1)S(1)}, u32[]{:S(2)}, u32[]{:S(2)}) %collective-permute-start.50) | collective-permute-done | bytes 221216 | tf_op jit(solution)/shard_map/ppermute | solution.py:25
  368.0 5.7 %collective-permute-done.57 = bf16[2,96,768]{2,1,0:T(8,128)(2,1)S(1)} collective-permute-done((bf16[2,96,768]{2,1,0:T(8,128)(2,1)S(1)}, bf16[2,96,768]{2,1,0:T(8,128)(2,1)S(1)}, u32[]{:S(2)}, u32[]{:S(2)}) %collective-permute-start.57) | collective-permute-done | bytes 294944 | tf_op jit(solution)/shard_map/ppermute | solution.py:25
  374.6 5.7 %collective-permute-done.52 = bf16[1,24,2304]{2,1,0:T(8,128)(2,1)S(1)} collective-permute-done((bf16[1,24,2304]{2,1,0:T(8,128)(2,1)S(1)}, bf16[1,24,2304]{2,1,0:T(8,128)(2,1)S(1)}, u32[]{:S(2)}, u32[]{:S(2)}) %collective-permute-start.52) | collective-permute-done | bytes 110624 | tf_op jit(solution)/shard_map/ppermute | solution.py:25
  380.4 3.3 collective-permute-start.53
  383.7 4.0 collective-permute-done.53
  (398 shorter events, 154.5 us)
Async XLA Ops:
  7.2 99.0 %all-gather.6.cloned.1.call-start = ((), (), s32[]{:S(2)}) async-start(), calls=%async_computation | async-start | bytes 5068800 | tf_op jit(solution)/shard_map/all_gather | solution.py:875
  24.4 121.0 %all-gather.8.cloned.1.call-start = ((), (), s32[]{:S(2)}) async-start(), calls=%async_computation.1 | async-start | bytes 3981312 | tf_op jit(solution)/shard_map/all_gather | solution.py:899
  55.1 15.1 %collective-permute-start.10 = (bf16[2,2,48,1536]{3,2,1,0:T(8,128)(2,1)S(1)}, bf16[2,2,48,1536]{3,2,1,0:T(8,128)(2,1)S(1)}, u32[]{:S(2)}, u32[]{:S(2)}) collective-permute-start(bf16[2,2,48,1536]{3,2,1,0:T(8,128)(2,1)S(1)} %get-tuple-element.140), channel_id=1, source_target_pairs={{0,16},{16,0},{1,17},{17,1},{2,18},{18,2},{3,19},{19,3},{4,20},{20... | collective-permute-start | bytes 1769480 | tf_op jit(solution)/shard_map/ppermute | solution.py:25
  56.6 15.8 %collective-permute-start.11 = (bf16[2,2,48,1536]{3,2,1,0:T(8,128)(2,1)S(1)}, bf16[2,2,48,1536]{3,2,1,0:T(8,128)(2,1)S(1)}, u32[]{:S(2)}, u32[]{:S(2)}) collective-permute-start(bf16[2,2,48,1536]{3,2,1,0:T(8,128)(2,1)S(1)} %get-tuple-element.141), channel_id=1, source_target_pairs={{0,8},{8,0},{1,9},{9,1},{2,10},{10,2},{3,11},{11,3},{4,12},{12,4},... | collective-permute-start | bytes 1769480 | tf_op jit(solution)/shard_map/ppermute | solution.py:25
  72.9 15.2 %collective-permute-start.15 = (bf16[2,192,384]{2,1,0:T(8,128)(2,1)S(1)}, bf16[2,192,384]{2,1,0:T(8,128)(2,1)S(1)}, u32[]{:S(2)}, u32[]{:S(2)}) collective-permute-start(bf16[2,192,384]{2,1,0:T(8,128)(2,1)S(1)} %get-tuple-element.315), channel_id=1, source_target_pairs={{0,16},{16,0},{1,17},{17,1},{2,18},{18,2},{3,19},{19,3},{4,20},{20... | collective-permute-start | bytes 884744 | tf_op jit(solution)/shard_map/ppermute | solution.py:25
  74.4 15.5 %collective-permute-start.14 = (bf16[2,192,384]{2,1,0:T(8,128)(2,1)S(1)}, bf16[2,192,384]{2,1,0:T(8,128)(2,1)S(1)}, u32[]{:S(2)}, u32[]{:S(2)}) collective-permute-start(bf16[2,192,384]{2,1,0:T(8,128)(2,1)S(1)} %get-tuple-element.316), channel_id=1, source_target_pairs={{0,8},{8,0},{1,9},{9,1},{2,10},{10,2},{3,11},{11,3},{4,12},{12,4},... | collective-permute-start | bytes 884744 | tf_op jit(solution)/shard_map/ppermute | solution.py:25
  90.2 15.2 %collective-permute-start.17 = (bf16[2,2,192,384]{3,2,1,0:T(8,128)(2,1)S(1)}, bf16[2,2,192,384]{3,2,1,0:T(8,128)(2,1)S(1)}, u32[]{:S(2)}, u32[]{:S(2)}) collective-permute-start(bf16[2,2,192,384]{3,2,1,0:T(8,128)(2,1)S(1)} %pad_maximum_fusion.16), channel_id=1, source_target_pairs={{0,8},{8,0},{1,9},{9,1},{2,10},{10,2},{3,11},{11,3},{4,12},{12,4},... | collective-permute-start | bytes 1769480 | tf_op jit(solution)/shard_map/ppermute | solution.py:25
  90.9 14.6 %collective-permute-start.16 = (bf16[2,2,192,384]{3,2,1,0:T(8,128)(2,1)S(1)}, bf16[2,2,192,384]{3,2,1,0:T(8,128)(2,1)S(1)}, u32[]{:S(2)}, u32[]{:S(2)}) collective-permute-start(bf16[2,2,192,384]{3,2,1,0:T(8,128)(2,1)S(1)} %pad_maximum_fusion.15), channel_id=1, source_target_pairs={{0,16},{16,0},{1,17},{17,1},{2,18},{18,2},{3,19},{19,3},{4,20},{20... | collective-permute-start | bytes 1769480 | tf_op jit(solution)/shard_map/ppermute | solution.py:25
  106.2 229.4 %all-gather.10.cloned.1.call-start = ((), (), s32[]{:S(2)}) async-start(), calls=%async_computation.2 | async-start | bytes 5160960 | tf_op jit(solution)/shard_map/all_gather | solution.py:926
  193.6 27.1 %collective-permute-start.35 = (bf16[32,1344]{1,0:T(8,128)(2,1)S(1)}, bf16[32,1344]{1,0:T(8,128)(2,1)S(1)}, u32[]{:S(2)}, u32[]{:S(2)}) collective-permute-start(bf16[32,1344]{1,0:T(8,128)(2,1)S(1)} %concatenate.91), channel_id=1, source_target_pairs={{0,16},{8,24},{16,0},{24,8},{1,17},{9,25},{17,1},{25,9},{2,18},{10... | collective-permute-start | bytes 258056 | tf_op jit(solution)/shard_map/ppermute | solution.py:113
  195.1 25.6 %collective-permute-start.36 = (bf16[32,1344]{1,0:T(8,128)(2,1)S(1)}, bf16[32,1344]{1,0:T(8,128)(2,1)S(1)}, u32[]{:S(2)}, u32[]{:S(2)}) collective-permute-start(bf16[32,1344]{1,0:T(8,128)(2,1)S(1)} %concatenate.91), channel_id=1, source_target_pairs={{0,24},{8,16},{16,8},{24,0},{1,25},{9,17},{17,9},{25,1},{2,26},{10... | collective-permute-start | bytes 258056 | tf_op jit(solution)/shard_map/ppermute | solution.py:113
  196.6 24.2 %collective-permute-start.34 = (bf16[32,1344]{1,0:T(8,128)(2,1)S(1)}, bf16[32,1344]{1,0:T(8,128)(2,1)S(1)}, u32[]{:S(2)}, u32[]{:S(2)}) collective-permute-start(bf16[32,1344]{1,0:T(8,128)(2,1)S(1)} %concatenate.91), channel_id=1, source_target_pairs={{0,8},{8,0},{16,24},{24,16},{1,9},{9,1},{17,25},{25,17},{2,10},{10... | collective-permute-start | bytes 258056 | tf_op jit(solution)/shard_map/ppermute | solution.py:113
  243.6 15.8 %collective-permute-start.39 = (bf16[2,192,768]{2,1,0:T(8,128)(2,1)S(1)}, bf16[2,192,768]{2,1,0:T(8,128)(2,1)S(1)}, u32[]{:S(2)}, u32[]{:S(2)}) collective-permute-start(bf16[2,192,768]{2,1,0:T(8,128)(2,1)S(1)} %pad_maximum_fusion.17), channel_id=1, source_target_pairs={{0,8},{8,0},{1,9},{9,1},{2,10},{10,2},{3,11},{11,3},{4,12},{12,4},... | collective-permute-start | bytes 1769480 | tf_op jit(solution)/shard_map/ppermute | solution.py:25
  245.2 15.5 %collective-permute-start.40 = (bf16[2,192,768]{2,1,0:T(8,128)(2,1)S(1)}, bf16[2,192,768]{2,1,0:T(8,128)(2,1)S(1)}, u32[]{:S(2)}, u32[]{:S(2)}) collective-permute-start(bf16[2,192,768]{2,1,0:T(8,128)(2,1)S(1)} %pad_maximum_fusion.18), channel_id=1, source_target_pairs={{0,16},{16,0},{1,17},{17,1},{2,18},{18,2},{3,19},{19,3},{4,20},{20... | collective-permute-start | bytes 1769480 | tf_op jit(solution)/shard_map/ppermute | solution.py:25
  272.3 26.1 %collective-permute-start.42 = (bf16[2,48,3968]{2,1,0:T(8,128)(2,1)S(1)}, bf16[2,48,3968]{2,1,0:T(8,128)(2,1)S(1)}, u32[]{:S(2)}, u32[]{:S(2)}) collective-permute-start(bf16[2,48,3968]{2,1,0:T(8,128)(2,1)S(1)} %pad_maximum_fusion.6), channel_id=1, source_target_pairs={{0,8},{8,0},{1,9},{9,1},{2,10},{10,2},{3,11},{11,3},{4,12},{12,4},... | collective-permute-start | bytes 2285576 | tf_op jit(solution)/shard_map/ppermute | solution.py:25
  273.0 25.6 %collective-permute-start.43 = (bf16[2,48,3968]{2,1,0:T(8,128)(2,1)S(1)}, bf16[2,48,3968]{2,1,0:T(8,128)(2,1)S(1)}, u32[]{:S(2)}, u32[]{:S(2)}) collective-permute-start(bf16[2,48,3968]{2,1,0:T(8,128)(2,1)S(1)} %pad_maximum_fusion.8), channel_id=1, source_target_pairs={{0,16},{16,0},{1,17},{17,1},{2,18},{18,2},{3,19},{19,3},{4,20},{20... | collective-permute-start | bytes 2285576 | tf_op jit(solution)/shard_map/ppermute | solution.py:25
  274.5 23.6 %collective-permute-start.44 = (bf16[192,768]{1,0:T(8,128)(2,1)S(1)}, bf16[192,768]{1,0:T(8,128)(2,1)S(1)}, u32[]{:S(2)}, u32[]{:S(2)}) collective-permute-start(bf16[192,768]{1,0:T(8,128)(2,1)S(1)} %copy-done.16), channel_id=1, source_target_pairs={{0,16},{16,0},{1,17},{17,1},{2,18},{18,2},{3,19},{19,3},{4,20},{20... | collective-permute-start | bytes 884744 | tf_op jit(solution)/shard_map/ppermute | solution.py:25
  275.1 23.1 %collective-permute-start.45 = (bf16[192,768]{1,0:T(8,128)(2,1)S(1)}, bf16[192,768]{1,0:T(8,128)(2,1)S(1)}, u32[]{:S(2)}, u32[]{:S(2)}) collective-permute-start(bf16[192,768]{1,0:T(8,128)(2,1)S(1)} %copy-done.15), channel_id=1, source_target_pairs={{0,8},{8,0},{1,9},{9,1},{2,10},{10,2},{3,11},{11,3},{4,12},{12,4},... | collective-permute-start | bytes 884744 | tf_op jit(solution)/shard_map/ppermute | solution.py:25
  298.8 18.9 %collective-permute-start.60 = (bf16[48,3968]{1,0:T(8,128)(2,1)S(1)}, bf16[48,3968]{1,0:T(8,128)(2,1)S(1)}, u32[]{:S(2)}, u32[]{:S(2)}) collective-permute-start(bf16[48,3968]{1,0:T(8,128)(2,1)S(1)} %get-tuple-element.207), channel_id=1, source_target_pairs={{0,16},{16,0},{1,17},{17,1},{2,18},{18,2},{3,19},{19,3},{4,20},{20... | collective-permute-start | bytes 1142792 | tf_op jit(solution)/shard_map/ppermute | solution.py:25
  300.3 17.3 %collective-permute-start.61 = (bf16[48,3968]{1,0:T(8,128)(2,1)S(1)}, bf16[48,3968]{1,0:T(8,128)(2,1)S(1)}, u32[]{:S(2)}, u32[]{:S(2)}) collective-permute-start(bf16[48,3968]{1,0:T(8,128)(2,1)S(1)} %get-tuple-element.209), channel_id=1, source_target_pairs={{0,8},{8,0},{1,9},{9,1},{2,10},{10,2},{3,11},{11,3},{4,12},{12,4},... | collective-permute-start | bytes 1142792 | tf_op jit(solution)/shard_map/ppermute | solution.py:25
  300.9 15.2 %collective-permute-start.54 = (bf16[2,96,768]{2,1,0:T(8,128)(2,1)S(1)}, bf16[2,96,768]{2,1,0:T(8,128)(2,1)S(1)}, u32[]{:S(2)}, u32[]{:S(2)}) collective-permute-start(bf16[2,96,768]{2,1,0:T(8,128)(2,1)S(1)} %dynamic-slice_bitcast_fusion.1), channel_id=1, source_target_pairs={{0,2},{2,0},{4,6},{6,4},{1,3},{3,1},{5,7},{7,5},{8,10},{10,8},{12,... | collective-permute-start | bytes 884744 | tf_op jit(solution)/shard_map/ppermute | solution.py:25
  316.2 16.1 %collective-permute-start.55 = (bf16[1,96,768]{2,1,0:T(8,128)(2,1)S(1)}, bf16[1,96,768]{2,1,0:T(8,128)(2,1)S(1)}, u32[]{:S(2)}, u32[]{:S(2)}) collective-permute-start(bf16[1,96,768]{2,1,0:T(8,128)(2,1)S(1)} %constant_dynamic-slice_fusion.1), channel_id=1, source_target_pairs={{0,4},{2,6},{4,0},{6,2},{1,5},{3,7},{5,1},{7,3},{8,12},{10,14},{12... | collective-permute-start | bytes 442376 | tf_op jit(solution)/shard_map/ppermute | solution.py:25
  317.9 14.4 %collective-permute-start.62 = (bf16[2,24,3968]{2,1,0:T(8,128)(2,1)S(1)}, bf16[2,24,3968]{2,1,0:T(8,128)(2,1)S(1)}, u32[]{:S(2)}, u32[]{:S(2)}) collective-permute-start(bf16[2,24,3968]{2,1,0:T(8,128)(2,1)S(1)} %dynamic-slice_bitcast_fusion), channel_id=1, source_target_pairs={{0,2},{2,0},{4,6},{6,4},{1,3},{3,1},{5,7},{7,5},{8,10},{10,8},{12,... | collective-permute-start | bytes 1142792 | tf_op jit(solution)/shard_map/ppermute | solution.py:25
  320.1 21.9 %collective-permute-start.49 = (bf16[96,2304]{1,0:T(8,128)(2,1)S(1)}, bf16[96,2304]{1,0:T(8,128)(2,1)S(1)}, u32[]{:S(2)}, u32[]{:S(2)}) collective-permute-start(bf16[96,2304]{1,0:T(8,128)(2,1)S(1)} %get-tuple-element.271), channel_id=1, source_target_pairs={{0,24},{8,16},{16,8},{24,0},{1,25},{9,17},{17,9},{25,1},{2,26},{10... | collective-permute-start | bytes 1327112 | tf_op jit(solution)/shard_map/ppermute | solution.py:113
  322.5 19.5 %collective-permute-start.48 = (bf16[96,2304]{1,0:T(8,128)(2,1)S(1)}, bf16[96,2304]{1,0:T(8,128)(2,1)S(1)}, u32[]{:S(2)}, u32[]{:S(2)}) collective-permute-start(bf16[96,2304]{1,0:T(8,128)(2,1)S(1)} %get-tuple-element.272), channel_id=1, source_target_pairs={{0,16},{8,24},{16,0},{24,8},{1,17},{9,25},{17,1},{25,9},{2,18},{10... | collective-permute-start | bytes 1327112 | tf_op jit(solution)/shard_map/ppermute | solution.py:113
  323.1 18.9 %collective-permute-start.47 = (bf16[96,2304]{1,0:T(8,128)(2,1)S(1)}, bf16[96,2304]{1,0:T(8,128)(2,1)}, u32[]{:S(2)}, u32[]{:S(2)}) collective-permute-start(bf16[96,2304]{1,0:T(8,128)(2,1)S(1)} %get-tuple-element.273), channel_id=1, source_target_pairs={{0,8},{8,0},{16,24},{24,16},{1,9},{9,1},{17,25},{25,17},{2,10},{10... | collective-permute-start | bytes 1327112 | tf_op jit(solution)/shard_map/ppermute | solution.py:113
  332.4 19.4 %collective-permute-start.56 = (bf16[1,96,768]{2,1,0:T(8,128)(2,1)S(1)}, bf16[1,96,768]{2,1,0:T(8,128)(2,1)S(1)}, u32[]{:S(2)}, u32[]{:S(2)}) collective-permute-start(bf16[1,96,768]{2,1,0:T(8,128)(2,1)S(1)} %add_convert_fusion.30), channel_id=1, source_target_pairs={{0,4},{2,6},{4,0},{6,2},{1,5},{3,7},{5,1},{7,3},{8,12},{10,14},{12... | collective-permute-start | bytes 442376 | tf_op jit(solution)/shard_map/ppermute | solution.py:25
  333.1 15.5 %collective-permute-start.63 = (bf16[1,24,3968]{2,1,0:T(8,128)(2,1)S(1)}, bf16[1,24,3968]{2,1,0:T(8,128)(2,1)}, u32[]{:S(2)}, u32[]{:S(2)}) collective-permute-start(bf16[1,24,3968]{2,1,0:T(8,128)(2,1)S(1)} %constant_dynamic-slice_fusion), channel_id=1, source_target_pairs={{0,4},{2,6},{4,0},{6,2},{1,5},{3,7},{5,1},{7,3},{8,12},{10,14},{12... | collective-permute-start | bytes 571400 | tf_op jit(solution)/shard_map/ppermute | solution.py:25
  351.9 13.0 %collective-permute-start.64 = (bf16[1,24,3968]{2,1,0:T(8,128)(2,1)S(1)}, bf16[1,24,3968]{2,1,0:T(8,128)(2,1)S(1)}, u32[]{:S(2)}, u32[]{:S(2)}) collective-permute-start(bf16[1,24,3968]{2,1,0:T(8,128)(2,1)S(1)} %add_convert_fusion.29), channel_id=1, source_target_pairs={{0,4},{2,6},{4,0},{6,2},{1,5},{3,7},{5,1},{7,3},{8,12},{10,14},{12... | collective-permute-start | bytes 571400 | tf_op jit(solution)/shard_map/ppermute | solution.py:25
  354.2 19.4 %collective-permute-start.57 = (bf16[2,96,768]{2,1,0:T(8,128)(2,1)S(1)}, bf16[2,96,768]{2,1,0:T(8,128)(2,1)S(1)}, u32[]{:S(2)}, u32[]{:S(2)}) collective-permute-start(bf16[2,96,768]{2,1,0:T(8,128)(2,1)S(1)} %maximum_bitcast_fusion.7), channel_id=1, source_target_pairs={{0,2},{2,0},{4,6},{6,4},{1,3},{3,1},{5,7},{7,5},{8,10},{10,8},{12,... | collective-permute-start | bytes 884744 | tf_op jit(solution)/shard_map/ppermute | solution.py:25
  365.9 17.7 %collective-permute-start.65 = (bf16[2,24,3968]{2,1,0:T(8,128)(2,1)S(1)}, bf16[2,24,3968]{2,1,0:T(8,128)(2,1)S(1)}, u32[]{:S(2)}, u32[]{:S(2)}) collective-permute-start(bf16[2,24,3968]{2,1,0:T(8,128)(2,1)S(1)} %maximum_bitcast_fusion.4), channel_id=1, source_target_pairs={{0,2},{2,0},{4,6},{6,4},{1,3},{3,1},{5,7},{7,5},{8,10},{10,8},{12,... | collective-permute-start | bytes 1142792 | tf_op jit(solution)/shard_map/ppermute | solution.py:25
  374.6 13.2 %collective-permute-start.58 = (bf16[384,768]{1,0:T(8,128)(2,1)S(1)}, bf16[384,768]{1,0:T(8,128)(2,1)S(1)}, u32[]{:S(2)}, u32[]{:S(2)}) collective-permute-start(bf16[384,768]{1,0:T(8,128)(2,1)S(1)} %bitcast.377), channel_id=1, source_target_pairs={{0,1},{1,0},{2,3},{3,2},{4,5},{5,4},{6,7},{7,6},{8,9},{9,8},{10,11... | collective-permute-start | bytes 1769480 | tf_op jit(solution)/shard_map/ppermute | solution.py:25
  (72 other events, 508.6 us)
Sparse Core Ops, SparseCore 0:
  24.5 76.9 all-gather.5
  106.3 39.0 all-gather.7
  264.5 49.9 all-gather.9

commit v5 on v4

--- a/solution.py
+++ b/solution.py
@@ -921,7 +921,6 @@
         lens, cot, tie(cls_here_grad, spread), z1, z2, slope, w_first, w_up, w_down, rows
     )
     spread = gather_f(spread, outer)
-    layer_out = hidden.reshape(groups, -1, width).at[:, 0].set(tie(cls_out.astype(bf16), outer))
     message, ends = doc_message(tie(spread, outer), pieces, fsize, width)
     docs = lax.all_gather(message, ("z", "c"), axis=0)
     red_down, red_up, red_qkv = RowReduce(), RowReduce(), RowReduce()
@@ -957,6 +956,7 @@
     red_up.far_z(token_grad, lead)
     red_qkv.near_z(later)
     lead = red_qkv.state
+    layer_out = hidden.reshape(groups, -1, width).at[:, 0].set(tie(cls_out.astype(bf16), lead))
     red_down.back_near(lead)
     red_up.back_far(lead)
     red_qkv.far_z()

time: 411 us -> 410 us (level)
  waiting for transfers between devices: 117 us -> 112 us
    ppermute x43, waiting for transfers between devices: 99.2 us -> 93.6 us  [swap(): got = lax.ppermute(value, axis, [(i, i ^ bit) for i in range(size)])]
where the time goes in v5:
time: 410 us; the launch traced here: 402 us
  Pallas kernels  129 us (31%)
  waiting for transfers between devices  112 us (27%)
  starting transfers between devices  76.3 us (19%)
  other arithmetic  30.3 us (7%)
  local copies, waits for them, and re-layouts  21.2 us (5%)
  matrix products  18.2 us (4%)
  between operations  15.4 us (4%)
    ppermute x43, waiting for transfers between devices, swap(): got = lax.ppermute(value, axis, [(i, i ^ bit) for i in range(size)])  93.6 us
    ppermute x43, starting transfers between devices, swap(): got = lax.ppermute(value, axis, [(i, i ^ bit) for i in range(size)])  47.7 us
    ppermute x24, starting transfers between devices, swap_f(): got = lax.ppermute(value, ('y', 'x'), [(i, i ^ dist) for i in range(count)])  28.2 us
    pallas_call x3, Pallas kernels, row_blocks_call(): pl.pallas_call(functools.partial(row_blocks_kernel, count=count), grid_sp...  24.4 us
    pallas_call x1, Pallas kernels, finish_call(): pl.pallas_call(functools.partial(finish_kernel, tile=tile, seg=total // g...  23.8 us
    pallas_call x1, Pallas kernels, finish_back_call(): pl.pallas_call(functools.partial(finish_back_kernel, tile=tile, seg=total...  23.5 us
    dot_general x19, matrix products, product(): jnp.einsum(einsum_form, left_op, right_op, preferred_element_type=f32)  18.2 us
    pallas_call x1, Pallas kernels, attend_back_call(): pl.pallas_call(functools.partial(attend_back_kernel, seg=total // counts....  17.9 us
  transfers between devices with their start and end apart: 70, of which 41 were waited for; matrix products, arithmetic and copies ran while one was open for 10% of the time, Pallas kernels for 29%

profile of v5, /device:TPU:0, one launch (start us, length us, event | category | flops | bytes accessed | tf_op | source)
XLA Modules:
  0.0 401.9 jit_solution(2297143974194912018)
XLA Ops:
  12.9 4.0 collective-permute-start.1
  16.9 7.3 %collective-permute-done.1 = bf16[1,48,1536]{2,1,0:T(8,128)(2,1)S(1)} collective-permute-done((bf16[1,48,1536]{2,1,0:T(8,128)(2,1)S(1)}, bf16[1,48,1536]{2,1,0:T(8,128)(2,1)S(1)}, u32[]{:S(2)}, u32[]{:S(2)}) %collective-permute-start.1) | collective-permute-done | bytes 147488 | tf_op jit(solution)/shard_map/ppermute | solution.py:25
  25.7 8.2 %collective-permute-done.2 = bf16[2,48,1536]{2,1,0:T(8,128)(2,1)S(1)} collective-permute-done((bf16[2,48,1536]{2,1,0:T(8,128)(2,1)S(1)}, bf16[2,48,1536]{2,1,0:T(8,128)(2,1)S(1)}, u32[]{:S(2)}, u32[]{:S(2)}) %collective-permute-start.2) | collective-permute-done | bytes 294944 | tf_op jit(solution)/shard_map/ppermute | solution.py:25
  47.7 3.7 collective-permute-done.5
  57.4 6.2 %collective-permute-done.12 = bf16[2,192,384]{2,1,0:T(8,128)(2,1)S(1)} collective-permute-done((bf16[2,192,384]{2,1,0:T(8,128)(2,1)S(1)}, bf16[2,192,384]{2,1,0:T(8,128)(2,1)S(1)}, u32[]{:S(2)}, u32[]{:S(2)}) %collective-permute-start.12) | collective-permute-done | bytes 294944 | tf_op jit(solution)/shard_map/ppermute | solution.py:25
  63.8 6.4 %collective-permute-done.10 = bf16[2,2,48,1536]{3,2,1,0:T(8,128)(2,1)S(1)} collective-permute-done((bf16[2,2,48,1536]{3,2,1,0:T(8,128)(2,1)S(1)}, bf16[2,2,48,1536]{3,2,1,0:T(8,128)(2,1)S(1)}, u32[]{:S(2)}, u32[]{:S(2)}) %collective-permute-start.10) | collective-permute-done | bytes 589856 | tf_op jit(solution)/shard_map/ppermute | solution.py:25
  78.3 9.7 %collective-permute-done.15 = bf16[2,192,384]{2,1,0:T(8,128)(2,1)S(1)} collective-permute-done((bf16[2,192,384]{2,1,0:T(8,128)(2,1)S(1)}, bf16[2,192,384]{2,1,0:T(8,128)(2,1)S(1)}, u32[]{:S(2)}, u32[]{:S(2)}) %collective-permute-start.15) | collective-permute-done | bytes 294944 | tf_op jit(solution)/shard_map/ppermute | solution.py:25
  91.0 12.6 %attend.1 = (bf16[1024,2304]{1,0:T(8,128)(2,1)}, bf16[1024,768]{1,0:T(8,128)(2,1)}) custom-call(s32[8]{0:T(128)} %bitcast.407, bf16[1024,768]{1,0:T(8,128)(2,1)} %bitcast.402, bf16[768,3072]{1,0:T(8,128)(2,1)} %copy-done), custom_call_target="tpu_custom_call" | custom-call | flops 4831838208 | bytes 16777216 | tf_op jit(solution)/shard_map/attend/pallas_call | solution.py:348
  111.2 3.1 pad_maximum_fusion.1
  116.8 23.8 %finish.1 = (f32[1024,768]{1,0:T(8,128)}, f32[1024,768]{1,0:T(8,128)}, bf16[1024,3072]{1,0:T(8,128)(2,1)}, bf16[1024,3072]{1,0:T(8,128)(2,1)}, bf16[1024,768]{1,0:T(8,128)(2,1)}, /*index=5*/f32[8,768]{1,0:T(8,128)}) custom-call(s32[8]{0:T(128)} %bitcast.408, bf16[1024,768]{1,0:T(8,128)(2,1)} %bitcast.403, ...), custom_call_target="tpu_custom_call" | custom-call | flops 10871635968 | bytes 41943040 | tf_op jit(solution)/shard_map/finish/pallas_call | solution.py:502
  145.4 4.8 %unpack.1 = (bf16[768,576]{1,0:T(8,128)(2,1)}, bf16[192,768]{1,0:T(8,128)(2,1)}, bf16[768,768]{1,0:T(8,128)(2,1)}, bf16[768,768]{1,0:T(8,128)(2,1)}) custom-call(bf16[8,96,2304]{2,1,0:T(8,128)(2,1)} %bitcast.372), custom_call_target="tpu_custom_call" | custom-call | tf_op jit(solution)/shard_map/unpack/pallas_call | solution.py:752
  175.6 2.7 collective-permute-done.30
  197.1 23.5 %finish_back.1 = (bf16[1024,768]{1,0:T(8,128)(2,1)}, bf16[1024,3072]{1,0:T(8,128)(2,1)}, f32[1024,768]{1,0:T(8,128)}, bf16[1024,768]{1,0:T(8,128)(2,1)}, bf16[10...) custom-call(s32[8]{0:T(128)} %bitcast.409, bf16[1024,768]{1,0:T(8,128)(2,1)} %bitcast.401, ...), custom_call_target="tpu_custom_call" | custom-call | flops 10871635968 | bytes 41943040 | tf_op jit(solution)/shard_map/finish_back/pallas_call | solution.py:574
  228.2 9.4 %wide_blocks.1 = (bf16[4,384,768]{2,1,0:T(8,128)(2,1)}, bf16[4,384,768]{2,1,0:T(8,128)(2,1)}) custom-call(s32[2]{0:T(128)} %pad_add_fusion.ids_ref, bf16[1024,768]{1,0:T(8,128)(2,1)} %get-tuple-element.174.a_ref, bf16[1024,3072]{1,0:T(8,128)(2,1)} %get-tuple-element.175.b_ref), custom_call_target="tpu_custom_call" | custom-call | flops 9663676416 | bytes 16777216 | tf_op jit(solution)/shard_map/wide_blocks/pallas_call | solution.py:680
  237.6 5.7 %row_blocks.3 = (bf16[384,896]{1,0:T(8,128)(2,1)}, bf16[384,896]{1,0:T(8,128)(2,1)}) custom-call(s32[2]{0:T(128)} %pad_add_fusion.ids_ref, bf16[1024,768]{1,0:T(8,128)(2,1)} %get-tuple-element.178.mixed_ref.a_ref, bf16[1024,768]{1,0:T(8,128)(2,1)} %get-tuple-element.179.b_ref, f32[16,768]{1,0:T(8,128)} %get-tuple-element.180.refs_0_), custom_call_target="tpu_custom_call" | custom-call | flops 2415919104 | bytes 16777216 | tf_op jit(solution)/shard_map/row_blocks/pallas_call | solution.py:648
  245.9 10.2 %row_blocks.4 = (bf16[384,3072]{1,0:T(8,128)(2,1)}, bf16[384,3072]{1,0:T(8,128)(2,1)}) custom-call(s32[2]{0:T(128)} %pad_add_fusion.ids_ref, bf16[1024,768]{1,0:T(8,128)(2,1)} %get-tuple-element.185.a_ref, bf16[1024,3072]{1,0:T(8,128)(2,1)} %get-tuple-element.186.b_ref), custom_call_target="tpu_custom_call" | custom-call | flops 9663676416 | bytes 16777216 | tf_op jit(solution)/shard_map/row_blocks/pallas_call | solution.py:648
  256.0 3.4 collective-permute-done.39
  262.5 5.3 %collective-permute-done.37 = bf16[384,896]{1,0:T(8,128)(2,1)} collective-permute-done((bf16[384,896]{1,0:T(8,128)(2,1)}, bf16[384,896]{1,0:T(8,128)(2,1)}, u32[]{:S(2)}, u32[]{:S(2)}) %collective-permute-start.37) | collective-permute-done | bytes 688160 | tf_op jit(solution)/shard_map/ppermute | solution.py:25
  276.5 17.9 %attend_back.1.b_ref.g_ref = bf16[1024,2304]{1,0:T(8,128)(2,1)} custom-call(s32[8]{0:T(128)} %bitcast.410, bf16[1024,2304]{1,0:T(8,128)(2,1)} %get-tuple-element.148.packed_ref, bf16[1024,768]{1,0:T(8,128)(2,1)} %get-tuple-element.198.grad_ref), custom_call_target="tpu_custom_call" | custom-call | flops 9663676416 | bytes 16777216 | tf_op jit(solution)/shard_map/attend_back/pallas_call | solution.py:401
  294.4 4.1 %collective-permute-done.44 = bf16[192,768]{1,0:T(8,128)(2,1)S(1)} collective-permute-done((bf16[192,768]{1,0:T(8,128)(2,1)S(1)}, bf16[192,768]{1,0:T(8,128)(2,1)S(1)}, u32[]{:S(2)}, u32[]{:S(2)}) %collective-permute-start.44) | collective-permute-done | bytes 294944 | tf_op jit(solution)/shard_map/ppermute | solution.py:25
  301.4 8.5 %row_blocks.5 = (bf16[384,2304]{1,0:T(8,128)(2,1)}, bf16[384,2304]{1,0:T(8,128)(2,1)}) custom-call(s32[2]{0:T(128)} %pad_add_fusion.ids_ref, bf16[1024,768]{1,0:T(8,128)(2,1)} %bitcast.404, bf16[1024,2304]{1,0:T(8,128)(2,1)} %attend_back.1.b_ref.g_ref), custom_call_target="tpu_custom_call" | custom-call | flops 7247757312 | bytes 16777216 | tf_op jit(solution)/shard_map/row_blocks/pallas_call | solution.py:648
  310.0 4.3 %collective-permute-done.54 = bf16[2,96,768]{2,1,0:T(8,128)(2,1)S(1)} collective-permute-done((bf16[2,96,768]{2,1,0:T(8,128)(2,1)S(1)}, bf16[2,96,768]{2,1,0:T(8,128)(2,1)S(1)}, u32[]{:S(2)}, u32[]{:S(2)}) %collective-permute-start.54) | collective-permute-done | bytes 294944 | tf_op jit(solution)/shard_map/ppermute | solution.py:25
  314.4 2.9 collective-permute-start.55
  321.8 8.7 %token_grad.1 = bf16[1024,768]{1,0:T(8,128)(2,1)} custom-call(f32[1024,768]{1,0:T(8,128)} %get-tuple-element.212.resid_ref, bf16[1024,2304]{1,0:T(8,128)(2,1)} %attend_back.1.b_ref.g_ref, bf16[768,3072]{1,0:T(8,128)(2,1)} %copy-done), custom_call_target="tpu_custom_call" | custom-call | flops 7247757312 | bytes 16777216 | tf_op jit(solution)/shard_map/token_grad/pallas_call | solution.py:701
  333.8 3.0 fusion.2
  336.8 3.4 fusion
  341.8 3.0 fusion.20
  353.8 9.1 %collective-permute-done.50 = bf16[2,24,2304]{2,1,0:T(8,128)(2,1)S(1)} collective-permute-done((bf16[2,24,2304]{2,1,0:T(8,128)(2,1)S(1)}, bf16[2,24,2304]{2,1,0:T(8,128)(2,1)S(1)}, u32[]{:S(2)}, u32[]{:S(2)}) %collective-permute-start.50) | collective-permute-done | bytes 221216 | tf_op jit(solution)/shard_map/ppermute | solution.py:25
  365.5 2.8 collective-permute-start.65
  374.4 4.5 %collective-permute-done.52 = bf16[1,24,2304]{2,1,0:T(8,128)(2,1)S(1)} collective-permute-done((bf16[1,24,2304]{2,1,0:T(8,128)(2,1)S(1)}, bf16[1,24,2304]{2,1,0:T(8,128)(2,1)S(1)}, u32[]{:S(2)}, u32[]{:S(2)}) %collective-permute-start.52) | collective-permute-done | bytes 110624 | tf_op jit(solution)/shard_map/ppermute | solution.py:25
  378.9 2.9 collective-permute-start.53
  381.9 3.9 collective-permute-done.53
  (398 shorter events, 157.3 us)
Async XLA Ops:
  7.2 99.0 %all-gather.6.cloned.1.call-start = ((), (), s32[]{:S(2)}) async-start(), calls=%async_computation | async-start | bytes 5068800 | tf_op jit(solution)/shard_map/all_gather | solution.py:875
  24.4 121.0 %all-gather.8.cloned.1.call-start = ((), (), s32[]{:S(2)}) async-start(), calls=%async_computation.1 | async-start | bytes 3981312 | tf_op jit(solution)/shard_map/all_gather | solution.py:899
  35.0 12.6 %collective-permute-start.6 = (bf16[1,192,384]{2,1,0:T(8,128)(2,1)S(1)}, bf16[1,192,384]{2,1,0:T(8,128)(2,1)S(1)}, u32[]{:S(2)}, u32[]{:S(2)}) collective-permute-start(bf16[1,192,384]{2,1,0:T(8,128)(2,1)S(1)} %bitcast.390), channel_id=1, source_target_pairs={{0,4},{2,6},{4,0},{6,2},{1,5},{3,7},{5,1},{7,3},{8,12},{10,14},{12... | collective-permute-start | bytes 442376 | tf_op jit(solution)/shard_map/ppermute | solution.py:25
  55.1 15.1 %collective-permute-start.10 = (bf16[2,2,48,1536]{3,2,1,0:T(8,128)(2,1)S(1)}, bf16[2,2,48,1536]{3,2,1,0:T(8,128)(2,1)S(1)}, u32[]{:S(2)}, u32[]{:S(2)}) collective-permute-start(bf16[2,2,48,1536]{3,2,1,0:T(8,128)(2,1)S(1)} %get-tuple-element.140), channel_id=1, source_target_pairs={{0,16},{16,0},{1,17},{17,1},{2,18},{18,2},{3,19},{19,3},{4,20},{20... | collective-permute-start | bytes 1769480 | tf_op jit(solution)/shard_map/ppermute | solution.py:25
  56.6 15.8 %collective-permute-start.11 = (bf16[2,2,48,1536]{3,2,1,0:T(8,128)(2,1)S(1)}, bf16[2,2,48,1536]{3,2,1,0:T(8,128)(2,1)S(1)}, u32[]{:S(2)}, u32[]{:S(2)}) collective-permute-start(bf16[2,2,48,1536]{3,2,1,0:T(8,128)(2,1)S(1)} %get-tuple-element.141), channel_id=1, source_target_pairs={{0,8},{8,0},{1,9},{9,1},{2,10},{10,2},{3,11},{11,3},{4,12},{12,4},... | collective-permute-start | bytes 1769480 | tf_op jit(solution)/shard_map/ppermute | solution.py:25
  72.9 15.2 %collective-permute-start.15 = (bf16[2,192,384]{2,1,0:T(8,128)(2,1)S(1)}, bf16[2,192,384]{2,1,0:T(8,128)(2,1)S(1)}, u32[]{:S(2)}, u32[]{:S(2)}) collective-permute-start(bf16[2,192,384]{2,1,0:T(8,128)(2,1)S(1)} %get-tuple-element.315), channel_id=1, source_target_pairs={{0,16},{16,0},{1,17},{17,1},{2,18},{18,2},{3,19},{19,3},{4,20},{20... | collective-permute-start | bytes 884744 | tf_op jit(solution)/shard_map/ppermute | solution.py:25
  74.4 15.5 %collective-permute-start.14 = (bf16[2,192,384]{2,1,0:T(8,128)(2,1)S(1)}, bf16[2,192,384]{2,1,0:T(8,128)(2,1)S(1)}, u32[]{:S(2)}, u32[]{:S(2)}) collective-permute-start(bf16[2,192,384]{2,1,0:T(8,128)(2,1)S(1)} %get-tuple-element.316), channel_id=1, source_target_pairs={{0,8},{8,0},{1,9},{9,1},{2,10},{10,2},{3,11},{11,3},{4,12},{12,4},... | collective-permute-start | bytes 884744 | tf_op jit(solution)/shard_map/ppermute | solution.py:25
  90.2 15.2 %collective-permute-start.17 = (bf16[2,2,192,384]{3,2,1,0:T(8,128)(2,1)S(1)}, bf16[2,2,192,384]{3,2,1,0:T(8,128)(2,1)S(1)}, u32[]{:S(2)}, u32[]{:S(2)}) collective-permute-start(bf16[2,2,192,384]{3,2,1,0:T(8,128)(2,1)S(1)} %pad_maximum_fusion.16), channel_id=1, source_target_pairs={{0,8},{8,0},{1,9},{9,1},{2,10},{10,2},{3,11},{11,3},{4,12},{12,4},... | collective-permute-start | bytes 1769480 | tf_op jit(solution)/shard_map/ppermute | solution.py:25
  90.9 14.6 %collective-permute-start.16 = (bf16[2,2,192,384]{3,2,1,0:T(8,128)(2,1)S(1)}, bf16[2,2,192,384]{3,2,1,0:T(8,128)(2,1)S(1)}, u32[]{:S(2)}, u32[]{:S(2)}) collective-permute-start(bf16[2,2,192,384]{3,2,1,0:T(8,128)(2,1)S(1)} %pad_maximum_fusion.15), channel_id=1, source_target_pairs={{0,16},{16,0},{1,17},{17,1},{2,18},{18,2},{3,19},{19,3},{4,20},{20... | collective-permute-start | bytes 1769480 | tf_op jit(solution)/shard_map/ppermute | solution.py:25
  106.2 227.6 %all-gather.10.cloned.1.call-start = ((), (), s32[]{:S(2)}) async-start(), calls=%async_computation.2 | async-start | bytes 5160960 | tf_op jit(solution)/shard_map/all_gather | solution.py:925
  193.6 27.1 %collective-permute-start.35 = (bf16[32,1344]{1,0:T(8,128)(2,1)S(1)}, bf16[32,1344]{1,0:T(8,128)(2,1)S(1)}, u32[]{:S(2)}, u32[]{:S(2)}) collective-permute-start(bf16[32,1344]{1,0:T(8,128)(2,1)S(1)} %concatenate.91), channel_id=1, source_target_pairs={{0,16},{8,24},{16,0},{24,8},{1,17},{9,25},{17,1},{25,9},{2,18},{10... | collective-permute-start | bytes 258056 | tf_op jit(solution)/shard_map/ppermute | solution.py:113
  195.1 25.6 %collective-permute-start.36 = (bf16[32,1344]{1,0:T(8,128)(2,1)S(1)}, bf16[32,1344]{1,0:T(8,128)(2,1)S(1)}, u32[]{:S(2)}, u32[]{:S(2)}) collective-permute-start(bf16[32,1344]{1,0:T(8,128)(2,1)S(1)} %concatenate.91), channel_id=1, source_target_pairs={{0,24},{8,16},{16,8},{24,0},{1,25},{9,17},{17,9},{25,1},{2,26},{10... | collective-permute-start | bytes 258056 | tf_op jit(solution)/shard_map/ppermute | solution.py:113
  196.6 24.2 %collective-permute-start.34 = (bf16[32,1344]{1,0:T(8,128)(2,1)S(1)}, bf16[32,1344]{1,0:T(8,128)(2,1)S(1)}, u32[]{:S(2)}, u32[]{:S(2)}) collective-permute-start(bf16[32,1344]{1,0:T(8,128)(2,1)S(1)} %concatenate.91), channel_id=1, source_target_pairs={{0,8},{8,0},{16,24},{24,16},{1,9},{9,1},{17,25},{25,17},{2,10},{10... | collective-permute-start | bytes 258056 | tf_op jit(solution)/shard_map/ppermute | solution.py:113
  243.6 15.8 %collective-permute-start.39 = (bf16[2,192,768]{2,1,0:T(8,128)(2,1)S(1)}, bf16[2,192,768]{2,1,0:T(8,128)(2,1)S(1)}, u32[]{:S(2)}, u32[]{:S(2)}) collective-permute-start(bf16[2,192,768]{2,1,0:T(8,128)(2,1)S(1)} %pad_maximum_fusion.17), channel_id=1, source_target_pairs={{0,8},{8,0},{1,9},{9,1},{2,10},{10,2},{3,11},{11,3},{4,12},{12,4},... | collective-permute-start | bytes 1769480 | tf_op jit(solution)/shard_map/ppermute | solution.py:25
  245.2 15.5 %collective-permute-start.40 = (bf16[2,192,768]{2,1,0:T(8,128)(2,1)S(1)}, bf16[2,192,768]{2,1,0:T(8,128)(2,1)S(1)}, u32[]{:S(2)}, u32[]{:S(2)}) collective-permute-start(bf16[2,192,768]{2,1,0:T(8,128)(2,1)S(1)} %pad_maximum_fusion.18), channel_id=1, source_target_pairs={{0,16},{16,0},{1,17},{17,1},{2,18},{18,2},{3,19},{19,3},{4,20},{20... | collective-permute-start | bytes 1769480 | tf_op jit(solution)/shard_map/ppermute | solution.py:25
  272.1 26.6 %collective-permute-start.42 = (bf16[2,48,3968]{2,1,0:T(8,128)(2,1)S(1)}, bf16[2,48,3968]{2,1,0:T(8,128)(2,1)S(1)}, u32[]{:S(2)}, u32[]{:S(2)}) collective-permute-start(bf16[2,48,3968]{2,1,0:T(8,128)(2,1)S(1)} %pad_maximum_fusion.6), channel_id=1, source_target_pairs={{0,8},{8,0},{1,9},{9,1},{2,10},{10,2},{3,11},{11,3},{4,12},{12,4},... | collective-permute-start | bytes 2285576 | tf_op jit(solution)/shard_map/ppermute | solution.py:25
  273.3 25.6 %collective-permute-start.43 = (bf16[2,48,3968]{2,1,0:T(8,128)(2,1)S(1)}, bf16[2,48,3968]{2,1,0:T(8,128)(2,1)S(1)}, u32[]{:S(2)}, u32[]{:S(2)}) collective-permute-start(bf16[2,48,3968]{2,1,0:T(8,128)(2,1)S(1)} %pad_maximum_fusion.8), channel_id=1, source_target_pairs={{0,16},{16,0},{1,17},{17,1},{2,18},{18,2},{3,19},{19,3},{4,20},{20... | collective-permute-start | bytes 2285576 | tf_op jit(solution)/shard_map/ppermute | solution.py:25
  274.9 23.6 %collective-permute-start.44 = (bf16[192,768]{1,0:T(8,128)(2,1)S(1)}, bf16[192,768]{1,0:T(8,128)(2,1)S(1)}, u32[]{:S(2)}, u32[]{:S(2)}) collective-permute-start(bf16[192,768]{1,0:T(8,128)(2,1)S(1)} %copy-done.16), channel_id=1, source_target_pairs={{0,16},{16,0},{1,17},{17,1},{2,18},{18,2},{3,19},{19,3},{4,20},{20... | collective-permute-start | bytes 884744 | tf_op jit(solution)/shard_map/ppermute | solution.py:25
  275.4 23.1 %collective-permute-start.45 = (bf16[192,768]{1,0:T(8,128)(2,1)S(1)}, bf16[192,768]{1,0:T(8,128)(2,1)S(1)}, u32[]{:S(2)}, u32[]{:S(2)}) collective-permute-start(bf16[192,768]{1,0:T(8,128)(2,1)S(1)} %copy-done.15), channel_id=1, source_target_pairs={{0,8},{8,0},{1,9},{9,1},{2,10},{10,2},{3,11},{11,3},{4,12},{12,4},... | collective-permute-start | bytes 884744 | tf_op jit(solution)/shard_map/ppermute | solution.py:25
  299.1 18.2 %collective-permute-start.60 = (bf16[48,3968]{1,0:T(8,128)(2,1)S(1)}, bf16[48,3968]{1,0:T(8,128)(2,1)S(1)}, u32[]{:S(2)}, u32[]{:S(2)}) collective-permute-start(bf16[48,3968]{1,0:T(8,128)(2,1)S(1)} %get-tuple-element.205), channel_id=1, source_target_pairs={{0,16},{16,0},{1,17},{17,1},{2,18},{18,2},{3,19},{19,3},{4,20},{20... | collective-permute-start | bytes 1142792 | tf_op jit(solution)/shard_map/ppermute | solution.py:25
  300.6 16.7 %collective-permute-start.61 = (bf16[48,3968]{1,0:T(8,128)(2,1)S(1)}, bf16[48,3968]{1,0:T(8,128)(2,1)S(1)}, u32[]{:S(2)}, u32[]{:S(2)}) collective-permute-start(bf16[48,3968]{1,0:T(8,128)(2,1)S(1)} %get-tuple-element.207), channel_id=1, source_target_pairs={{0,8},{8,0},{1,9},{9,1},{2,10},{10,2},{3,11},{11,3},{4,12},{12,4},... | collective-permute-start | bytes 1142792 | tf_op jit(solution)/shard_map/ppermute | solution.py:25
  301.2 13.1 %collective-permute-start.54 = (bf16[2,96,768]{2,1,0:T(8,128)(2,1)S(1)}, bf16[2,96,768]{2,1,0:T(8,128)(2,1)S(1)}, u32[]{:S(2)}, u32[]{:S(2)}) collective-permute-start(bf16[2,96,768]{2,1,0:T(8,128)(2,1)S(1)} %dynamic-slice_bitcast_fusion.1), channel_id=1, source_target_pairs={{0,2},{2,0},{4,6},{6,4},{1,3},{3,1},{5,7},{7,5},{8,10},{10,8},{12,... | collective-permute-start | bytes 884744 | tf_op jit(solution)/shard_map/ppermute | solution.py:25
  314.4 16.1 %collective-permute-start.55 = (bf16[1,96,768]{2,1,0:T(8,128)(2,1)S(1)}, bf16[1,96,768]{2,1,0:T(8,128)(2,1)S(1)}, u32[]{:S(2)}, u32[]{:S(2)}) collective-permute-start(bf16[1,96,768]{2,1,0:T(8,128)(2,1)S(1)} %constant_dynamic-slice_fusion.1), channel_id=1, source_target_pairs={{0,4},{2,6},{4,0},{6,2},{1,5},{3,7},{5,1},{7,3},{8,12},{10,14},{12... | collective-permute-start | bytes 442376 | tf_op jit(solution)/shard_map/ppermute | solution.py:25
  317.6 12.9 %collective-permute-start.62 = (bf16[2,24,3968]{2,1,0:T(8,128)(2,1)S(1)}, bf16[2,24,3968]{2,1,0:T(8,128)(2,1)S(1)}, u32[]{:S(2)}, u32[]{:S(2)}) collective-permute-start(bf16[2,24,3968]{2,1,0:T(8,128)(2,1)S(1)} %dynamic-slice_bitcast_fusion), channel_id=1, source_target_pairs={{0,2},{2,0},{4,6},{6,4},{1,3},{3,1},{5,7},{7,5},{8,10},{10,8},{12,... | collective-permute-start | bytes 1142792 | tf_op jit(solution)/shard_map/ppermute | solution.py:25
  318.3 21.9 %collective-permute-start.48 = (bf16[96,2304]{1,0:T(8,128)(2,1)S(1)}, bf16[96,2304]{1,0:T(8,128)(2,1)S(1)}, u32[]{:S(2)}, u32[]{:S(2)}) collective-permute-start(bf16[96,2304]{1,0:T(8,128)(2,1)S(1)} %get-tuple-element.271), channel_id=1, source_target_pairs={{0,16},{8,24},{16,0},{24,8},{1,17},{9,25},{17,1},{25,9},{2,18},{10... | collective-permute-start | bytes 1327112 | tf_op jit(solution)/shard_map/ppermute | solution.py:113
  319.8 20.4 %collective-permute-start.49 = (bf16[96,2304]{1,0:T(8,128)(2,1)S(1)}, bf16[96,2304]{1,0:T(8,128)(2,1)S(1)}, u32[]{:S(2)}, u32[]{:S(2)}) collective-permute-start(bf16[96,2304]{1,0:T(8,128)(2,1)S(1)} %get-tuple-element.272), channel_id=1, source_target_pairs={{0,24},{8,16},{16,8},{24,0},{1,25},{9,17},{17,9},{25,1},{2,26},{10... | collective-permute-start | bytes 1327112 | tf_op jit(solution)/shard_map/ppermute | solution.py:113
  321.3 19.2 %collective-permute-start.47 = (bf16[96,2304]{1,0:T(8,128)(2,1)S(1)}, bf16[96,2304]{1,0:T(8,128)(2,1)}, u32[]{:S(2)}, u32[]{:S(2)}) collective-permute-start(bf16[96,2304]{1,0:T(8,128)(2,1)S(1)} %get-tuple-element.273), channel_id=1, source_target_pairs={{0,8},{8,0},{16,24},{24,16},{1,9},{9,1},{17,25},{25,17},{2,10},{10... | collective-permute-start | bytes 1327112 | tf_op jit(solution)/shard_map/ppermute | solution.py:113
  330.6 19.7 %collective-permute-start.56 = (bf16[1,96,768]{2,1,0:T(8,128)(2,1)S(1)}, bf16[1,96,768]{2,1,0:T(8,128)(2,1)S(1)}, u32[]{:S(2)}, u32[]{:S(2)}) collective-permute-start(bf16[1,96,768]{2,1,0:T(8,128)(2,1)S(1)} %add_convert_fusion.30), channel_id=1, source_target_pairs={{0,4},{2,6},{4,0},{6,2},{1,5},{3,7},{5,1},{7,3},{8,12},{10,14},{12... | collective-permute-start | bytes 442376 | tf_op jit(solution)/shard_map/ppermute | solution.py:25
  331.8 15.2 %collective-permute-start.63 = (bf16[1,24,3968]{2,1,0:T(8,128)(2,1)S(1)}, bf16[1,24,3968]{2,1,0:T(8,128)(2,1)}, u32[]{:S(2)}, u32[]{:S(2)}) collective-permute-start(bf16[1,24,3968]{2,1,0:T(8,128)(2,1)S(1)} %constant_dynamic-slice_fusion), channel_id=1, source_target_pairs={{0,4},{2,6},{4,0},{6,2},{1,5},{3,7},{5,1},{7,3},{8,12},{10,14},{12... | collective-permute-start | bytes 571400 | tf_op jit(solution)/shard_map/ppermute | solution.py:25
  350.3 12.7 %collective-permute-start.64 = (bf16[1,24,3968]{2,1,0:T(8,128)(2,1)S(1)}, bf16[1,24,3968]{2,1,0:T(8,128)(2,1)S(1)}, u32[]{:S(2)}, u32[]{:S(2)}) collective-permute-start(bf16[1,24,3968]{2,1,0:T(8,128)(2,1)S(1)} %add_convert_fusion.29), channel_id=1, source_target_pairs={{0,4},{2,6},{4,0},{6,2},{1,5},{3,7},{5,1},{7,3},{8,12},{10,14},{12... | collective-permute-start | bytes 571400 | tf_op jit(solution)/shard_map/ppermute | solution.py:25
  352.7 19.0 %collective-permute-start.57 = (bf16[2,96,768]{2,1,0:T(8,128)(2,1)S(1)}, bf16[2,96,768]{2,1,0:T(8,128)(2,1)S(1)}, u32[]{:S(2)}, u32[]{:S(2)}) collective-permute-start(bf16[2,96,768]{2,1,0:T(8,128)(2,1)S(1)} %maximum_bitcast_fusion.7), channel_id=1, source_target_pairs={{0,2},{2,0},{4,6},{6,4},{1,3},{3,1},{5,7},{7,5},{8,10},{10,8},{12,... | collective-permute-start | bytes 884744 | tf_op jit(solution)/shard_map/ppermute | solution.py:25
  365.5 16.3 %collective-permute-start.65 = (bf16[2,24,3968]{2,1,0:T(8,128)(2,1)S(1)}, bf16[2,24,3968]{2,1,0:T(8,128)(2,1)S(1)}, u32[]{:S(2)}, u32[]{:S(2)}) collective-permute-start(bf16[2,24,3968]{2,1,0:T(8,128)(2,1)S(1)} %maximum_bitcast_fusion.4), channel_id=1, source_target_pairs={{0,2},{2,0},{4,6},{6,4},{1,3},{3,1},{5,7},{7,5},{8,10},{10,8},{12,... | collective-permute-start | bytes 1142792 | tf_op jit(solution)/shard_map/ppermute | solution.py:25
  (72 other events, 505.9 us)
Sparse Core Ops, SparseCore 0:
  24.5 76.9 all-gather.5
  106.3 39.0 all-gather.7
  262.7 50.8 all-gather.9
